TPU v7x, 32 devices: a whole 2x2x4 slice. The times are simulated.
32 devices in a mesh: shots: 2 (over y), lat: 4 (over z), freq: 2 (over x), sub: 2 (over core).
Axes of the slice: x: 2, y: 2, z: 4, core: 2. Of those that a mesh axis runs over, the one named last changes fastest.
Arguments:
- wavefields: float32 [4, 4, 64, 1024], P(('shots', 'freq'), None, 'lat', 'sub'), parts along dimension 0, may hold values from -6 to 6
- velocity: float32 [8, 64, 1024], P('freq', 'lat', 'sub'), may hold values from 0 to 31
- filter_table: float32 [32, 32, 9, 2], replicated, may hold values from -1 to 1
- freq_pick: int32 [2], P('freq'), may hold values from 0 to 31
- slab_order: int32 [4], replicated, may hold values from 0 to 7
Outputs:
- fields_out: float32 [4, 4, 64, 1024], P(('shots', 'freq'), None, 'lat', 'sub'), parts along dimension 0
- image: float32 [8, 64, 1024], P(('shots', 'freq'), 'lat', 'sub'), parts along dimension 0
There are 2 independent parts, one for each index of `shots`. A program takes and returns all parts, laid end to end along the dimension named above; an argument that names none is the same for every part. Nothing has to cross between parts.
All inputs are finite; a program needn't handle non-finite values.
Results may differ from a plain program's by a relative error of at most 0.0003.
Values sent between devices are 32-bit elements; how exact they have to be, the bound alone decides.
No kernel may reach another device: no remote copies, remote signals or barrier semaphores. Data moves between devices by JAX's collectives and lax.ppermute only.
A program may use at most 64 MiB of HBM per device.

v0:
```python
import jax
import jax.numpy as jnp
from jax import lax
from jax.sharding import PartitionSpec as P

KCHEB = 8
NBINS = 32
TABLE_FREQS = 32


def padded_2(cells, sides, width):
    for axis, dim in sides:
        count = lax.axis_size(axis)
        ends = count - 1
        head = lax.slice_in_dim(cells, 0, width, axis=dim)
        tail = lax.slice_in_dim(cells, cells.shape[dim] - width, cells.shape[dim], axis=dim)
        cells = jnp.concatenate(
            [
                lax.ppermute(tail, axis, [(i, (i + 1) % count) for i in range(ends)]),
                cells,
                lax.ppermute(head, axis, [((i + 1) % count, i) for i in range(ends)]),
            ],
            axis=dim,
        )
    return cells


def spread(value, axis, source):
    kept = jnp.where(lax.axis_index(axis) == source, value, 0).astype(value.dtype)
    return lax.psum(kept, axis)


def stencil(padded):
    edges = (
        padded[:, :, 2:, 1:-1]
        + padded[:, :, :-2, 1:-1]
        + padded[:, :, 1:-1, 2:]
        + padded[:, :, 1:-1, :-2]
    )
    corners = (
        padded[:, :, 2:, 2:]
        + padded[:, :, 2:, :-2]
        + padded[:, :, :-2, 2:]
        + padded[:, :, :-2, :-2]
    )
    return -0.5 * padded[:, :, 1:-1, 1:-1] + 0.25 * edges + 0.125 * corners


def combine(pair, term):
    real_part = pair[:, 0][:, None]
    imag_part = pair[:, 1][:, None]
    turned = jnp.stack([term[:, 1], -term[:, 0], -term[:, 3], term[:, 2]], axis=1)
    return real_part * term + imag_part * turned


def trim_edges(array, width):
    return array[:, :, width : array.shape[2] - width, width : array.shape[3] - width]


def propagate(fields, coefficients):
    rows_here = fields.shape[2]
    cols_here = fields.shape[3]
    padded = padded_2(fields, (("lat", 2), ("sub", 3)), KCHEB)
    row_ids = (
        lax.axis_index("lat") * rows_here
        - KCHEB
        + jnp.arange(rows_here + 2 * KCHEB, dtype=jnp.int32)
    )
    col_ids = (
        lax.axis_index("sub") * cols_here
        - KCHEB
        + jnp.arange(cols_here + 2 * KCHEB, dtype=jnp.int32)
    )
    row_inside = (row_ids >= 0) & (row_ids < rows_here * lax.axis_size("lat"))
    col_inside = (col_ids >= 0) & (col_ids < cols_here * lax.axis_size("sub"))
    inside = (row_inside[:, None] & col_inside[None, :]).astype(jnp.float32)[None, None]
    current = stencil(padded) * trim_edges(inside, 1)
    summed = combine(coefficients[:, 0], trim_edges(padded, KCHEB))
    summed = summed + combine(coefficients[:, 1], trim_edges(current, KCHEB - 1))
    previous = trim_edges(padded, 1)
    for order in range(2, KCHEB + 1):
        following = (2.0 * stencil(current) - trim_edges(previous, 1)) * trim_edges(inside, order)
        previous = trim_edges(current, 1)
        current = following
        summed = summed + combine(coefficients[:, order], trim_edges(current, KCHEB - order))
    return summed


def body(wavefields, velocity, filter_table, freq_pick, slab_order):
    highest = lax.Precision.HIGHEST
    freq_here = wavefields.shape[0]
    rows_here = wavefields.shape[2]
    cols_here = wavefields.shape[3]
    depth_count = slab_order.shape[0]
    slab_size = velocity.shape[0]
    onehot = (freq_pick[:, None] == jnp.arange(TABLE_FREQS, dtype=jnp.int32)[None, :]).astype(
        jnp.float32
    )
    selected = jnp.einsum("ft,btkc->bfkc", onehot, filter_table, precision=highest)
    selected = selected.reshape(NBINS, freq_here * (KCHEB + 1) * 2).T
    bin_grid = jnp.arange(NBINS, dtype=jnp.float32)[:, None]
    fields = wavefields
    images = []
    for depth_step in range(depth_count):
        stored_row = slab_order[depth_step]
        owner_index = stored_row // slab_size
        local_slab = lax.dynamic_index_in_dim(velocity, stored_row % slab_size, 0, keepdims=False)
        slowness = spread(local_slab, "freq", owner_index)
        weights = jnp.maximum(0.0, 1.0 - jnp.abs(slowness.reshape(1, -1) - bin_grid))
        coefficients = jnp.dot(
            selected, weights, precision=highest, preferred_element_type=jnp.float32
        )
        coefficients = coefficients.reshape(freq_here, KCHEB + 1, 2, rows_here, cols_here)
        fields = propagate(fields, coefficients)
        images.append(jnp.sum(fields[:, 0] * fields[:, 2] + fields[:, 1] * fields[:, 3], axis=0))
    image = lax.psum_scatter(jnp.stack(images), "freq", scatter_dimension=0, tiled=True)
    return (fields, image)


def solution(mesh):
    return jax.shard_map(
        body,
        mesh=mesh,
        in_specs=(
            P(("shots", "freq"), None, "lat", "sub"),
            P("freq", "lat", "sub"),
            P(),
            P("freq"),
            P(),
        ),
        out_specs=(P(("shots", "freq"), None, "lat", "sub"), P(("shots", "freq"), "lat", "sub")),
        check_vma=False,
    )
```

profile of v0, /device:TPU:0, one launch (start us, length us, event | category | flops | bytes accessed | tf_op | source)
XLA Modules:
  0.0 132.2 jit_solution(1288073521802857635)
XLA Ops:
  7.2 0.9 fusion.356
  8.2 1.4 %collective-permute-start.1 = (f32[1,4,8,512]{3,2,1,0:T(8,128)S(1)}, f32[1,4,8,512]{3,2,1,0:T(8,128)S(1)}, u32[]{:S(2)}, u32[]{:S(2)}) collective-permute-start(f32[1,4,8,512]{3,2,1,0:T(8,128)S(1)} %get-tuple-element.207), channel_id=1, source_target_pairs={{4,0},{8,4},{12,8},{5,1},{9,5},{13,9},{6,2},{10,6},{14,10},{7,3},{... | collective-permute-start | bytes 196616 | tf_op jit(solution)/shard_map/ppermute | solution.py:21
  9.6 5.6 %collective-permute-start = (f32[1,4,8,512]{3,2,1,0:T(8,128)S(1)}, f32[1,4,8,512]{3,2,1,0:T(8,128)S(1)}, u32[]{:S(2)}, u32[]{:S(2)}) collective-permute-start(f32[1,4,8,512]{3,2,1,0:T(8,128)S(1)} %get-tuple-element.208), channel_id=1, source_target_pairs={{0,4},{4,8},{8,12},{1,5},{5,9},{9,13},{2,6},{6,10},{10,14},{3,7},{... | collective-permute-start | bytes 196616 | tf_op jit(solution)/shard_map/ppermute | solution.py:19
  30.5 1.5 %collective-permute-start.2 = (f32[1,4,32,8]{3,2,1,0:T(8,128)S(1)}, f32[1,4,32,8]{3,2,1,0:T(8,128)S(1)}, u32[]{:S(2)}, u32[]{:S(2)}) collective-permute-start(f32[1,4,32,8]{3,2,1,0:T(8,128)S(1)} %get-tuple-element.96), channel_id=1, source_target_pairs={{0,1},{2,3},{4,5},{6,7},{8,9},{10,11},{12,13},{14,15},{16,17},{18,... | collective-permute-start | bytes 12296 | tf_op jit(solution)/shard_map/ppermute | solution.py:19
  32.0 1.3 collective-permute-start.3
  33.4 1.7 %collective-permute-done.3 = f32[1,4,32,8]{3,2,1,0:T(8,128)S(1)} collective-permute-done((f32[1,4,32,8]{3,2,1,0:T(8,128)S(1)}, f32[1,4,32,8]{3,2,1,0:T(8,128)S(1)}, u32[]{:S(2)}, u32[]{:S(2)}) %collective-permute-start.3) | collective-permute-done | bytes 4128 | tf_op jit(solution)/shard_map/ppermute | solution.py:21
  40.2 0.8 fusion.330
  41.3 0.8 fusion.347
  42.1 7.4 %all-reduce.3.cloned.1.call-done = (f32[16,512]{1,0:T(8,128)}, f32[16,512]{1,0:T(8,128)}, f32[16,512]{1,0:T(8,128)}, f32[16,512]{1,0:T(8,128)}) async-done(((f32[16,512]{1,0:T(8,128)}, f32[16,512]{1,0:T(8,128)}, f32[16,512]{1,0:T(8,128)}, f32[16,512]{1,0:T(8,128)}), (f32[16,512]{1,0:T(8,128)}, f32[16,512]{1,0:T(8,128)}, f32[16,512]{1,0:T(8,128)}, f32[16,512]{1,0:T(8,128)})) %all-reduce.3.cloned.1.call-update) | async-done | bytes 131088 | tf_op jit(solution)/shard_map/psum | solution.py:30
  49.4 1.8 %convolution_bitcast_fusion = f32[1,9,2,16,512]{4,1,3,2,0:T(8,128)S(1)} fusion(f32[16,512]{1,0:T(8,128)} %get-tuple-element.2, f32[9,2,32,1]{2,1,0,3:T(2,128)S(1)} %bitcast.356), kind=kOutput, calls=%fused_computation | convolution fusion | flops 57671680 | bytes 624896 | tf_op jit(solution)/shard_map/dot_general | solution.py:110
  53.6 3.4 %collective-permute-start.4 = (f32[1,4,8,512]{3,2,1,0:T(8,128)S(1)}, f32[1,4,8,512]{3,2,1,0:T(8,128)S(1)}, u32[]{:S(2)}, u32[]{:S(2)}) collective-permute-start(f32[1,4,8,512]{3,2,1,0:T(8,128)S(1)} %get-tuple-element.193), channel_id=1, source_target_pairs={{0,4},{4,8},{8,12},{1,5},{5,9},{9,13},{2,6},{6,10},{10,14},{3,7},{... | collective-permute-start | bytes 196616 | tf_op jit(solution)/shard_map/ppermute | solution.py:19
  57.0 1.5 %collective-permute-start.5 = (f32[1,4,8,512]{3,2,1,0:T(8,128)S(1)}, f32[1,4,8,512]{3,2,1,0:T(8,128)S(1)}, u32[]{:S(2)}, u32[]{:S(2)}) collective-permute-start(f32[1,4,8,512]{3,2,1,0:T(8,128)S(1)} %get-tuple-element.194), channel_id=1, source_target_pairs={{4,0},{8,4},{12,8},{5,1},{9,5},{13,9},{6,2},{10,6},{14,10},{7,3},{... | collective-permute-start | bytes 196616 | tf_op jit(solution)/shard_map/ppermute | solution.py:21
  58.5 1.0 convolution_bitcast_fusion.1
  60.0 0.7 copy-done.26
  60.7 1.0 convolution_bitcast_fusion.2
  63.0 1.0 convolution_bitcast_fusion.3
  64.9 1.3 collective-permute-start.6
  66.2 1.3 collective-permute-start.7
  67.8 1.6 %collective-permute-done.7 = f32[1,4,32,8]{3,2,1,0:T(8,128)S(1)} collective-permute-done((f32[1,4,32,8]{3,2,1,0:T(8,128)S(1)}, f32[1,4,32,8]{3,2,1,0:T(8,128)S(1)}, u32[]{:S(2)}, u32[]{:S(2)}) %collective-permute-start.7) | collective-permute-done | bytes 4128 | tf_op jit(solution)/shard_map/ppermute | solution.py:21
  75.1 4.5 %collective-permute-start.8 = (f32[1,4,8,512]{3,2,1,0:T(8,128)S(1)}, f32[1,4,8,512]{3,2,1,0:T(8,128)S(1)}, u32[]{:S(2)}, u32[]{:S(2)}) collective-permute-start(f32[1,4,8,512]{3,2,1,0:T(8,128)S(1)} %get-tuple-element.187), channel_id=1, source_target_pairs={{0,4},{4,8},{8,12},{1,5},{5,9},{9,13},{2,6},{6,10},{10,14},{3,7},{... | collective-permute-start | bytes 196616 | tf_op jit(solution)/shard_map/ppermute | solution.py:19
  79.7 1.3 collective-permute-start.9
  81.6 4.3 %collective-permute-done.9 = f32[1,4,8,512]{3,2,1,0:T(8,128)S(1)} collective-permute-done((f32[1,4,8,512]{3,2,1,0:T(8,128)S(1)}, f32[1,4,8,512]{3,2,1,0:T(8,128)S(1)}, u32[]{:S(2)}, u32[]{:S(2)}) %collective-permute-start.9) | collective-permute-done | bytes 65568 | tf_op jit(solution)/shard_map/ppermute | solution.py:21
  85.9 1.3 collective-permute-start.10
  87.2 1.5 %collective-permute-start.11 = (f32[1,4,32,8]{3,2,1,0:T(8,128)S(1)}, f32[1,4,32,8]{3,2,1,0:T(8,128)S(1)}, u32[]{:S(2)}, u32[]{:S(2)}) collective-permute-start(f32[1,4,32,8]{3,2,1,0:T(8,128)S(1)} %get-tuple-element.93), channel_id=1, source_target_pairs={{1,0},{3,2},{5,4},{7,6},{9,8},{11,10},{13,12},{15,14},{17,16},{19,... | collective-permute-start | bytes 12296 | tf_op jit(solution)/shard_map/ppermute | solution.py:21
  88.8 1.6 %collective-permute-done.11 = f32[1,4,32,8]{3,2,1,0:T(8,128)S(1)} collective-permute-done((f32[1,4,32,8]{3,2,1,0:T(8,128)S(1)}, f32[1,4,32,8]{3,2,1,0:T(8,128)S(1)}, u32[]{:S(2)}, u32[]{:S(2)}) %collective-permute-start.11) | collective-permute-done | bytes 4128 | tf_op jit(solution)/shard_map/ppermute | solution.py:21
  96.1 3.4 %collective-permute-start.12 = (f32[1,4,8,512]{3,2,1,0:T(8,128)S(1)}, f32[1,4,8,512]{3,2,1,0:T(8,128)S(1)}, u32[]{:S(2)}, u32[]{:S(2)}) collective-permute-start(f32[1,4,8,512]{3,2,1,0:T(8,128)S(1)} %get-tuple-element.181), channel_id=1, source_target_pairs={{0,4},{4,8},{8,12},{1,5},{5,9},{9,13},{2,6},{6,10},{10,14},{3,7},{... | collective-permute-start | bytes 196616 | tf_op jit(solution)/shard_map/ppermute | solution.py:19
  99.5 1.3 collective-permute-start.13
  101.4 4.3 %collective-permute-done.13 = f32[1,4,8,512]{3,2,1,0:T(8,128)S(1)} collective-permute-done((f32[1,4,8,512]{3,2,1,0:T(8,128)S(1)}, f32[1,4,8,512]{3,2,1,0:T(8,128)S(1)}, u32[]{:S(2)}, u32[]{:S(2)}) %collective-permute-start.13) | collective-permute-done | bytes 65568 | tf_op jit(solution)/shard_map/ppermute | solution.py:21
  105.7 1.3 collective-permute-start.14
  107.0 1.3 collective-permute-start.15
  108.4 1.8 %collective-permute-done.15 = f32[1,4,32,8]{3,2,1,0:T(8,128)S(1)} collective-permute-done((f32[1,4,32,8]{3,2,1,0:T(8,128)S(1)}, f32[1,4,32,8]{3,2,1,0:T(8,128)S(1)}, u32[]{:S(2)}, u32[]{:S(2)}) %collective-permute-start.15) | collective-permute-done | bytes 4128 | tf_op jit(solution)/shard_map/ppermute | solution.py:21
  116.6 8.7 %reduce-scatter.2.cloned.1.call-done = f32[2,16,512]{2,1,0:T(8,128)} async-done(((f32[4,16,512]{2,1,0:T(8,128)}), f32[2,16,512]{2,1,0:T(8,128)}) %reduce-scatter.2.cloned.1.call-update) | async-done | bytes 65552 | tf_op jit(solution)/shard_map/reduce_scatter | solution.py:116
  (261 shorter events, 32.8 us)
Async XLA Ops:
  7.2 22.4 %copy-start = (f32[32,32,9,2]{1,3,2,0:T(2,128)S(1)}, f32[32,32,9,2]{1,3,2,0:T(2,128)}, u32[]{:S(2)}) copy-start(f32[32,32,9,2]{1,3,2,0:T(2,128)} %param.7) | copy-start | bytes 221188
  7.2 42.3 %all-reduce.3.cloned.1.call-start = ((), (), s32[]{:S(2)}) async-start(), calls=%async_computation.2 | async-start | bytes 262144 | tf_op jit(solution)/shard_map/psum | solution.py:30
  7.2 8.0 %copy-start.28 = (s32[4]{0:T(128)S(1)}, s32[4]{0:T(128)}, u32[]{:S(2)}) copy-start(s32[4]{0:T(128)} %param.9) | copy-start | bytes 52
  8.2 18.0 %copy-start.24 = (f32[4,16,512]{2,1,0:T(8,128)S(1)}, f32[4,16,512]{2,1,0:T(8,128)}, u32[]{:S(2)}) copy-start(f32[4,16,512]{2,1,0:T(8,128)} %param.6) | copy-start | bytes 393220
  8.2 22.3 %collective-permute-start.1 = (f32[1,4,8,512]{3,2,1,0:T(8,128)S(1)}, f32[1,4,8,512]{3,2,1,0:T(8,128)S(1)}, u32[]{:S(2)}, u32[]{:S(2)}) collective-permute-start(f32[1,4,8,512]{3,2,1,0:T(8,128)S(1)} %get-tuple-element.207), channel_id=1, source_target_pairs={{4,0},{8,4},{12,8},{5,1},{9,5},{13,9},{6,2},{10,6},{14,10},{7,3},{... | collective-permute-start | bytes 196616 | tf_op jit(solution)/shard_map/ppermute | solution.py:21
  9.6 20.8 %collective-permute-start = (f32[1,4,8,512]{3,2,1,0:T(8,128)S(1)}, f32[1,4,8,512]{3,2,1,0:T(8,128)S(1)}, u32[]{:S(2)}, u32[]{:S(2)}) collective-permute-start(f32[1,4,8,512]{3,2,1,0:T(8,128)S(1)} %get-tuple-element.208), channel_id=1, source_target_pairs={{0,4},{4,8},{8,12},{1,5},{5,9},{9,13},{2,6},{6,10},{10,14},{3,7},{... | collective-permute-start | bytes 196616 | tf_op jit(solution)/shard_map/ppermute | solution.py:19
  26.9 98.5 %reduce-scatter.2.cloned.1.call-start = ((), (), s32[]{:S(2)}) async-start(), calls=%async_computation.1 | async-start | bytes 196608 | tf_op jit(solution)/shard_map/reduce_scatter | solution.py:116
  27.4 0.9 copy-start.1
  30.5 2.9 %collective-permute-start.2 = (f32[1,4,32,8]{3,2,1,0:T(8,128)S(1)}, f32[1,4,32,8]{3,2,1,0:T(8,128)S(1)}, u32[]{:S(2)}, u32[]{:S(2)}) collective-permute-start(f32[1,4,32,8]{3,2,1,0:T(8,128)S(1)} %get-tuple-element.96), channel_id=1, source_target_pairs={{0,1},{2,3},{4,5},{6,7},{8,9},{10,11},{12,13},{14,15},{16,17},{18,... | collective-permute-start | bytes 12296 | tf_op jit(solution)/shard_map/ppermute | solution.py:19
  32.0 3.1 %collective-permute-start.3 = (f32[1,4,32,8]{3,2,1,0:T(8,128)S(1)}, f32[1,4,32,8]{3,2,1,0:T(8,128)S(1)}, u32[]{:S(2)}, u32[]{:S(2)}) collective-permute-start(f32[1,4,32,8]{3,2,1,0:T(8,128)S(1)} %get-tuple-element.97), channel_id=1, source_target_pairs={{1,0},{3,2},{5,4},{7,6},{9,8},{11,10},{13,12},{15,14},{17,16},{19,... | collective-permute-start | bytes 12296 | tf_op jit(solution)/shard_map/ppermute | solution.py:21
  52.1 0.8 copy-start.13
  52.1 0.8 copy-start.11
  52.2 0.8 copy-start.6
  52.2 0.8 copy-start.7
  52.2 0.8 copy-start.8
  52.2 0.8 copy-start.9
  52.2 0.8 copy-start.5
  52.2 0.8 copy-start.3
  52.2 0.8 copy-start.4
  53.5 4.9 %copy-start.27 = (f32[16,512]{1,0:T(8,128)S(1)}, f32[16,512]{1,0:T(8,128)}, u32[]{:S(2)}) copy-start(f32[16,512]{1,0:T(8,128)} %get-tuple-element.3) | copy-start | bytes 98308
  53.6 11.3 %collective-permute-start.4 = (f32[1,4,8,512]{3,2,1,0:T(8,128)S(1)}, f32[1,4,8,512]{3,2,1,0:T(8,128)S(1)}, u32[]{:S(2)}, u32[]{:S(2)}) collective-permute-start(f32[1,4,8,512]{3,2,1,0:T(8,128)S(1)} %get-tuple-element.193), channel_id=1, source_target_pairs={{0,4},{4,8},{8,12},{1,5},{5,9},{9,13},{2,6},{6,10},{10,14},{3,7},{... | collective-permute-start | bytes 196616 | tf_op jit(solution)/shard_map/ppermute | solution.py:19
  57.0 7.9 %collective-permute-start.5 = (f32[1,4,8,512]{3,2,1,0:T(8,128)S(1)}, f32[1,4,8,512]{3,2,1,0:T(8,128)S(1)}, u32[]{:S(2)}, u32[]{:S(2)}) collective-permute-start(f32[1,4,8,512]{3,2,1,0:T(8,128)S(1)} %get-tuple-element.194), channel_id=1, source_target_pairs={{4,0},{8,4},{12,8},{5,1},{9,5},{13,9},{6,2},{10,6},{14,10},{7,3},{... | collective-permute-start | bytes 196616 | tf_op jit(solution)/shard_map/ppermute | solution.py:21
  64.9 2.8 %collective-permute-start.6 = (f32[1,4,32,8]{3,2,1,0:T(8,128)S(1)}, f32[1,4,32,8]{3,2,1,0:T(8,128)S(1)}, u32[]{:S(2)}, u32[]{:S(2)}) collective-permute-start(f32[1,4,32,8]{3,2,1,0:T(8,128)S(1)} %get-tuple-element.94), channel_id=1, source_target_pairs={{0,1},{2,3},{4,5},{6,7},{8,9},{10,11},{12,13},{14,15},{16,17},{18,... | collective-permute-start | bytes 12296 | tf_op jit(solution)/shard_map/ppermute | solution.py:19
  66.2 3.1 %collective-permute-start.7 = (f32[1,4,32,8]{3,2,1,0:T(8,128)S(1)}, f32[1,4,32,8]{3,2,1,0:T(8,128)S(1)}, u32[]{:S(2)}, u32[]{:S(2)}) collective-permute-start(f32[1,4,32,8]{3,2,1,0:T(8,128)S(1)} %get-tuple-element.95), channel_id=1, source_target_pairs={{1,0},{3,2},{5,4},{7,6},{9,8},{11,10},{13,12},{15,14},{17,16},{19,... | collective-permute-start | bytes 12296 | tf_op jit(solution)/shard_map/ppermute | solution.py:21
  75.1 6.4 %collective-permute-start.8 = (f32[1,4,8,512]{3,2,1,0:T(8,128)S(1)}, f32[1,4,8,512]{3,2,1,0:T(8,128)S(1)}, u32[]{:S(2)}, u32[]{:S(2)}) collective-permute-start(f32[1,4,8,512]{3,2,1,0:T(8,128)S(1)} %get-tuple-element.187), channel_id=1, source_target_pairs={{0,4},{4,8},{8,12},{1,5},{5,9},{9,13},{2,6},{6,10},{10,14},{3,7},{... | collective-permute-start | bytes 196616 | tf_op jit(solution)/shard_map/ppermute | solution.py:19
  79.7 6.2 %collective-permute-start.9 = (f32[1,4,8,512]{3,2,1,0:T(8,128)S(1)}, f32[1,4,8,512]{3,2,1,0:T(8,128)S(1)}, u32[]{:S(2)}, u32[]{:S(2)}) collective-permute-start(f32[1,4,8,512]{3,2,1,0:T(8,128)S(1)} %get-tuple-element.188), channel_id=1, source_target_pairs={{4,0},{8,4},{12,8},{5,1},{9,5},{13,9},{6,2},{10,6},{14,10},{7,3},{... | collective-permute-start | bytes 196616 | tf_op jit(solution)/shard_map/ppermute | solution.py:21
  85.9 2.8 %collective-permute-start.10 = (f32[1,4,32,8]{3,2,1,0:T(8,128)S(1)}, f32[1,4,32,8]{3,2,1,0:T(8,128)S(1)}, u32[]{:S(2)}, u32[]{:S(2)}) collective-permute-start(f32[1,4,32,8]{3,2,1,0:T(8,128)S(1)} %get-tuple-element.92), channel_id=1, source_target_pairs={{0,1},{2,3},{4,5},{6,7},{8,9},{10,11},{12,13},{14,15},{16,17},{18,... | collective-permute-start | bytes 12296 | tf_op jit(solution)/shard_map/ppermute | solution.py:19
  87.2 3.1 %collective-permute-start.11 = (f32[1,4,32,8]{3,2,1,0:T(8,128)S(1)}, f32[1,4,32,8]{3,2,1,0:T(8,128)S(1)}, u32[]{:S(2)}, u32[]{:S(2)}) collective-permute-start(f32[1,4,32,8]{3,2,1,0:T(8,128)S(1)} %get-tuple-element.93), channel_id=1, source_target_pairs={{1,0},{3,2},{5,4},{7,6},{9,8},{11,10},{13,12},{15,14},{17,16},{19,... | collective-permute-start | bytes 12296 | tf_op jit(solution)/shard_map/ppermute | solution.py:21
  96.1 5.3 %collective-permute-start.12 = (f32[1,4,8,512]{3,2,1,0:T(8,128)S(1)}, f32[1,4,8,512]{3,2,1,0:T(8,128)S(1)}, u32[]{:S(2)}, u32[]{:S(2)}) collective-permute-start(f32[1,4,8,512]{3,2,1,0:T(8,128)S(1)} %get-tuple-element.181), channel_id=1, source_target_pairs={{0,4},{4,8},{8,12},{1,5},{5,9},{9,13},{2,6},{6,10},{10,14},{3,7},{... | collective-permute-start | bytes 196616 | tf_op jit(solution)/shard_map/ppermute | solution.py:19
  99.5 6.2 %collective-permute-start.13 = (f32[1,4,8,512]{3,2,1,0:T(8,128)S(1)}, f32[1,4,8,512]{3,2,1,0:T(8,128)S(1)}, u32[]{:S(2)}, u32[]{:S(2)}) collective-permute-start(f32[1,4,8,512]{3,2,1,0:T(8,128)S(1)} %get-tuple-element.182), channel_id=1, source_target_pairs={{4,0},{8,4},{12,8},{5,1},{9,5},{13,9},{6,2},{10,6},{14,10},{7,3},{... | collective-permute-start | bytes 196616 | tf_op jit(solution)/shard_map/ppermute | solution.py:21
  105.7 2.6 %collective-permute-start.14 = (f32[1,4,32,8]{3,2,1,0:T(8,128)S(1)}, f32[1,4,32,8]{3,2,1,0:T(8,128)S(1)}, u32[]{:S(2)}, u32[]{:S(2)}) collective-permute-start(f32[1,4,32,8]{3,2,1,0:T(8,128)S(1)} %get-tuple-element.90), channel_id=1, source_target_pairs={{0,1},{2,3},{4,5},{6,7},{8,9},{10,11},{12,13},{14,15},{16,17},{18,... | collective-permute-start | bytes 12296 | tf_op jit(solution)/shard_map/ppermute | solution.py:19
  107.0 3.1 %collective-permute-start.15 = (f32[1,4,32,8]{3,2,1,0:T(8,128)S(1)}, f32[1,4,32,8]{3,2,1,0:T(8,128)S(1)}, u32[]{:S(2)}, u32[]{:S(2)}) collective-permute-start(f32[1,4,32,8]{3,2,1,0:T(8,128)S(1)} %get-tuple-element.91), channel_id=1, source_target_pairs={{1,0},{3,2},{5,4},{7,6},{9,8},{11,10},{13,12},{15,14},{17,16},{19,... | collective-permute-start | bytes 12296 | tf_op jit(solution)/shard_map/ppermute | solution.py:21
  (15 other events, 11.7 us)
Sparse Core Ops, SparseCore 0:
  27.0 22.4 all-reduce.2
  116.7 8.5 reduce-scatter.1
where the time goes:
time: 133 us; the launch traced here: 132 us
  starting transfers between devices  33.2 us (25%)
  waiting for transfers between devices  32.2 us (24%)
  between operations  26.7 us (20%)
  other arithmetic  26.5 us (20%)
  local copies, waits for them, and re-layouts  7.93 us (6%)
  matrix products  5.61 us (4%)
    ppermute x8, starting transfers between devices, padded_2(): lax.ppermute(tail, axis, [(i, (i + 1) % count) for i in range(ends)])  22.2 us
    ppermute x8, waiting for transfers between devices, padded_2(): lax.ppermute(head, axis, [((i + 1) % count, i) for i in range(ends)])  15.3 us
    mul x28, other arithmetic, propagate(): (2.0 * stencil(current) - trim_edges(previous, 1)) * trim_edges(inside, o...  14.8 us
    ppermute x8, starting transfers between devices, padded_2(): lax.ppermute(head, axis, [((i + 1) % count, i) for i in range(ends)])  10.9 us
    reduce_scatter x1, waiting for transfers between devices, body(): lax.psum_scatter(jnp.stack(images), 'freq', scatter_dimension=0, tiled=True)  8.7 us
    psum x1, waiting for transfers between devices, spread(): return lax.psum(kept, axis)  7.36 us
    slice x29, other arithmetic, combine(): term[:, 1]  5.18 us
    dot_general x4, matrix products, body(): jnp.dot(selected, weights, precision=highest, preferred_element_type=jnp....  4.92 us
  transfers between devices with their start and end apart: 18, of which 10 were waited for; matrix products, arithmetic and copies ran while one was open for 12% of the time, Pallas kernels for 0%

commit v1 on v0

v1 whole, which is shorter than its diff:
```python
import functools

import jax
import jax.numpy as jnp
from jax import lax
from jax.experimental import pallas as pl
from jax.experimental.pallas import tpu as pltpu
from jax.sharding import PartitionSpec as P

PARTS = 4
LANES = 128
ROWS = 8


def lane_ids():
    return lax.broadcasted_iota(jnp.int32, (ROWS, LANES), 1)


def pick(tile, index):
    return jnp.take_along_axis(tile, index, axis=1)


def interleaved(natural):
    count = len(natural)
    lane = lane_ids()
    span = LANES // count
    home = lane // span
    tiles = []
    for j in range(count):
        index = count * (lane % span) + j
        out = pick(natural[0], index)
        for t in range(1, count):
            out = jnp.where(home == t, pick(natural[t], index), out)
        tiles.append(out)
    return tiles


def straightened(tiles):
    count = len(tiles)
    lane = lane_ids()
    home = lane % count
    natural = []
    for t in range(count):
        index = (LANES // count) * t + lane // count
        out = pick(tiles[0], index)
        for j in range(1, count):
            out = jnp.where(home == j, pick(tiles[j], index), out)
        natural.append(out)
    return natural


def chain_permutation(lat, freq):
    def flat(z, f, c):
        return (z * freq + f) * 2 + c

    pairs = []
    for f in range(freq):
        for z in range(lat - 1):
            pairs.append((flat(z, f, 1), flat(z + 1, f, 0)))
            pairs.append((flat(z + 1, f, 0), flat(z, f, 1)))
        if freq % 2 == 0:
            pairs.append((flat(0, f, 0), flat(0, f ^ 1, 0)))
            pairs.append((flat(lat - 1, f, 1), flat(lat - 1, f ^ 1, 1)))
    return pairs


SWAP = [(0, 1), (1, 0)]


def vmem(count):
    return [pl.BlockSpec(memory_space=pltpu.VMEM)] * count


def pack_fields(x_ref, other_ref, own_ref, mate_ref):
    core = lax.axis_index("sub")
    half = x_ref.shape[3] // LANES
    for target, row in ((own_ref, core), (mate_ref, 1 - core)):
        rows = pl.ds(pl.multiple_of(row * ROWS, ROWS), ROWS)
        for p in range(PARTS):
            mine = [x_ref[0, p, rows, t * LANES : (t + 1) * LANES] for t in range(half)]
            theirs = [other_ref[0, p, rows, t * LANES : (t + 1) * LANES] for t in range(half)]
            left = [jnp.where(core == 0, a, b) for a, b in zip(mine, theirs)]
            right = [jnp.where(core == 0, b, a) for a, b in zip(mine, theirs)]
            for j, tile in enumerate(interleaved(left + right)):
                target[p * 2 * half + j] = tile


def pack_velocity(order_ref, *refs):
    slabs, (keep_ref, send_ref) = refs[:-2], refs[-2:]
    core = lax.axis_index("sub")
    here = lax.axis_index("freq")
    count = len(slabs)
    size = slabs[0].shape[0]
    for d in range(keep_ref.shape[0]):
        stored = order_ref[d]
        slot = lax.rem(stored // size - here + count, count)
        local = lax.rem(stored, size)
        for target, row in ((keep_ref, core), (send_ref, 1 - core)):
            rows = pl.ds(pl.multiple_of(row * ROWS, ROWS), ROWS)
            value = slabs[0][local, rows, :]
            for s in range(1, count):
                value = jnp.where(slot == s, slabs[s][local, rows, :], value)
            target[d] = value


def chebyshev(terms, tiles, kcheb, up_scale, down_scale):
    lane = lane_ids()
    sub = lax.broadcasted_iota(jnp.int32, (ROWS, LANES), 0)
    first = lane == 0
    last = lane == LANES - 1
    half = ROWS // 2
    inside = jnp.full((ROWS, LANES), 0.25, jnp.float32)
    upper = jnp.where(sub < half, up_scale, inside)
    lower = jnp.where(sub >= half, down_scale, inside)
    own = 2 * ROWS
    for k in range(kcheb):
        reach = kcheb - (k + 1)
        if reach > half:
            windows = ((own - ROWS, up_scale), (own, inside), (own + ROWS, down_scale))
        elif reach > 0:
            windows = ((own - half, upper), (own + half, lower))
        else:
            windows = ((own, inside),)
        for row, scale in windows:
            for p in range(PARTS):
                base = p * tiles
                twice = []
                sums = []
                for j in range(tiles):
                    value = terms[k, base + j, pl.ds(row, ROWS), :]
                    double = value + value
                    around = terms[k, base + j, pl.ds(row - 1, ROWS), :] + terms[k, base + j, pl.ds(row + 1, ROWS), :]
                    sums.append(around + double)
                    twice.append(value if k == 0 else double)
                before = jnp.where(first, 0.0, pltpu.roll(sums[tiles - 1], 1, 1))
                after = jnp.where(last, 0.0, pltpu.roll(sums[0], LANES - 1, 1))
                pair = [sums[j] + sums[j + 1] for j in range(tiles - 1)]
                full = [pair[0] + (sums[0] + before)]
                full += [pair[j - 1] + pair[j] for j in range(1, tiles - 1)]
                full.append(pair[tiles - 2] + (sums[tiles - 1] + after))
                for j in range(tiles):
                    if k == 0:
                        new = (0.5 * scale) * full[j] - twice[j]
                    else:
                        new = scale * full[j] - (twice[j] + terms[k - 1, base + j, pl.ds(row, ROWS), :])
                    terms[k + 1, base + j, pl.ds(row, ROWS), :] = new


def combined(terms, velocity, table, tiles, kcheb, bins):
    own = 2 * ROWS
    out = []
    for j in range(tiles):
        v = velocity[j]
        low = jnp.clip(v.astype(jnp.int32), 0, bins - 1)
        part = v - low.astype(jnp.float32)
        total = [None] * PARTS
        for k in range(kcheb + 1):
            a, b = [
                pick(table[0, 2 * k + c], low) + part * pick(table[1, 2 * k + c], low) for c in range(2)
            ]
            sr, si, rr, ri = [terms[k, p * tiles + j, pl.ds(own, ROWS), :] for p in range(PARTS)]
            adds = (a * sr + b * si, a * si - b * sr, a * rr - b * ri, a * ri + b * rr)
            total = [x if y is None else y + x for x, y in zip(adds, total)]
        out.append((total, total[0] * total[2] + total[1] * total[3]))
    return out


def depth_step(depth, kcheb, bins, final, table_ref, keep_ref, other_ref, own_ref, mate_ref, zmate_ref, *refs):
    core = lax.axis_index("sub")
    block = lax.axis_index("lat") * 2 + core
    blocks = 2 * lax.axis_size("lat")
    tiles = own_ref.shape[0] // PARTS
    half = tiles // 2
    if final:
        past, refs = refs[: depth], refs[depth:]
        kept_ref, sub_ref, here_ref, cross_ref, terms, table = refs
    else:
        new_ref, image_ref, terms, table = refs
    own = 2 * ROWS
    up_ok = block > 0
    down_ok = block < blocks - 1
    for i in range(PARTS * tiles):
        terms[0, i, pl.ds(own, ROWS), :] = own_ref[i]
        a = mate_ref[i]
        b = zmate_ref[i]
        terms[0, i, pl.ds(own - ROWS, ROWS), :] = jnp.where(up_ok, jnp.where(core == 0, b, a), 0.0)
        terms[0, i, pl.ds(own + ROWS, ROWS), :] = jnp.where(down_ok, jnp.where(core == 0, a, b), 0.0)
    low = table_ref[...]
    step = pltpu.roll(low, LANES - 1, 1) - low
    for i in range(2 * (kcheb + 1)):
        table[0, i] = jnp.broadcast_to(low[i : i + 1], (ROWS, LANES))
        table[1, i] = jnp.broadcast_to(step[i : i + 1], (ROWS, LANES))
    mine = [keep_ref[depth, :, t * LANES : (t + 1) * LANES] for t in range(half)]
    theirs = [other_ref[depth, :, t * LANES : (t + 1) * LANES] for t in range(half)]
    left = [jnp.where(core == 0, a, b) for a, b in zip(mine, theirs)]
    right = [jnp.where(core == 0, b, a) for a, b in zip(mine, theirs)]
    velocity = interleaved(left + right)

    shape = (ROWS, LANES)
    up_scale = jnp.where(up_ok, jnp.full(shape, 0.25, jnp.float32), 0.0)
    down_scale = jnp.where(down_ok, jnp.full(shape, 0.25, jnp.float32), 0.0)
    chebyshev(terms, tiles, kcheb, up_scale, down_scale)
    result = combined(terms, velocity, table, tiles, kcheb, bins)

    if not final:
        for j, (total, image) in enumerate(result):
            for p in range(PARTS):
                new_ref[p * tiles + j] = total[p]
            image_ref[j] = image
        return
    depths = depth + 1
    owners = lax.axis_size("freq")
    each = depths // owners
    here = lax.axis_index("freq")

    def halves(stack):
        natural = straightened(stack)
        left, right = natural[:half], natural[half:]
        mine = [jnp.where(core == 0, a, b) for a, b in zip(left, right)]
        theirs = [jnp.where(core == 0, b, a) for a, b in zip(left, right)]
        return jnp.concatenate(mine, axis=1), jnp.concatenate(theirs, axis=1)

    for p in range(PARTS):
        mine, theirs = halves([result[j][0][p] for j in range(tiles)])
        kept_ref[p] = mine
        sub_ref[p] = theirs
    for d in range(depths):
        stack = [result[j][1] for j in range(tiles)] if d == depth else [past[d][j] for j in range(tiles)]
        mine, theirs = halves(stack)
        shift = lax.rem(d // each - here + owners, owners)
        slot = d % each

        @pl.when(shift == 0)
        def _():
            kept_ref[PARTS + slot] = mine
            sub_ref[PARTS + slot] = theirs

        @pl.when(shift != 0)
        def _():
            here_ref[shift - 1, slot] = mine
            cross_ref[shift - 1, slot] = theirs


def assemble(kept_ref, sub_ref, *refs):
    pairs, (fields_ref, image_ref) = refs[:-2], refs[-2:]
    core = lax.axis_index("sub")
    each = image_ref.shape[0]
    mine = pl.ds(pl.multiple_of(core * ROWS, ROWS), ROWS)
    theirs = pl.ds(pl.multiple_of((1 - core) * ROWS, ROWS), ROWS)
    for p in range(PARTS):
        fields_ref[0, p, mine, :] = kept_ref[p]
        fields_ref[0, p, theirs, :] = sub_ref[p]
    for d in range(each):
        image_ref[d, mine, :] = functools.reduce(jnp.add, [r[d] for r in pairs[0::2]], kept_ref[PARTS + d])
        image_ref[d, theirs, :] = functools.reduce(jnp.add, [r[d] for r in pairs[1::2]], sub_ref[PARTS + d])


def body(wavefields, velocity, filter_table, freq_pick, slab_order):
    f32 = jnp.float32
    lat = lax.axis_size("lat")
    freq = lax.axis_size("freq")
    bins, _, terms, _ = filter_table.shape
    kcheb = terms - 1
    _, parts, rows, cols = wavefields.shape
    depths = slab_order.shape[0]
    tiles = 2 * cols // LANES
    each = depths // freq
    assert rows == 2 * ROWS and kcheb == ROWS and parts == PARTS and lax.axis_size("sub") == 2

    slabs = [velocity]
    for s in range(1, freq):
        slabs.append(lax.ppermute(velocity, "freq", [((i + s) % freq, i) for i in range(freq)]))
    other = lax.ppermute(wavefields, "sub", SWAP)

    table = lax.dynamic_index_in_dim(filter_table, freq_pick[0], 1, keepdims=False)
    table = table.reshape(bins, 2 * terms).T
    table = jnp.pad(table, ((0, 0), (0, LANES - bins)))

    block = jax.ShapeDtypeStruct((PARTS * tiles, ROWS, LANES), f32)
    own, mate = pl.pallas_call(
        pack_fields, out_shape=(block, block), in_specs=vmem(2), out_specs=tuple(vmem(2)), name="pack_fields"
    )(wavefields, other)
    chain = chain_permutation(lat, freq)
    axes = ("lat", "freq", "sub")
    zmate = lax.ppermute(own, axes, chain)

    strip = jax.ShapeDtypeStruct((depths, ROWS, cols), f32)
    keep, send = pl.pallas_call(
        pack_velocity,
        out_shape=(strip, strip),
        in_specs=[pl.BlockSpec(memory_space=pltpu.SMEM)] + vmem(freq),
        out_specs=tuple(vmem(2)),
        name="pack_velocity",
    )(slab_order, *slabs)
    theirs = lax.ppermute(send, "sub", SWAP)

    scratch = [
        pltpu.VMEM((terms, PARTS * tiles, 5 * ROWS, LANES), f32),
        pltpu.VMEM((2, 2 * terms, ROWS, LANES), f32),
    ]
    images = []
    for depth in range(depths):
        final = depth == depths - 1
        if final:
            out_shape = (
                jax.ShapeDtypeStruct((PARTS + each, ROWS, cols), f32),
                jax.ShapeDtypeStruct((PARTS + each, ROWS, cols), f32),
                jax.ShapeDtypeStruct((freq - 1, each, ROWS, cols), f32),
                jax.ShapeDtypeStruct((freq - 1, each, ROWS, cols), f32),
            )
        else:
            out_shape = (block, jax.ShapeDtypeStruct((tiles, ROWS, LANES), f32))
        args = (table, keep, theirs, own, mate, zmate) + (tuple(images) if final else ())
        out = pl.pallas_call(
            functools.partial(depth_step, depth, kcheb, bins, final),
            out_shape=out_shape,
            in_specs=vmem(len(args)),
            out_specs=tuple(vmem(len(out_shape))),
            scratch_shapes=scratch,
            name="last_step" if final else "depth_step",
        )(*args)
        if not final:
            own, image = out
            images.append(image)
            zmate = lax.ppermute(own, axes, chain)
            mate = lax.ppermute(own, "sub", SWAP)

    kept, sub_send, here_send, cross_send = out
    sub_got = lax.ppermute(sub_send, "sub", SWAP)
    pairs = []
    for s in range(1, freq):
        pairs.append(lax.ppermute(here_send[s - 1], "freq", [(i, (i + s) % freq) for i in range(freq)]))
        cross = [(2 * i + c, 2 * ((i + s) % freq) + 1 - c) for i in range(freq) for c in range(2)]
        pairs.append(lax.ppermute(cross_send[s - 1], ("freq", "sub"), cross))
    return pl.pallas_call(
        assemble,
        out_shape=(
            jax.ShapeDtypeStruct(wavefields.shape, f32),
            jax.ShapeDtypeStruct((each, rows, cols), f32),
        ),
        in_specs=vmem(2 + len(pairs)),
        out_specs=tuple(vmem(2)),
        name="assemble",
    )(kept, sub_got, *pairs)


def solution(mesh):
    return jax.shard_map(
        body,
        mesh=mesh,
        in_specs=(
            P(("shots", "freq"), None, "lat", "sub"),
            P("freq", "lat", "sub"),
            P(),
            P("freq"),
            P(),
        ),
        out_specs=(P(("shots", "freq"), None, "lat", "sub"), P(("shots", "freq"), "lat", "sub")),
        check_vma=False,
    )
```

time: 133 us -> 52.6 us (0.40)
  other arithmetic: 26.5 us -> 0 us
  between operations: 26.7 us -> 1.36 us
  starting transfers between devices: 33.2 us -> 11.2 us
  Pallas kernels: 0 us -> 18.4 us
  waiting for transfers between devices: 32.2 us -> 14.3 us
  matrix products: 5.61 us -> 0 us
    ppermute x16 -> x13, starting transfers between devices: 33.1 us -> 11.2 us  [the longest x4 5.74 us: body(): zmate = lax.ppermute(own, axes, chain)]
    pallas_call x0 -> x7, Pallas kernels: none -> 18.4 us  [the longest x4 12.6 us: body(): pl.pallas_call(functools.partial(depth_step, depth, kcheb, bins, final),...]
    mul x32 -> x0, other arithmetic: 17.1 us -> none  [the longest x28 14.8 us: propagate(): (2.0 * stencil(current) - trim_edges(previous, 1)) * trim_edges(inside, o...]
    reduce_scatter x1 -> x0, waiting for transfers between devices: 8.7 us -> none  [body(): lax.psum_scatter(jnp.stack(images), 'freq', scatter_dimension=0, tiled=True)]
    psum x1 -> x0, waiting for transfers between devices: 7.36 us -> none  [spread(): return lax.psum(kept, axis)]
    dot_general x5 -> x0, matrix products: 5.61 us -> none  [the longest x4 4.92 us: body(): jnp.dot(selected, weights, precision=highest, preferred_element_type=jnp....]
    slice x32 -> x0, other arithmetic: 5.43 us -> none  [the longest x29 5.18 us: combine(): term[:, 1]]
    unnamed x128 -> x28, local copies, waits for them, and re-layouts: 3.4 us -> 5.95 us
  transfers between devices with their start and end apart: 18 -> 13, of which waited for: 10 -> 6; matrix products, arithmetic and copies ran while one was open for 12% -> 2% of each run, Pallas kernels for 0% -> 8%
where the time goes in v1:
time: 52.6 us; the launch traced here: 52.3 us
  Pallas kernels  18.4 us (35%)
  waiting for transfers between devices  14.3 us (27%)
  starting transfers between devices  11.2 us (21%)
  local copies, waits for them, and re-layouts  7.13 us (14%)
  between operations  1.36 us (3%)
    pallas_call x4, Pallas kernels, body(): pl.pallas_call(functools.partial(depth_step, depth, kcheb, bins, final),...  12.6 us
    ppermute x4, waiting for transfers between devices, body(): zmate = lax.ppermute(own, axes, chain)  11 us
    unnamed x28, local copies, waits for them, and re-layouts  5.95 us
    ppermute x4, starting transfers between devices, body(): zmate = lax.ppermute(own, axes, chain)  5.74 us
    ppermute x1, starting transfers between devices, body(): lax.ppermute(velocity, 'freq', [((i + s) % freq, i) for i in range(freq)])  2.55 us
    pallas_call x1, Pallas kernels, body(): pl.pallas_call(pack_fields, out_shape=(block, block), in_specs=vmem(2), o...  2.44 us
    ppermute x1, waiting for transfers between devices, body(): lax.ppermute(here_send[s - 1], 'freq', [(i, (i + s) % freq) for i in rang...  2.32 us
    pallas_call x1, Pallas kernels, body(): pl.pallas_call(pack_velocity, out_shape=(strip, strip), in_specs=[pl.Bloc...  1.68 us
  transfers between devices with their start and end apart: 13, of which 6 were waited for; matrix products, arithmetic and copies ran while one was open for 2% of the time, Pallas kernels for 8%

profile of v1, /device:TPU:0, one launch (start us, length us, event | category | flops | bytes accessed | tf_op | source)
XLA Modules:
  0.0 52.3 jit_solution(1609701879761045085)
XLA Ops:
  0.6 0.6 %collective-permute-start.2 = (f32[1,4,16,512]{3,2,1,0:T(8,128)}, f32[1,4,16,512]{3,2,1,0:T(8,128)S(1)}, u32[]{:S(2)}, u32[]{:S(2)}) collective-permute-start(f32[1,4,16,512]{3,2,1,0:T(8,128)} %x_ref.1), channel_id=1, source_target_pairs={{0,1},{1,0},{2,3},{3,2},{4,5},{5,4},{6,7},{7,6},{8,9},{9,8},{10,11... | collective-permute-start | bytes 393224 | tf_op jit(solution)/shard_map/ppermute | solution.py:273
  1.2 2.6 %collective-permute-start = (f32[4,16,512]{2,1,0:T(8,128)}, f32[4,16,512]{2,1,0:T(8,128)S(1)}, u32[]{:S(2)}, u32[]{:S(2)}) collective-permute-start(f32[4,16,512]{2,1,0:T(8,128)} %refs_0_.1), channel_id=1, source_target_pairs={{2,0},{0,2},{3,1},{1,3},{6,4},{4,6},{7,5},{5,7},{10,8},{8,10},{11,... | collective-permute-start | bytes 393224 | tf_op jit(solution)/shard_map/ppermute | solution.py:272
  3.8 0.7 %copy-done.5 = f32[1,4,16,512]{3,2,1,0:T(8,128)} copy-done((f32[1,4,16,512]{3,2,1,0:T(8,128)}, f32[1,4,16,512]{3,2,1,0:T(8,128)S(1)}, u32[]{:S(2)}) %copy-start.5) | copy-done | bytes 131096
  4.4 2.4 %pack_fields.1 = (f32[32,8,128]{2,1,0:T(8,128)}, f32[32,8,128]{2,1,0:T(8,128)}) custom-call(f32[1,4,16,512]{3,2,1,0:T(8,128)} %x_ref.1, f32[1,4,16,512]{3,2,1,0:T(8,128)} %copy-done.5), custom_call_target="tpu_custom_call" | custom-call | tf_op jit(solution)/shard_map/pack_fields/pallas_call | solution.py:280
  6.9 1.5 %collective-permute-start.3 = (f32[32,8,128]{2,1,0:T(8,128)}, f32[32,8,128]{2,1,0:T(8,128)S(1)}, u32[]{:S(2)}, u32[]{:S(2)}) collective-permute-start(f32[32,8,128]{2,1,0:T(8,128)} %get-tuple-element.18.own_ref), channel_id=1, source_target_pairs={{1,4},{4,1},{5,8},{8,5},{9,12},{12,9},{0,2},{13,15},{3,6},{6,3},{7... | collective-permute-start | bytes 393224 | tf_op jit(solution)/shard_map/ppermute | solution.py:285
  9.0 0.6 %copy-done.4 = f32[4,16,512]{2,1,0:T(8,128)} copy-done((f32[4,16,512]{2,1,0:T(8,128)}, f32[4,16,512]{2,1,0:T(8,128)S(1)}, u32[]{:S(2)}) %copy-start.4) | copy-done | bytes 131096
  9.7 1.7 %pack_velocity.1 = (f32[4,8,512]{2,1,0:T(8,128)}, f32[4,8,512]{2,1,0:T(8,128)}) custom-call(s32[4]{0:T(128)} %order_ref.1, f32[4,16,512]{2,1,0:T(8,128)} %refs_0_.1, f32[4,16,512]{2,1,0:T(8,128)} %copy-done.4), custom_call_target="tpu_custom_call" | custom-call | tf_op jit(solution)/shard_map/pack_velocity/pallas_call | solution.py:288
  11.3 0.2 collective-permute-start.1
  11.6 0.4 constant_dynamic-slice_fusion
  12.1 0.6 %pad.4.table_ref = f32[18,128]{1,0:T(8,128)} pad(f32[18,32]{1,0:T(8,128)S(1)} %bitcast.9, f32[]{:T(128)} %constant.8.clone.1), padding=0_0x0_96 | pad | bytes 11524 | tf_op jit(solution)/shard_map/jit(_pad)/pad | solution.py:277
  12.8 0.6 %copy-done.1 = f32[4,8,512]{2,1,0:T(8,128)} copy-done((f32[4,8,512]{2,1,0:T(8,128)}, f32[4,8,512]{2,1,0:T(8,128)S(1)}, u32[]{:S(2)}) %copy-start.1) | copy-done | bytes 65560
  13.5 2.9 %depth_step.3 = (f32[32,8,128]{2,1,0:T(8,128)}, f32[8,8,128]{2,1,0:T(8,128)}) custom-call(f32[18,128]{1,0:T(8,128)} %pad.4.table_ref, f32[4,8,512]{2,1,0:T(8,128)} %get-tuple-element.16.keep_ref, f32[4,8,512]{2,1,0:T(8,128)} %copy-done.1, f32[32,8,128]{2,1,0:T(8,128)} %get-tuple-element.18.own_ref, f32[32,8,128]{2,1,0:T(8,128)} %get-tuple-element.19.mate_ref, ...), custom_call_target="tpu_custom_call" | custom-call | tf_op jit(solution)/shard_map/depth_step/pallas_call | solution.py:314
  16.4 1.4 %collective-permute-start.5 = (f32[32,8,128]{2,1,0:T(8,128)}, f32[32,8,128]{2,1,0:T(8,128)S(1)}, u32[]{:S(2)}, u32[]{:S(2)}) collective-permute-start(f32[32,8,128]{2,1,0:T(8,128)} %get-tuple-element.20.own_ref), channel_id=1, source_target_pairs={{1,4},{4,1},{5,8},{8,5},{9,12},{12,9},{0,2},{13,15},{3,6},{6,3},{7... | collective-permute-start | bytes 393224 | tf_op jit(solution)/shard_map/ppermute | solution.py:325
  18.0 3.5 %collective-permute-done.5.zmate_ref = f32[32,8,128]{2,1,0:T(8,128)S(1)} collective-permute-done((f32[32,8,128]{2,1,0:T(8,128)}, f32[32,8,128]{2,1,0:T(8,128)S(1)}, u32[]{:S(2)}, u32[]{:S(2)}) %collective-permute-start.5) | collective-permute-done | bytes 131104 | tf_op jit(solution)/shard_map/ppermute | solution.py:325
  21.6 0.6 %copy-done.7 = f32[32,8,128]{2,1,0:T(8,128)} copy-done((f32[32,8,128]{2,1,0:T(8,128)}, f32[32,8,128]{2,1,0:T(8,128)S(1)}, u32[]{:S(2)}) %copy-start.7) | copy-done | bytes 131096
  22.2 0.7 %copy-done.9 = f32[32,8,128]{2,1,0:T(8,128)} copy-done((f32[32,8,128]{2,1,0:T(8,128)}, f32[32,8,128]{2,1,0:T(8,128)S(1)}, u32[]{:S(2)}) %copy-start.9) | copy-done | bytes 131096
  22.9 2.9 %depth_step.4 = (f32[32,8,128]{2,1,0:T(8,128)}, f32[8,8,128]{2,1,0:T(8,128)}) custom-call(f32[18,128]{1,0:T(8,128)} %pad.4.table_ref, f32[4,8,512]{2,1,0:T(8,128)} %get-tuple-element.16.keep_ref, f32[4,8,512]{2,1,0:T(8,128)} %copy-done.1, f32[32,8,128]{2,1,0:T(8,128)} %get-tuple-element.20.own_ref, f32[32,8,128]{2,1,0:T(8,128)} %copy-done.9, ...), custom_call_target="tpu_custom_call" | custom-call | tf_op jit(solution)/shard_map/depth_step/pallas_call | solution.py:314
  25.8 1.4 %collective-permute-start.7 = (f32[32,8,128]{2,1,0:T(8,128)}, f32[32,8,128]{2,1,0:T(8,128)S(1)}, u32[]{:S(2)}, u32[]{:S(2)}) collective-permute-start(f32[32,8,128]{2,1,0:T(8,128)} %get-tuple-element.21.own_ref), channel_id=1, source_target_pairs={{1,4},{4,1},{5,8},{8,5},{9,12},{12,9},{0,2},{13,15},{3,6},{6,3},{7... | collective-permute-start | bytes 393224 | tf_op jit(solution)/shard_map/ppermute | solution.py:325
  27.2 3.8 %collective-permute-done.7.zmate_ref = f32[32,8,128]{2,1,0:T(8,128)S(1)} collective-permute-done((f32[32,8,128]{2,1,0:T(8,128)}, f32[32,8,128]{2,1,0:T(8,128)S(1)}, u32[]{:S(2)}, u32[]{:S(2)}) %collective-permute-start.7) | collective-permute-done | bytes 131104 | tf_op jit(solution)/shard_map/ppermute | solution.py:325
  31.0 0.7 %copy-done.8 = f32[32,8,128]{2,1,0:T(8,128)} copy-done((f32[32,8,128]{2,1,0:T(8,128)}, f32[32,8,128]{2,1,0:T(8,128)S(1)}, u32[]{:S(2)}) %copy-start.8) | copy-done | bytes 131096
  31.6 0.7 %copy-done.10 = f32[32,8,128]{2,1,0:T(8,128)} copy-done((f32[32,8,128]{2,1,0:T(8,128)}, f32[32,8,128]{2,1,0:T(8,128)S(1)}, u32[]{:S(2)}) %copy-start.10) | copy-done | bytes 131096
  32.3 2.9 %depth_step.5 = (f32[32,8,128]{2,1,0:T(8,128)}, f32[8,8,128]{2,1,0:T(8,128)}) custom-call(f32[18,128]{1,0:T(8,128)} %pad.4.table_ref, f32[4,8,512]{2,1,0:T(8,128)} %get-tuple-element.16.keep_ref, f32[4,8,512]{2,1,0:T(8,128)} %copy-done.1, f32[32,8,128]{2,1,0:T(8,128)} %get-tuple-element.21.own_ref, f32[32,8,128]{2,1,0:T(8,128)} %copy-done.10, ...), custom_call_target="tpu_custom_call" | custom-call | tf_op jit(solution)/shard_map/depth_step/pallas_call | solution.py:314
  35.2 1.4 %collective-permute-start.9 = (f32[32,8,128]{2,1,0:T(8,128)}, f32[32,8,128]{2,1,0:T(8,128)S(1)}, u32[]{:S(2)}, u32[]{:S(2)}) collective-permute-start(f32[32,8,128]{2,1,0:T(8,128)} %get-tuple-element.22.own_ref), channel_id=1, source_target_pairs={{1,4},{4,1},{5,8},{8,5},{9,12},{12,9},{0,2},{13,15},{3,6},{6,3},{7... | collective-permute-start | bytes 393224 | tf_op jit(solution)/shard_map/ppermute | solution.py:325
  36.6 3.8 %collective-permute-done.9.zmate_ref = f32[32,8,128]{2,1,0:T(8,128)S(1)} collective-permute-done((f32[32,8,128]{2,1,0:T(8,128)}, f32[32,8,128]{2,1,0:T(8,128)S(1)}, u32[]{:S(2)}, u32[]{:S(2)}) %collective-permute-start.9) | collective-permute-done | bytes 131104 | tf_op jit(solution)/shard_map/ppermute | solution.py:325
  40.4 0.6 %copy-done.2 = f32[32,8,128]{2,1,0:T(8,128)} copy-done((f32[32,8,128]{2,1,0:T(8,128)}, f32[32,8,128]{2,1,0:T(8,128)S(1)}, u32[]{:S(2)}) %copy-start.2) | copy-done | bytes 131096
  41.1 3.9 %last_step.1 = (f32[6,8,512]{2,1,0:T(8,128)}, f32[6,8,512]{2,1,0:T(8,128)}, f32[1,2,8,512]{3,2,1,0:T(8,128)}, f32[1,2,8,512]{3,2,1,0:T(8,128)}) custom-call(f32[18,128]{1,0:T(8,128)} %pad.4.table_ref, f32[4,8,512]{2,1,0:T(8,128)} %get-tuple-element.16.keep_ref, f32[4,8,512]{2,1,0:T(8,128)} %copy-done.1, f32[32,8,128]{2,1,0:T(8,128)} %get-tuple-element.22.own_ref, ...), custom_call_target="tpu_custom_call" | custom-call | tf_op jit(solution)/shard_map/last_step/pallas_call | solution.py:314
  45.0 1.5 %collective-permute-start.11 = (f32[2,8,512]{2,1,0:T(8,128)}, f32[2,8,512]{2,1,0:T(8,128)S(1)}, u32[]{:S(2)}, u32[]{:S(2)}) collective-permute-start(f32[2,8,512]{2,1,0:T(8,128)} %bitcast.11), channel_id=1, source_target_pairs={{0,2},{2,0},{1,3},{3,1},{4,6},{6,4},{5,7},{7,5},{8,10},{10,8},{9,1... | collective-permute-start | bytes 98312 | tf_op jit(solution)/shard_map/ppermute | solution.py:332
  46.4 0.4 collective-permute-start.12
  46.8 2.3 %collective-permute-done.11.refs_0_ = f32[2,8,512]{2,1,0:T(8,128)S(1)} collective-permute-done((f32[2,8,512]{2,1,0:T(8,128)}, f32[2,8,512]{2,1,0:T(8,128)S(1)}, u32[]{:S(2)}, u32[]{:S(2)}) %collective-permute-start.11) | collective-permute-done | bytes 32800 | tf_op jit(solution)/shard_map/ppermute | solution.py:332
  49.1 0.8 %collective-permute-done.12.refs_1_ = f32[2,8,512]{2,1,0:T(8,128)S(1)} collective-permute-done((f32[2,8,512]{2,1,0:T(8,128)}, f32[2,8,512]{2,1,0:T(8,128)S(1)}, u32[]{:S(2)}, u32[]{:S(2)}) %collective-permute-start.12) | collective-permute-done | bytes 32800 | tf_op jit(solution)/shard_map/ppermute | solution.py:334
  50.0 0.6 %copy-done.13 = f32[2,8,512]{2,1,0:T(8,128)} copy-done((f32[2,8,512]{2,1,0:T(8,128)}, f32[2,8,512]{2,1,0:T(8,128)S(1)}, u32[]{:S(2)}) %copy-start.13) | copy-done | bytes 32792
  50.7 1.6 %assemble.1 = (f32[1,4,16,512]{3,2,1,0:T(8,128)}, f32[2,16,512]{2,1,0:T(8,128)}) custom-call(f32[6,8,512]{2,1,0:T(8,128)} %get-tuple-element.26.kept_ref, f32[6,8,512]{2,1,0:T(8,128)} %copy-done.11, f32[2,8,512]{2,1,0:T(8,128)} %copy-done.12, f32[2,8,512]{2,1,0:T(8,128)} %copy-done.13), custom_call_target="tpu_custom_call" | custom-call | tf_op jit(solution)/shard_map/assemble/pallas_call | solution.py:335
  (33 shorter events, 0.7 us)
Async XLA Ops:
  0.6 10.9 %copy-start = (f32[32,32,9,2]{1,3,2,0:T(2,128)S(1)}, f32[32,32,9,2]{1,3,2,0:T(2,128)}, u32[]{:S(2)}) copy-start(f32[32,32,9,2]{1,3,2,0:T(2,128)} %param.7) | copy-start | bytes 221188
  0.6 3.1 %collective-permute-start.2 = (f32[1,4,16,512]{3,2,1,0:T(8,128)}, f32[1,4,16,512]{3,2,1,0:T(8,128)S(1)}, u32[]{:S(2)}, u32[]{:S(2)}) collective-permute-start(f32[1,4,16,512]{3,2,1,0:T(8,128)} %x_ref.1), channel_id=1, source_target_pairs={{0,1},{1,0},{2,3},{3,2},{4,5},{5,4},{6,7},{7,6},{8,9},{9,8},{10,11... | collective-permute-start | bytes 393224 | tf_op jit(solution)/shard_map/ppermute | solution.py:273
  1.2 7.8 %collective-permute-start = (f32[4,16,512]{2,1,0:T(8,128)}, f32[4,16,512]{2,1,0:T(8,128)S(1)}, u32[]{:S(2)}, u32[]{:S(2)}) collective-permute-start(f32[4,16,512]{2,1,0:T(8,128)} %refs_0_.1), channel_id=1, source_target_pairs={{2,0},{0,2},{3,1},{1,3},{6,4},{4,6},{7,5},{5,7},{10,8},{8,10},{11,... | collective-permute-start | bytes 393224 | tf_op jit(solution)/shard_map/ppermute | solution.py:272
  3.8 0.7 %copy-start.5 = (f32[1,4,16,512]{3,2,1,0:T(8,128)}, f32[1,4,16,512]{3,2,1,0:T(8,128)S(1)}, u32[]{:S(2)}) copy-start(f32[1,4,16,512]{3,2,1,0:T(8,128)S(1)} %collective-permute-done.2.other_ref) | copy-start | bytes 393220
  6.9 6.0 %collective-permute-start.3 = (f32[32,8,128]{2,1,0:T(8,128)}, f32[32,8,128]{2,1,0:T(8,128)S(1)}, u32[]{:S(2)}, u32[]{:S(2)}) collective-permute-start(f32[32,8,128]{2,1,0:T(8,128)} %get-tuple-element.18.own_ref), channel_id=1, source_target_pairs={{1,4},{4,1},{5,8},{8,5},{9,12},{12,9},{0,2},{13,15},{3,6},{6,3},{7... | collective-permute-start | bytes 393224 | tf_op jit(solution)/shard_map/ppermute | solution.py:285
  9.0 0.7 %copy-start.4 = (f32[4,16,512]{2,1,0:T(8,128)}, f32[4,16,512]{2,1,0:T(8,128)S(1)}, u32[]{:S(2)}) copy-start(f32[4,16,512]{2,1,0:T(8,128)S(1)} %collective-permute-done.refs_1_) | copy-start | bytes 393220
  11.3 1.5 %collective-permute-start.1 = (f32[4,8,512]{2,1,0:T(8,128)}, f32[4,8,512]{2,1,0:T(8,128)S(1)}, u32[]{:S(2)}, u32[]{:S(2)}) collective-permute-start(f32[4,8,512]{2,1,0:T(8,128)} %get-tuple-element.17), channel_id=1, source_target_pairs={{0,1},{1,0},{2,3},{3,2},{4,5},{5,4},{6,7},{7,6},{8,9},{9,8},{10,11... | collective-permute-start | bytes 196616 | tf_op jit(solution)/shard_map/ppermute | solution.py:295
  12.8 0.6 %copy-start.1 = (f32[4,8,512]{2,1,0:T(8,128)}, f32[4,8,512]{2,1,0:T(8,128)S(1)}, u32[]{:S(2)}) copy-start(f32[4,8,512]{2,1,0:T(8,128)S(1)} %collective-permute-done.1.other_ref) | copy-start | bytes 196612
  12.8 0.7 %copy-start.6 = (f32[32,8,128]{2,1,0:T(8,128)}, f32[32,8,128]{2,1,0:T(8,128)S(1)}, u32[]{:S(2)}) copy-start(f32[32,8,128]{2,1,0:T(8,128)S(1)} %collective-permute-done.3.zmate_ref) | copy-start | bytes 393220
  16.4 5.2 %collective-permute-start.5 = (f32[32,8,128]{2,1,0:T(8,128)}, f32[32,8,128]{2,1,0:T(8,128)S(1)}, u32[]{:S(2)}, u32[]{:S(2)}) collective-permute-start(f32[32,8,128]{2,1,0:T(8,128)} %get-tuple-element.20.own_ref), channel_id=1, source_target_pairs={{1,4},{4,1},{5,8},{8,5},{9,12},{12,9},{0,2},{13,15},{3,6},{6,3},{7... | collective-permute-start | bytes 393224 | tf_op jit(solution)/shard_map/ppermute | solution.py:325
  17.8 3.8 %collective-permute-start.4 = (f32[32,8,128]{2,1,0:T(8,128)}, f32[32,8,128]{2,1,0:T(8,128)S(1)}, u32[]{:S(2)}, u32[]{:S(2)}) collective-permute-start(f32[32,8,128]{2,1,0:T(8,128)} %get-tuple-element.20.own_ref), channel_id=1, source_target_pairs={{0,1},{1,0},{2,3},{3,2},{4,5},{5,4},{6,7},{7,6},{8,9},{9,8},{10,11... | collective-permute-start | bytes 393224 | tf_op jit(solution)/shard_map/ppermute | solution.py:326
  21.6 0.7 %copy-start.7 = (f32[32,8,128]{2,1,0:T(8,128)}, f32[32,8,128]{2,1,0:T(8,128)S(1)}, u32[]{:S(2)}) copy-start(f32[32,8,128]{2,1,0:T(8,128)S(1)} %collective-permute-done.5.zmate_ref) | copy-start | bytes 393220
  22.2 0.7 %copy-start.9 = (f32[32,8,128]{2,1,0:T(8,128)}, f32[32,8,128]{2,1,0:T(8,128)S(1)}, u32[]{:S(2)}) copy-start(f32[32,8,128]{2,1,0:T(8,128)S(1)} %collective-permute-done.4.mate_ref) | copy-start | bytes 393220
  25.8 5.2 %collective-permute-start.7 = (f32[32,8,128]{2,1,0:T(8,128)}, f32[32,8,128]{2,1,0:T(8,128)S(1)}, u32[]{:S(2)}, u32[]{:S(2)}) collective-permute-start(f32[32,8,128]{2,1,0:T(8,128)} %get-tuple-element.21.own_ref), channel_id=1, source_target_pairs={{1,4},{4,1},{5,8},{8,5},{9,12},{12,9},{0,2},{13,15},{3,6},{6,3},{7... | collective-permute-start | bytes 393224 | tf_op jit(solution)/shard_map/ppermute | solution.py:325
  27.2 3.8 %collective-permute-start.6 = (f32[32,8,128]{2,1,0:T(8,128)}, f32[32,8,128]{2,1,0:T(8,128)S(1)}, u32[]{:S(2)}, u32[]{:S(2)}) collective-permute-start(f32[32,8,128]{2,1,0:T(8,128)} %get-tuple-element.21.own_ref), channel_id=1, source_target_pairs={{0,1},{1,0},{2,3},{3,2},{4,5},{5,4},{6,7},{7,6},{8,9},{9,8},{10,11... | collective-permute-start | bytes 393224 | tf_op jit(solution)/shard_map/ppermute | solution.py:326
  31.0 0.7 %copy-start.8 = (f32[32,8,128]{2,1,0:T(8,128)}, f32[32,8,128]{2,1,0:T(8,128)S(1)}, u32[]{:S(2)}) copy-start(f32[32,8,128]{2,1,0:T(8,128)S(1)} %collective-permute-done.7.zmate_ref) | copy-start | bytes 393220
  31.6 0.7 %copy-start.10 = (f32[32,8,128]{2,1,0:T(8,128)}, f32[32,8,128]{2,1,0:T(8,128)S(1)}, u32[]{:S(2)}) copy-start(f32[32,8,128]{2,1,0:T(8,128)S(1)} %collective-permute-done.6.mate_ref) | copy-start | bytes 393220
  35.2 5.2 %collective-permute-start.9 = (f32[32,8,128]{2,1,0:T(8,128)}, f32[32,8,128]{2,1,0:T(8,128)S(1)}, u32[]{:S(2)}, u32[]{:S(2)}) collective-permute-start(f32[32,8,128]{2,1,0:T(8,128)} %get-tuple-element.22.own_ref), channel_id=1, source_target_pairs={{1,4},{4,1},{5,8},{8,5},{9,12},{12,9},{0,2},{13,15},{3,6},{6,3},{7... | collective-permute-start | bytes 393224 | tf_op jit(solution)/shard_map/ppermute | solution.py:325
  36.6 3.8 %collective-permute-start.8 = (f32[32,8,128]{2,1,0:T(8,128)}, f32[32,8,128]{2,1,0:T(8,128)S(1)}, u32[]{:S(2)}, u32[]{:S(2)}) collective-permute-start(f32[32,8,128]{2,1,0:T(8,128)} %get-tuple-element.22.own_ref), channel_id=1, source_target_pairs={{0,1},{1,0},{2,3},{3,2},{4,5},{5,4},{6,7},{7,6},{8,9},{9,8},{10,11... | collective-permute-start | bytes 393224 | tf_op jit(solution)/shard_map/ppermute | solution.py:326
  40.4 0.7 %copy-start.2 = (f32[32,8,128]{2,1,0:T(8,128)}, f32[32,8,128]{2,1,0:T(8,128)S(1)}, u32[]{:S(2)}) copy-start(f32[32,8,128]{2,1,0:T(8,128)S(1)} %collective-permute-done.9.zmate_ref) | copy-start | bytes 393220
  40.4 0.7 %copy-start.3 = (f32[32,8,128]{2,1,0:T(8,128)}, f32[32,8,128]{2,1,0:T(8,128)S(1)}, u32[]{:S(2)}) copy-start(f32[32,8,128]{2,1,0:T(8,128)S(1)} %collective-permute-done.8.mate_ref) | copy-start | bytes 393220
  45.0 5.0 %collective-permute-start.10 = (f32[6,8,512]{2,1,0:T(8,128)}, f32[6,8,512]{2,1,0:T(8,128)S(1)}, u32[]{:S(2)}, u32[]{:S(2)}) collective-permute-start(f32[6,8,512]{2,1,0:T(8,128)} %get-tuple-element.27), channel_id=1, source_target_pairs={{0,1},{1,0},{2,3},{3,2},{4,5},{5,4},{6,7},{7,6},{8,9},{9,8},{10,11... | collective-permute-start | bytes 294920 | tf_op jit(solution)/shard_map/ppermute | solution.py:329
  45.0 4.2 %collective-permute-start.11 = (f32[2,8,512]{2,1,0:T(8,128)}, f32[2,8,512]{2,1,0:T(8,128)S(1)}, u32[]{:S(2)}, u32[]{:S(2)}) collective-permute-start(f32[2,8,512]{2,1,0:T(8,128)} %bitcast.11), channel_id=1, source_target_pairs={{0,2},{2,0},{1,3},{3,1},{4,6},{6,4},{5,7},{7,5},{8,10},{10,8},{9,1... | collective-permute-start | bytes 98312 | tf_op jit(solution)/shard_map/ppermute | solution.py:332
  46.4 3.6 %collective-permute-start.12 = (f32[2,8,512]{2,1,0:T(8,128)}, f32[2,8,512]{2,1,0:T(8,128)S(1)}, u32[]{:S(2)}, u32[]{:S(2)}) collective-permute-start(f32[2,8,512]{2,1,0:T(8,128)} %bitcast.10), channel_id=1, source_target_pairs={{0,3},{1,2},{2,1},{3,0},{4,7},{5,6},{6,5},{7,4},{8,11},{9,10},{10,... | collective-permute-start | bytes 98312 | tf_op jit(solution)/shard_map/ppermute | solution.py:334
  49.1 0.9 %copy-start.12 = (f32[2,8,512]{2,1,0:T(8,128)}, f32[2,8,512]{2,1,0:T(8,128)S(1)}, u32[]{:S(2)}) copy-start(f32[2,8,512]{2,1,0:T(8,128)S(1)} %collective-permute-done.11.refs_0_) | copy-start | bytes 98308
  50.0 0.6 %copy-start.13 = (f32[2,8,512]{2,1,0:T(8,128)}, f32[2,8,512]{2,1,0:T(8,128)S(1)}, u32[]{:S(2)}) copy-start(f32[2,8,512]{2,1,0:T(8,128)S(1)} %collective-permute-done.12.refs_1_) | copy-start | bytes 98308
  50.0 0.7 %copy-start.11 = (f32[6,8,512]{2,1,0:T(8,128)}, f32[6,8,512]{2,1,0:T(8,128)S(1)}, u32[]{:S(2)}) copy-start(f32[6,8,512]{2,1,0:T(8,128)S(1)} %collective-permute-done.10.sub_ref) | copy-start | bytes 294916

commit v2 on v1

--- a/solution.py
+++ b/solution.py
@@ -65,6 +65,8 @@
 
 
 SWAP = [(0, 1), (1, 0)]
+SMALL = pltpu.CompilerParams(vmem_limit_bytes=4 << 20)
+STEP = pltpu.CompilerParams(vmem_limit_bytes=12 << 20)
 
 
 def vmem(count):
@@ -278,7 +280,8 @@
 
     block = jax.ShapeDtypeStruct((PARTS * tiles, ROWS, LANES), f32)
     own, mate = pl.pallas_call(
-        pack_fields, out_shape=(block, block), in_specs=vmem(2), out_specs=tuple(vmem(2)), name="pack_fields"
+        pack_fields, out_shape=(block, block), in_specs=vmem(2), out_specs=tuple(vmem(2)), compiler_params=SMALL,
+        name="pack_fields",
     )(wavefields, other)
     chain = chain_permutation(lat, freq)
     axes = ("lat", "freq", "sub")
@@ -290,6 +293,7 @@
         out_shape=(strip, strip),
         in_specs=[pl.BlockSpec(memory_space=pltpu.SMEM)] + vmem(freq),
         out_specs=tuple(vmem(2)),
+        compiler_params=SMALL,
         name="pack_velocity",
     )(slab_order, *slabs)
     theirs = lax.ppermute(send, "sub", SWAP)
@@ -317,6 +321,7 @@
             in_specs=vmem(len(args)),
             out_specs=tuple(vmem(len(out_shape))),
             scratch_shapes=scratch,
+            compiler_params=STEP,
             name="last_step" if final else "depth_step",
         )(*args)
         if not final:
@@ -340,6 +345,7 @@
         ),
         in_specs=vmem(2 + len(pairs)),
         out_specs=tuple(vmem(2)),
+        compiler_params=SMALL,
         name="assemble",
     )(kept, sub_got, *pairs)
 

time: 52.6 us -> 36.9 us (0.70)
  Pallas kernels: 18.4 us -> 7.56 us
  local copies, waits for them, and re-layouts: 7.13 us -> 1.77 us
    pallas_call x4, Pallas kernels: 12.6 us -> 5.46 us  [body(): pl.pallas_call(functools.partial(depth_step, depth, kcheb, bins, final),...]
    unnamed x28 -> x8, local copies, waits for them, and re-layouts: 5.95 us -> 1.19 us
    pallas_call x1, Pallas kernels: 2.44 us -> 0.81 us  [body(): pl.pallas_call(pack_fields, out_shape=(block, block), in_specs=vmem(2), o...]
    pallas_call x1, Pallas kernels: 1.68 us -> 0.59 us  [body(): pl.pallas_call(pack_velocity, out_shape=(strip, strip), in_specs=[pl.Bloc...]
    pallas_call x1, Pallas kernels: 1.64 us -> 0.7 us  [body(): pl.pallas_call(assemble, out_shape=(jax.ShapeDtypeStruct(wavefields.shape...]
    pad x1, local copies, waits for them, and re-layouts: 0.61 us -> 0.01 us  [body(): table = jnp.pad(table, ((0, 0), (0, LANES - bins)))]
  transfers between devices with their start and end apart: 13 -> 13, of which waited for: 6 -> 8; matrix products, arithmetic and copies ran while one was open for 2% -> 2% of each run, Pallas kernels for 8% -> 4%
where the time goes in v2:
time: 36.9 us; the launch traced here: 36.8 us
  waiting for transfers between devices  14.6 us (40%)
  starting transfers between devices  11.5 us (31%)
  Pallas kernels  7.56 us (20%)
  local copies, waits for them, and re-layouts  1.77 us (5%)
  between operations  1.38 us (4%)
    ppermute x4, waiting for transfers between devices, body(): zmate = lax.ppermute(own, axes, chain)  10.7 us
    ppermute x4, starting transfers between devices, body(): zmate = lax.ppermute(own, axes, chain)  6.17 us
    pallas_call x4, Pallas kernels, body(): pl.pallas_call(functools.partial(depth_step, depth, kcheb, bins, final),...  5.46 us
    ppermute x1, starting transfers between devices, body(): lax.ppermute(velocity, 'freq', [((i + s) % freq, i) for i in range(freq)])  2.55 us
    ppermute x1, waiting for transfers between devices, body(): lax.ppermute(here_send[s - 1], 'freq', [(i, (i + s) % freq) for i in rang...  2.13 us
    ppermute x1, starting transfers between devices, body(): lax.ppermute(here_send[s - 1], 'freq', [(i, (i + s) % freq) for i in rang...  1.55 us
    unnamed x8, local copies, waits for them, and re-layouts  1.19 us
    ppermute x1, waiting for transfers between devices, body(): pairs.append(lax.ppermute(cross_send[s - 1], ('freq', 'sub'), cross))  0.92 us
  transfers between devices with their start and end apart: 13, of which 8 were waited for; matrix products, arithmetic and copies ran while one was open for 2% of the time, Pallas kernels for 4%

profile of v2, /device:TPU:0, one launch (start us, length us, event | category | flops | bytes accessed | tf_op | source)
XLA Modules:
  0.0 36.8 jit_solution(10963131477397496403)
XLA Ops:
  0.6 0.0 copy-start
  0.6 0.6 %collective-permute-start.2 = (f32[1,4,16,512]{3,2,1,0:T(8,128)}, f32[1,4,16,512]{3,2,1,0:T(8,128)S(1)}, u32[]{:S(2)}, u32[]{:S(2)}) collective-permute-start(f32[1,4,16,512]{3,2,1,0:T(8,128)} %x_ref.1), channel_id=1, source_target_pairs={{0,1},{1,0},{2,3},{3,2},{4,5},{5,4},{6,7},{7,6},{8,9},{9,8},{10,11... | collective-permute-start | bytes 393224 | tf_op jit(solution)/shard_map/ppermute | solution.py:275
  1.2 2.6 %collective-permute-start = (f32[4,16,512]{2,1,0:T(8,128)}, f32[4,16,512]{2,1,0:T(8,128)S(1)}, u32[]{:S(2)}, u32[]{:S(2)}) collective-permute-start(f32[4,16,512]{2,1,0:T(8,128)} %refs_0_.1), channel_id=1, source_target_pairs={{2,0},{0,2},{3,1},{1,3},{6,4},{4,6},{7,5},{5,7},{10,8},{8,10},{11,... | collective-permute-start | bytes 393224 | tf_op jit(solution)/shard_map/ppermute | solution.py:274
  3.8 0.9 %copy-done.1 = f32[1,4,16,512]{3,2,1,0:T(8,128)S(1)} copy-done((f32[1,4,16,512]{3,2,1,0:T(8,128)S(1)}, f32[1,4,16,512]{3,2,1,0:T(8,128)}, u32[]{:S(2)}) %copy-start.1) | copy-done | bytes 131096
  4.7 0.8 %pack_fields.1 = (f32[32,8,128]{2,1,0:T(8,128)S(1)}, f32[32,8,128]{2,1,0:T(8,128)S(1)}) custom-call(f32[1,4,16,512]{3,2,1,0:T(8,128)S(1)} %copy-done.1, f32[1,4,16,512]{3,2,1,0:T(8,128)S(1)} %collective-permute-done.2.other_ref), custom_call_target="tpu_custom_call" | custom-call | tf_op jit(solution)/shard_map/pack_fields/pallas_call | solution.py:282
  5.5 1.5 %collective-permute-start.3 = (f32[32,8,128]{2,1,0:T(8,128)S(1)}, f32[32,8,128]{2,1,0:T(8,128)S(1)}, u32[]{:S(2)}, u32[]{:S(2)}) collective-permute-start(f32[32,8,128]{2,1,0:T(8,128)S(1)} %get-tuple-element.18.own_ref), channel_id=1, source_target_pairs={{1,4},{4,1},{5,8},{8,5},{9,12},{12,9},{0,2},{13,15},{3,6},{6,3},{7... | collective-permute-start | bytes 393224 | tf_op jit(solution)/shard_map/ppermute | solution.py:288
  7.7 0.0 copy-start.3
  7.7 0.4 %collective-permute-done.refs_1_ = f32[4,16,512]{2,1,0:T(8,128)S(1)} collective-permute-done((f32[4,16,512]{2,1,0:T(8,128)}, f32[4,16,512]{2,1,0:T(8,128)S(1)}, u32[]{:S(2)}, u32[]{:S(2)}) %collective-permute-start) | collective-permute-done | bytes 131104 | tf_op jit(solution)/shard_map/ppermute | solution.py:274
  8.1 0.3 copy-done.3
  8.3 0.6 %pack_velocity.1 = (f32[4,8,512]{2,1,0:T(8,128)S(1)}, f32[4,8,512]{2,1,0:T(8,128)S(1)}) custom-call(s32[4]{0:T(128)S(1)} %copy-done.3, f32[4,16,512]{2,1,0:T(8,128)S(1)} %copy-done.2, f32[4,16,512]{2,1,0:T(8,128)S(1)} %collective-permute-done.refs_1_), custom_call_target="tpu_custom_call" | custom-call | tf_op jit(solution)/shard_map/pack_velocity/pallas_call | solution.py:291
  8.9 0.3 collective-permute-start.1
  9.2 0.4 %constant_dynamic-slice_fusion = f32[32,1,9,2]{1,3,2,0:T(2,128)S(1)} fusion(f32[32,32,9,2]{1,3,2,0:T(2,128)S(1)} %copy-done, s32[]{:T(128)S(6)} %select_n.4), kind=kLoop, calls=%fused_computation | loop fusion | bytes 4612 | tf_op jit(solution)/shard_map/jit(dynamic_index_in_dim)/dynamic_slice | solution.py:277
  9.6 0.2 copy.7
  9.8 0.4 %collective-permute-done.1.other_ref = f32[4,8,512]{2,1,0:T(8,128)S(1)} collective-permute-done((f32[4,8,512]{2,1,0:T(8,128)S(1)}, f32[4,8,512]{2,1,0:T(8,128)S(1)}, u32[]{:S(2)}, u32[]{:S(2)}) %collective-permute-start.1) | collective-permute-done | bytes 65568 | tf_op jit(solution)/shard_map/ppermute | solution.py:299
  10.3 0.3 collective-permute-done.3.zmate_ref
  10.5 1.1 %depth_step.3 = (f32[32,8,128]{2,1,0:T(8,128)S(1)}, f32[8,8,128]{2,1,0:T(8,128)S(1)}) custom-call(f32[18,128]{1,0:T(8,128)S(1)} %pad.4.table_ref, f32[4,8,512]{2,1,0:T(8,128)S(1)} %get-tuple-element.16.keep_ref, f32[4,8,512]{2,1,0:T(8,128)S(1)} %collective-permute-done.1.other_ref, f32[32,8,128]{2,1,0:T(8,128)S(1)} %get-tuple-element.18.own_ref, ...), custom_call_target="tpu_custom_call" | custom-call | tf_op jit(solution)/shard_map/depth_step/pallas_call | solution.py:318
  11.7 1.5 %collective-permute-start.5 = (f32[32,8,128]{2,1,0:T(8,128)S(1)}, f32[32,8,128]{2,1,0:T(8,128)S(1)}, u32[]{:S(2)}, u32[]{:S(2)}) collective-permute-start(f32[32,8,128]{2,1,0:T(8,128)S(1)} %get-tuple-element.20.own_ref), channel_id=1, source_target_pairs={{1,4},{4,1},{5,8},{8,5},{9,12},{12,9},{0,2},{13,15},{3,6},{6,3},{7... | collective-permute-start | bytes 393224 | tf_op jit(solution)/shard_map/ppermute | solution.py:330
  13.2 3.5 %collective-permute-done.5.zmate_ref = f32[32,8,128]{2,1,0:T(8,128)S(1)} collective-permute-done((f32[32,8,128]{2,1,0:T(8,128)S(1)}, f32[32,8,128]{2,1,0:T(8,128)S(1)}, u32[]{:S(2)}, u32[]{:S(2)}) %collective-permute-start.5) | collective-permute-done | bytes 131104 | tf_op jit(solution)/shard_map/ppermute | solution.py:330
  16.7 0.0 collective-permute-done.4.mate_ref
  16.7 1.1 %depth_step.4 = (f32[32,8,128]{2,1,0:T(8,128)S(1)}, f32[8,8,128]{2,1,0:T(8,128)S(1)}) custom-call(f32[18,128]{1,0:T(8,128)S(1)} %pad.4.table_ref, f32[4,8,512]{2,1,0:T(8,128)S(1)} %get-tuple-element.16.keep_ref, f32[4,8,512]{2,1,0:T(8,128)S(1)} %collective-permute-done.1.other_ref, f32[32,8,128]{2,1,0:T(8,128)S(1)} %get-tuple-element.20.own_ref, ...), custom_call_target="tpu_custom_call" | custom-call | tf_op jit(solution)/shard_map/depth_step/pallas_call | solution.py:318
  17.8 1.5 %collective-permute-start.7 = (f32[32,8,128]{2,1,0:T(8,128)S(1)}, f32[32,8,128]{2,1,0:T(8,128)S(1)}, u32[]{:S(2)}, u32[]{:S(2)}) collective-permute-start(f32[32,8,128]{2,1,0:T(8,128)S(1)} %get-tuple-element.21.own_ref), channel_id=1, source_target_pairs={{1,4},{4,1},{5,8},{8,5},{9,12},{12,9},{0,2},{13,15},{3,6},{6,3},{7... | collective-permute-start | bytes 393224 | tf_op jit(solution)/shard_map/ppermute | solution.py:330
  19.4 3.5 %collective-permute-done.7.zmate_ref = f32[32,8,128]{2,1,0:T(8,128)S(1)} collective-permute-done((f32[32,8,128]{2,1,0:T(8,128)S(1)}, f32[32,8,128]{2,1,0:T(8,128)S(1)}, u32[]{:S(2)}, u32[]{:S(2)}) %collective-permute-start.7) | collective-permute-done | bytes 131104 | tf_op jit(solution)/shard_map/ppermute | solution.py:330
  22.9 1.1 %depth_step.5 = (f32[32,8,128]{2,1,0:T(8,128)S(1)}, f32[8,8,128]{2,1,0:T(8,128)S(1)}) custom-call(f32[18,128]{1,0:T(8,128)S(1)} %pad.4.table_ref, f32[4,8,512]{2,1,0:T(8,128)S(1)} %get-tuple-element.16.keep_ref, f32[4,8,512]{2,1,0:T(8,128)S(1)} %collective-permute-done.1.other_ref, f32[32,8,128]{2,1,0:T(8,128)S(1)} %get-tuple-element.21.own_ref, ...), custom_call_target="tpu_custom_call" | custom-call | tf_op jit(solution)/shard_map/depth_step/pallas_call | solution.py:318
  24.0 1.5 %collective-permute-start.9 = (f32[32,8,128]{2,1,0:T(8,128)S(1)}, f32[32,8,128]{2,1,0:T(8,128)S(1)}, u32[]{:S(2)}, u32[]{:S(2)}) collective-permute-start(f32[32,8,128]{2,1,0:T(8,128)S(1)} %get-tuple-element.22.own_ref), channel_id=1, source_target_pairs={{1,4},{4,1},{5,8},{8,5},{9,12},{12,9},{0,2},{13,15},{3,6},{6,3},{7... | collective-permute-start | bytes 393224 | tf_op jit(solution)/shard_map/ppermute | solution.py:330
  25.6 3.5 %collective-permute-done.9.zmate_ref = f32[32,8,128]{2,1,0:T(8,128)S(1)} collective-permute-done((f32[32,8,128]{2,1,0:T(8,128)S(1)}, f32[32,8,128]{2,1,0:T(8,128)S(1)}, u32[]{:S(2)}, u32[]{:S(2)}) %collective-permute-start.9) | collective-permute-done | bytes 131104 | tf_op jit(solution)/shard_map/ppermute | solution.py:330
  29.1 2.0 %last_step.1 = (f32[6,8,512]{2,1,0:T(8,128)S(1)}, f32[6,8,512]{2,1,0:T(8,128)S(1)}, f32[1,2,8,512]{3,2,1,0:T(8,128)S(1)}, f32[1,2,8,512]{3,2,1,0:T(8,128)S(1)}) custom-call(f32[18,128]{1,0:T(8,128)S(1)} %pad.4.table_ref, f32[4,8,512]{2,1,0:T(8,128)S(1)} %get-tuple-element.16.keep_ref, f32[4,8,512]{2,1,0:T(8,128)S(1)} %collective-permute-done.1.other_ref, ...), custom_call_target="tpu_custom_call" | custom-call | tf_op jit(solution)/shard_map/last_step/pallas_call | solution.py:318
  31.1 0.1 collective-permute-start.10
  31.2 1.5 %collective-permute-start.11 = (f32[2,8,512]{2,1,0:T(8,128)S(1)}, f32[2,8,512]{2,1,0:T(8,128)S(1)}, u32[]{:S(2)}, u32[]{:S(2)}) collective-permute-start(f32[2,8,512]{2,1,0:T(8,128)S(1)} %bitcast.10), channel_id=1, source_target_pairs={{0,2},{2,0},{1,3},{3,1},{4,6},{6,4},{5,7},{7,5},{8,10},{10,8},{9,1... | collective-permute-start | bytes 98312 | tf_op jit(solution)/shard_map/ppermute | solution.py:337
  32.7 0.3 collective-permute-start.12
  33.0 2.1 %collective-permute-done.11.refs_0_ = f32[2,8,512]{2,1,0:T(8,128)S(1)} collective-permute-done((f32[2,8,512]{2,1,0:T(8,128)S(1)}, f32[2,8,512]{2,1,0:T(8,128)S(1)}, u32[]{:S(2)}, u32[]{:S(2)}) %collective-permute-start.11) | collective-permute-done | bytes 32800 | tf_op jit(solution)/shard_map/ppermute | solution.py:337
  35.2 0.9 %collective-permute-done.12.refs_1_ = f32[2,8,512]{2,1,0:T(8,128)S(1)} collective-permute-done((f32[2,8,512]{2,1,0:T(8,128)S(1)}, f32[2,8,512]{2,1,0:T(8,128)S(1)}, u32[]{:S(2)}, u32[]{:S(2)}) %collective-permute-start.12) | collective-permute-done | bytes 32800 | tf_op jit(solution)/shard_map/ppermute | solution.py:339
  36.1 0.7 %assemble.1 = (f32[1,4,16,512]{3,2,1,0:T(8,128)}, f32[2,16,512]{2,1,0:T(8,128)}) custom-call(f32[6,8,512]{2,1,0:T(8,128)S(1)} %get-tuple-element.26.kept_ref, f32[6,8,512]{2,1,0:T(8,128)S(1)} %collective-permute-done.10.sub_ref, f32[2,8,512]{2,1,0:T(8,128)S(1)} %collective-permute-done.11.refs_0_, f32[2,8,512]{2,1,0:T(8,128)S(1)} %collective-permute-done.12.refs_1_), custom_call_target="tpu_custom_call" | custom-call | tf_op jit(solution)/shard_map/assemble/pallas_call | solution.py:340
  (13 shorter events, 0.1 us)
Async XLA Ops:
  0.6 8.6 %copy-start = (f32[32,32,9,2]{1,3,2,0:T(2,128)S(1)}, f32[32,32,9,2]{1,3,2,0:T(2,128)}, u32[]{:S(2)}) copy-start(f32[32,32,9,2]{1,3,2,0:T(2,128)} %param.7) | copy-start | bytes 221188
  0.6 3.1 %collective-permute-start.2 = (f32[1,4,16,512]{3,2,1,0:T(8,128)}, f32[1,4,16,512]{3,2,1,0:T(8,128)S(1)}, u32[]{:S(2)}, u32[]{:S(2)}) collective-permute-start(f32[1,4,16,512]{3,2,1,0:T(8,128)} %x_ref.1), channel_id=1, source_target_pairs={{0,1},{1,0},{2,3},{3,2},{4,5},{5,4},{6,7},{7,6},{8,9},{9,8},{10,11... | collective-permute-start | bytes 393224 | tf_op jit(solution)/shard_map/ppermute | solution.py:275
  1.2 6.9 %collective-permute-start = (f32[4,16,512]{2,1,0:T(8,128)}, f32[4,16,512]{2,1,0:T(8,128)S(1)}, u32[]{:S(2)}, u32[]{:S(2)}) collective-permute-start(f32[4,16,512]{2,1,0:T(8,128)} %refs_0_.1), channel_id=1, source_target_pairs={{2,0},{0,2},{3,1},{1,3},{6,4},{4,6},{7,5},{5,7},{10,8},{8,10},{11,... | collective-permute-start | bytes 393224 | tf_op jit(solution)/shard_map/ppermute | solution.py:274
  3.8 0.9 %copy-start.1 = (f32[1,4,16,512]{3,2,1,0:T(8,128)S(1)}, f32[1,4,16,512]{3,2,1,0:T(8,128)}, u32[]{:S(2)}) copy-start(f32[1,4,16,512]{3,2,1,0:T(8,128)} %x_ref.1) | copy-start | bytes 393220
  4.7 3.4 %copy-start.2 = (f32[4,16,512]{2,1,0:T(8,128)S(1)}, f32[4,16,512]{2,1,0:T(8,128)}, u32[]{:S(2)}) copy-start(f32[4,16,512]{2,1,0:T(8,128)} %refs_0_.1) | copy-start | bytes 393220
  5.5 5.0 %collective-permute-start.3 = (f32[32,8,128]{2,1,0:T(8,128)S(1)}, f32[32,8,128]{2,1,0:T(8,128)S(1)}, u32[]{:S(2)}, u32[]{:S(2)}) collective-permute-start(f32[32,8,128]{2,1,0:T(8,128)S(1)} %get-tuple-element.18.own_ref), channel_id=1, source_target_pairs={{1,4},{4,1},{5,8},{8,5},{9,12},{12,9},{0,2},{13,15},{3,6},{6,3},{7... | collective-permute-start | bytes 393224 | tf_op jit(solution)/shard_map/ppermute | solution.py:288
  7.7 0.7 %copy-start.3 = (s32[4]{0:T(128)S(1)}, s32[4]{0:T(128)}, u32[]{:S(2)}) copy-start(s32[4]{0:T(128)} %order_ref.1) | copy-start | bytes 52
  8.9 1.3 %collective-permute-start.1 = (f32[4,8,512]{2,1,0:T(8,128)S(1)}, f32[4,8,512]{2,1,0:T(8,128)S(1)}, u32[]{:S(2)}, u32[]{:S(2)}) collective-permute-start(f32[4,8,512]{2,1,0:T(8,128)S(1)} %get-tuple-element.17), channel_id=1, source_target_pairs={{0,1},{1,0},{2,3},{3,2},{4,5},{5,4},{6,7},{7,6},{8,9},{9,8},{10,11... | collective-permute-start | bytes 196616 | tf_op jit(solution)/shard_map/ppermute | solution.py:299
  11.7 5.0 %collective-permute-start.5 = (f32[32,8,128]{2,1,0:T(8,128)S(1)}, f32[32,8,128]{2,1,0:T(8,128)S(1)}, u32[]{:S(2)}, u32[]{:S(2)}) collective-permute-start(f32[32,8,128]{2,1,0:T(8,128)S(1)} %get-tuple-element.20.own_ref), channel_id=1, source_target_pairs={{1,4},{4,1},{5,8},{8,5},{9,12},{12,9},{0,2},{13,15},{3,6},{6,3},{7... | collective-permute-start | bytes 393224 | tf_op jit(solution)/shard_map/ppermute | solution.py:330
  13.2 3.5 %collective-permute-start.4 = (f32[32,8,128]{2,1,0:T(8,128)S(1)}, f32[32,8,128]{2,1,0:T(8,128)S(1)}, u32[]{:S(2)}, u32[]{:S(2)}) collective-permute-start(f32[32,8,128]{2,1,0:T(8,128)S(1)} %get-tuple-element.20.own_ref), channel_id=1, source_target_pairs={{0,1},{1,0},{2,3},{3,2},{4,5},{5,4},{6,7},{7,6},{8,9},{9,8},{10,11... | collective-permute-start | bytes 393224 | tf_op jit(solution)/shard_map/ppermute | solution.py:331
  17.8 5.0 %collective-permute-start.7 = (f32[32,8,128]{2,1,0:T(8,128)S(1)}, f32[32,8,128]{2,1,0:T(8,128)S(1)}, u32[]{:S(2)}, u32[]{:S(2)}) collective-permute-start(f32[32,8,128]{2,1,0:T(8,128)S(1)} %get-tuple-element.21.own_ref), channel_id=1, source_target_pairs={{1,4},{4,1},{5,8},{8,5},{9,12},{12,9},{0,2},{13,15},{3,6},{6,3},{7... | collective-permute-start | bytes 393224 | tf_op jit(solution)/shard_map/ppermute | solution.py:330
  19.4 3.5 %collective-permute-start.6 = (f32[32,8,128]{2,1,0:T(8,128)S(1)}, f32[32,8,128]{2,1,0:T(8,128)S(1)}, u32[]{:S(2)}, u32[]{:S(2)}) collective-permute-start(f32[32,8,128]{2,1,0:T(8,128)S(1)} %get-tuple-element.21.own_ref), channel_id=1, source_target_pairs={{0,1},{1,0},{2,3},{3,2},{4,5},{5,4},{6,7},{7,6},{8,9},{9,8},{10,11... | collective-permute-start | bytes 393224 | tf_op jit(solution)/shard_map/ppermute | solution.py:331
  24.0 5.0 %collective-permute-start.9 = (f32[32,8,128]{2,1,0:T(8,128)S(1)}, f32[32,8,128]{2,1,0:T(8,128)S(1)}, u32[]{:S(2)}, u32[]{:S(2)}) collective-permute-start(f32[32,8,128]{2,1,0:T(8,128)S(1)} %get-tuple-element.22.own_ref), channel_id=1, source_target_pairs={{1,4},{4,1},{5,8},{8,5},{9,12},{12,9},{0,2},{13,15},{3,6},{6,3},{7... | collective-permute-start | bytes 393224 | tf_op jit(solution)/shard_map/ppermute | solution.py:330
  25.6 3.5 %collective-permute-start.8 = (f32[32,8,128]{2,1,0:T(8,128)S(1)}, f32[32,8,128]{2,1,0:T(8,128)S(1)}, u32[]{:S(2)}, u32[]{:S(2)}) collective-permute-start(f32[32,8,128]{2,1,0:T(8,128)S(1)} %get-tuple-element.22.own_ref), channel_id=1, source_target_pairs={{0,1},{1,0},{2,3},{3,2},{4,5},{5,4},{6,7},{7,6},{8,9},{9,8},{10,11... | collective-permute-start | bytes 393224 | tf_op jit(solution)/shard_map/ppermute | solution.py:331
  31.1 5.0 %collective-permute-start.10 = (f32[6,8,512]{2,1,0:T(8,128)S(1)}, f32[6,8,512]{2,1,0:T(8,128)S(1)}, u32[]{:S(2)}, u32[]{:S(2)}) collective-permute-start(f32[6,8,512]{2,1,0:T(8,128)S(1)} %get-tuple-element.27), channel_id=1, source_target_pairs={{0,1},{1,0},{2,3},{3,2},{4,5},{5,4},{6,7},{7,6},{8,9},{9,8},{10,11... | collective-permute-start | bytes 294920 | tf_op jit(solution)/shard_map/ppermute | solution.py:334
  31.2 4.0 %collective-permute-start.11 = (f32[2,8,512]{2,1,0:T(8,128)S(1)}, f32[2,8,512]{2,1,0:T(8,128)S(1)}, u32[]{:S(2)}, u32[]{:S(2)}) collective-permute-start(f32[2,8,512]{2,1,0:T(8,128)S(1)} %bitcast.10), channel_id=1, source_target_pairs={{0,2},{2,0},{1,3},{3,1},{4,6},{6,4},{5,7},{7,5},{8,10},{10,8},{9,1... | collective-permute-start | bytes 98312 | tf_op jit(solution)/shard_map/ppermute | solution.py:337
  32.7 3.4 %collective-permute-start.12 = (f32[2,8,512]{2,1,0:T(8,128)S(1)}, f32[2,8,512]{2,1,0:T(8,128)S(1)}, u32[]{:S(2)}, u32[]{:S(2)}) collective-permute-start(f32[2,8,512]{2,1,0:T(8,128)S(1)} %bitcast.9), channel_id=1, source_target_pairs={{0,3},{1,2},{2,1},{3,0},{4,7},{5,6},{6,5},{7,4},{8,11},{9,10},{10,... | collective-permute-start | bytes 98312 | tf_op jit(solution)/shard_map/ppermute | solution.py:339

commit v3 on v1

v3 whole, which is shorter than its diff:
```python
import functools

import jax
import jax.numpy as jnp
from jax import lax
from jax.experimental import pallas as pl
from jax.experimental.pallas import tpu as pltpu
from jax.sharding import PartitionSpec as P


PARTS = 4
LANES = 128
ROWS = 8


def lane_ids():
    return lax.broadcasted_iota(jnp.int32, (ROWS, LANES), 1)


def pick(tile, index):
    return jnp.take_along_axis(tile, index, axis=1)


def straightened(tiles):
    count = len(tiles)
    lane = lane_ids()
    home = lane % count
    natural = []
    for t in range(count):
        index = (LANES // count) * t + lane // count
        out = pick(tiles[0], index)
        for j in range(1, count):
            out = jnp.where(home == j, pick(tiles[j], index), out)
        natural.append(out)
    return natural


def chain_permutation(lat, freq):
    def flat(z, f, c):
        return (z * freq + f) * 2 + c

    pairs = []
    for f in range(freq):
        for z in range(lat - 1):
            pairs.append((flat(z, f, 1), flat(z + 1, f, 0)))
            pairs.append((flat(z + 1, f, 0), flat(z, f, 1)))
        if freq % 2 == 0:
            pairs.append((flat(0, f, 0), flat(0, f ^ 1, 0)))
            pairs.append((flat(lat - 1, f, 1), flat(lat - 1, f ^ 1, 1)))
    return pairs


SWAP = [(0, 1), (1, 0)]
SMALL = pltpu.CompilerParams(vmem_limit_bytes=4 << 20)
STEP = pltpu.CompilerParams(vmem_limit_bytes=12 << 20)


def vmem(count):
    return [pl.BlockSpec(memory_space=pltpu.VMEM)] * count


def cost(flops):
    return pl.CostEstimate(flops=flops, bytes_accessed=1 << 16, transcendentals=0)


def spread_half(natural, core, out, tiles):
    lane = lane_ids()
    span = LANES // tiles
    home = lane // span - core * (tiles // 2)
    result = []
    for j in range(tiles):
        index = tiles * (lane % span) + j
        value = out[j]
        for t, tile in enumerate(natural):
            got = pick(tile, index)
            value = got if value is None else jnp.where(home == t, got, value)
        result.append(value)
    return result


def compacted(natural):
    half = len(natural)
    lane = lane_ids()
    within = lane % (LANES // 2)
    span = LANES // (2 * half)
    home = within // span
    tiles = []
    for i in range(half):
        index = 2 * half * (within % span) + i + half * (lane // (LANES // 2))
        value = pick(natural[0], index)
        for t in range(1, half):
            value = jnp.where(home == t, pick(natural[t], index), value)
        tiles.append(value)
    return tiles


def merged(left, right):
    middle = LANES // 2
    low = lane_ids() < middle
    first = [jnp.where(low, a, pltpu.roll(b, middle, 1)) for a, b in zip(left, right)]
    second = [jnp.where(low, pltpu.roll(a, middle, 1), b) for a, b in zip(left, right)]
    return first + second


def arrange_fields(x_ref, own_ref, mate_ref):
    half = x_ref.shape[3] // LANES
    for target, rows in zip((own_ref, mate_ref), both_rows()):
        for p in range(PARTS):
            natural = [x_ref[0, p, rows, t * LANES : (t + 1) * LANES] for t in range(half)]
            for i, tile in enumerate(compacted(natural)):
                target[p * half + i] = tile


def pack_velocity(order_ref, *refs):
    slabs, (keep_ref, send_ref) = refs[:-2], refs[-2:]
    core = lax.axis_index("sub")
    here = lax.axis_index("freq")
    count = len(slabs)
    size = slabs[0].shape[0]
    half = keep_ref.shape[2] // LANES
    for target, row in ((keep_ref, core), (send_ref, 1 - core)):
        rows = pl.ds(pl.multiple_of(row * ROWS, ROWS), ROWS)
        for t in range(half):
            columns = slice(t * LANES, (t + 1) * LANES)
            values = [[slabs[s][i, rows, columns] for i in range(size)] for s in range(count)]
            for d in range(keep_ref.shape[0]):
                stored = order_ref[d]
                value = values[0][0]
                for s in range(count):
                    first = lax.rem(here + s, count) * size
                    for i in range(size):
                        if s or i:
                            value = jnp.where(stored == first + i, values[s][i], value)
                target[d, :, columns] = value


def chebyshev(terms, tiles, kcheb, up_scale, down_scale):
    lane = lane_ids()
    sub = lax.broadcasted_iota(jnp.int32, (ROWS, LANES), 0)
    first = lane == 0
    last = lane == LANES - 1
    half = ROWS // 2
    inside = jnp.full((ROWS, LANES), 0.25, jnp.float32)
    upper = jnp.where(sub < half, up_scale, inside)
    lower = jnp.where(sub >= half, down_scale, inside)
    own = 2 * ROWS
    for k in range(kcheb):
        reach = kcheb - (k + 1)
        if reach > half:
            windows = ((own - ROWS, up_scale), (own, inside), (own + ROWS, down_scale))
        elif reach > 0:
            windows = ((own - half, upper), (own + half, lower))
        else:
            windows = ((own, inside),)
        for row, scale in windows:
            for p in range(PARTS):
                base = p * tiles
                twice = []
                sums = []
                for j in range(tiles):
                    value = terms[k, base + j, pl.ds(row, ROWS), :]
                    double = value + value
                    around = terms[k, base + j, pl.ds(row - 1, ROWS), :] + terms[k, base + j, pl.ds(row + 1, ROWS), :]
                    sums.append(around + double)
                    twice.append(value if k == 0 else double)
                before = jnp.where(first, 0.0, pltpu.roll(sums[tiles - 1], 1, 1))
                after = jnp.where(last, 0.0, pltpu.roll(sums[0], LANES - 1, 1))
                pair = [sums[j] + sums[j + 1] for j in range(tiles - 1)]
                full = [pair[0] + (sums[0] + before)]
                full += [pair[j - 1] + pair[j] for j in range(1, tiles - 1)]
                full.append(pair[tiles - 2] + (sums[tiles - 1] + after))
                for j in range(tiles):
                    if k == 0:
                        new = (0.5 * scale) * full[j] - twice[j]
                    else:
                        new = scale * full[j] - (twice[j] + terms[k - 1, base + j, pl.ds(row, ROWS), :])
                    terms[k + 1, base + j, pl.ds(row, ROWS), :] = new


def coefficients(depth, bins, table_ref, keep_ref, other_ref, *refs):
    out_ref = refs[-1]
    core = lax.axis_index("sub")
    count, tiles = out_ref.shape[:2]
    half = tiles // 2
    velocity = [None] * tiles
    for ref, home in ((keep_ref, core), (other_ref, 1 - core)):
        strips = [ref[depth, :, t * LANES : (t + 1) * LANES] for t in range(half)]
        velocity = spread_half(strips, home, velocity, tiles)
    lows = [jnp.clip(v.astype(jnp.int32), 0, bins - 1) for v in velocity]
    parts = [v - low.astype(jnp.float32) for v, low in zip(velocity, lows)]
    table = table_ref[...]
    step = pltpu.roll(table, LANES - 1, 1) - table
    for i in range(count):
        at_low = jnp.broadcast_to(table[i : i + 1], (ROWS, LANES))
        rise = jnp.broadcast_to(step[i : i + 1], (ROWS, LANES))
        for j in range(tiles):
            out_ref[i, j] = pick(at_low, lows[j]) + parts[j] * pick(rise, lows[j])


def combined(terms, coefficient, j, tiles, kcheb):
    own = 2 * ROWS
    total = None
    for k in range(kcheb + 1):
        a = coefficient[2 * k, j]
        b = coefficient[2 * k + 1, j]
        sr, si, rr, ri = [terms[k, p * tiles + j, pl.ds(own, ROWS), :] for p in range(PARTS)]
        adds = (a * sr + b * si, a * si - b * sr, a * rr - b * ri, a * ri + b * rr)
        total = adds if total is None else tuple(y + x for x, y in zip(adds, total))
    return total


def halves(stack, core):
    natural = straightened(stack)
    half = len(natural) // 2
    left, right = natural[:half], natural[half:]
    mine = [jnp.where(core == 0, a, b) for a, b in zip(left, right)]
    theirs = [jnp.where(core == 0, b, a) for a, b in zip(left, right)]
    return jnp.concatenate(mine, axis=1), jnp.concatenate(theirs, axis=1)


def whole_blocks(refs):
    core = lax.axis_index("sub")
    half = refs[0].shape[0] // PARTS
    blocks = []
    for ours, others in (refs[0:2], refs[2:4], refs[4:6]):
        tiles = []
        for p in range(PARTS):
            a = [ours[p * half + i] for i in range(half)]
            b = [others[p * half + i] for i in range(half)]
            left = [jnp.where(core == 0, x, y) for x, y in zip(a, b)]
            right = [jnp.where(core == 0, y, x) for x, y in zip(a, b)]
            tiles += merged(left, right)
        blocks.append(tiles)
    return blocks


def depth_step(kcheb, first, final, *refs):
    core = lax.axis_index("sub")
    block = lax.axis_index("lat") * 2 + core
    blocks = 2 * lax.axis_size("lat")
    terms = refs[-1]
    coefficient, refs = refs[0], refs[1:-1]
    tiles = coefficient.shape[1]
    own = 2 * ROWS
    up_ok = block > 0
    down_ok = block < blocks - 1
    if first:
        parts, refs = whole_blocks(refs[:6]), refs[6:]
    else:
        parts, refs = [[r[i] for i in range(PARTS * tiles)] for r in refs[:3]], refs[3:]
    for i in range(PARTS * tiles):
        mine, a, b = [part[i] for part in parts]
        terms[0, i, pl.ds(own, ROWS), :] = mine
        terms[0, i, pl.ds(own - ROWS, ROWS), :] = jnp.where(up_ok, jnp.where(core == 0, b, a), 0.0)
        terms[0, i, pl.ds(own + ROWS, ROWS), :] = jnp.where(down_ok, jnp.where(core == 0, a, b), 0.0)
    shape = (ROWS, LANES)
    up_scale = jnp.where(up_ok, jnp.full(shape, 0.25, jnp.float32), 0.0)
    down_scale = jnp.where(down_ok, jnp.full(shape, 0.25, jnp.float32), 0.0)
    chebyshev(terms, tiles, kcheb, up_scale, down_scale)
    result = [combined(terms, coefficient, j, tiles, kcheb) for j in range(tiles)]
    images = [sr * rr + si * ri for sr, si, rr, ri in result]
    if not final:
        new_ref, image_ref = refs
        for j in range(tiles):
            for p in range(PARTS):
                new_ref[p * tiles + j] = result[j][p]
            image_ref[j] = images[j]
        return
    fields_ref, here_ref, sub_ref, cross_ref = refs[1:]
    mine, theirs = halves(images, core)
    here_ref[0] = mine
    cross_ref[0] = theirs
    sub_ref[PARTS] = theirs
    for p in range(PARTS):
        fields_ref[p], sub_ref[p] = halves([total[p] for total in result], core)


def early_images(*refs):
    past, (kept_ref, sub_ref, here_ref, cross_ref) = refs[:-5], refs[-4:]
    core = lax.axis_index("sub")
    owners = lax.axis_size("freq")
    here = lax.axis_index("freq")
    each = kept_ref.shape[0]
    empty = jnp.zeros(kept_ref.shape[1:], jnp.float32)
    for depth in range(len(past) + 1):
        if depth < len(past):
            mine, theirs = halves([past[depth][j] for j in range(past[depth].shape[0])], core)
        else:
            mine = theirs = empty
        shift = lax.rem(depth // each - here + owners, owners)
        slot = depth % each

        @pl.when(shift == 0)
        def _():
            kept_ref[slot] = mine
            sub_ref[slot] = theirs

        @pl.when(shift != 0)
        def _():
            here_ref[shift - 1, slot] = mine
            cross_ref[shift - 1, slot] = theirs


def both_rows():
    core = lax.axis_index("sub")
    return [pl.ds(pl.multiple_of(c * ROWS, ROWS), ROWS) for c in (core, 1 - core)]


def assemble_fields(kept_ref, sub_ref, fields_ref):
    mine, theirs = both_rows()
    for p in range(PARTS):
        fields_ref[0, p, mine, :] = kept_ref[p]
        fields_ref[0, p, theirs, :] = sub_ref[p]


def assemble_images(count, *refs):
    early, late, image_ref = refs[: 2 * count], refs[2 * count : 4 * count], refs[-1]
    each = image_ref.shape[0]
    holds_last = lax.axis_index("freq") == lax.axis_size("freq") - 1
    for side, rows in enumerate(both_rows()):
        for d in range(each):
            value = functools.reduce(jnp.add, [r[d] for r in early[side::2]])
            if d == each - 1:
                last = functools.reduce(jnp.add, [r[r.shape[0] - 1] for r in late[side::2]])
                value = value + jnp.where(holds_last, last, 0.0)
            image_ref[d, rows, :] = value


def body(wavefields, velocity, filter_table, freq_pick, slab_order):
    f32 = jnp.float32
    lat = lax.axis_size("lat")
    freq = lax.axis_size("freq")
    bins, _, terms, _ = filter_table.shape
    kcheb = terms - 1
    _, parts, rows, cols = wavefields.shape
    depths = slab_order.shape[0]
    tiles = 2 * cols // LANES
    each = depths // freq
    assert rows == 2 * ROWS and kcheb == ROWS and parts == PARTS and lax.axis_size("sub") == 2

    def call(kernel, outs, args, params=SMALL, specs=None, scratch=(), flops=1 << 20):
        return pl.pallas_call(
            kernel,
            out_shape=tuple(jax.ShapeDtypeStruct(o, f32) for o in outs),
            in_specs=vmem(len(args)) if specs is None else specs,
            out_specs=tuple(vmem(len(outs))),
            scratch_shapes=scratch,
            compiler_params=params,
            cost_estimate=cost(flops),
        )(*args)

    def shifted(value, s):
        return lax.ppermute(value, "freq", [(i, (i + s) % freq) for i in range(freq)])

    def crossed(value, s):
        pairs = [(2 * i + c, 2 * ((i + s) % freq) + 1 - c) for i in range(freq) for c in range(2)]
        return lax.ppermute(value, ("freq", "sub"), pairs)

    slabs = [velocity]
    for s in range(1, freq):
        slabs.append(lax.ppermute(velocity, "freq", [((i + s) % freq, i) for i in range(freq)]))

    table = lax.dynamic_index_in_dim(filter_table, freq_pick[0], 1, keepdims=False)
    table = table.reshape(bins, 2 * terms).T
    table = jnp.pad(table, ((0, 0), (0, LANES - bins)))
    order = jnp.broadcast_to(slab_order[:, None, None], (depths, ROWS, LANES))

    chain = chain_permutation(lat, freq)
    axes = ("lat", "freq", "sub")
    compact = (PARTS * tiles // 2, ROWS, LANES)
    own, mate = call(arrange_fields, (compact, compact), (wavefields,))
    across = lax.ppermute(mate, "sub", SWAP)
    start = (own, across, mate, lax.ppermute(own, "sub", SWAP))
    start += (lax.ppermute(across, axes, chain), lax.ppermute(own, axes, chain))

    strip = (depths, ROWS, cols)
    keep, send = call(pack_velocity, (strip, strip), (order, *slabs))
    theirs = lax.ppermute(send, "sub", SWAP)

    def coefficients_of(depth, after):
        return call(
            functools.partial(coefficients, depth, bins),
            ((2 * terms, tiles, ROWS, LANES),),
            (table, keep, theirs) + after,
        )[0]

    scratch = [pltpu.VMEM((terms, PARTS * tiles, 5 * ROWS, LANES), f32)]
    coefficient = coefficients_of(0, ())
    block = (PARTS * tiles, ROWS, LANES)
    state = start
    images = []
    for depth in range(depths - 1):
        own, image = call(
            functools.partial(depth_step, kcheb, depth == 0, False),
            (block, (tiles, ROWS, LANES)),
            (coefficient, *state),
            params=STEP,
            scratch=scratch,
        )
        images.append(image)
        zmate = lax.ppermute(own, axes, chain)
        state = (own, lax.ppermute(own, "sub", SWAP), zmate)
        coefficient = coefficients_of(depth + 1, (own,))

    row = (each, ROWS, cols)
    outs = (row, row, (freq - 1,) + row, (freq - 1,) + row)
    kept, sub_send, here_send, cross_send = call(early_images, outs, (*images, coefficient))
    early = [kept, lax.ppermute(sub_send, "sub", SWAP)]
    for s in range(1, freq):
        early.append(shifted(here_send[s - 1], s))
        early.append(crossed(cross_send[s - 1], s))

    strip = (ROWS, cols)
    fields, here, sub_send, cross = call(
        functools.partial(depth_step, kcheb, depths == 1, True),
        ((PARTS,) + strip, (1,) + strip, (PARTS + 1,) + strip, (1,) + strip),
        (coefficient, *state, kept),
        params=STEP,
        scratch=scratch,
    )
    sub_got = lax.ppermute(sub_send, "sub", SWAP)
    late = [here, sub_got]
    for s in range(1, freq):
        late += [shifted(here, s), crossed(cross, s)]
    fields = call(assemble_fields, (wavefields.shape,), (fields, sub_got))[0]
    image = call(functools.partial(assemble_images, freq), ((each, rows, cols),), (*early, *late))[0]
    return fields, image


def solution(mesh):
    return jax.shard_map(
        body,
        mesh=mesh,
        in_specs=(
            P(("shots", "freq"), None, "lat", "sub"),
            P("freq", "lat", "sub"),
            P(),
            P("freq"),
            P(),
        ),
        out_specs=(P(("shots", "freq"), None, "lat", "sub"), P(("shots", "freq"), "lat", "sub")),
        check_vma=False,
    )
```

time: 52.6 us -> 38.5 us (0.73)
  Pallas kernels: 18.4 us -> 10.6 us
  local copies, waits for them, and re-layouts: 7.13 us -> 1.6 us
  waiting for transfers between devices: 14.3 us -> 11.5 us
  starting transfers between devices: 11.2 us -> 13.3 us
    pallas_call x7 -> x13, Pallas kernels: 18.4 us -> 10.6 us  [call(): pl.pallas_call(kernel, out_shape=tuple((jax.ShapeDtypeStruct(o, f32) for...]
    unnamed x28 -> x8, local copies, waits for them, and re-layouts: 5.95 us -> 0.95 us
    ppermute x6 -> x12, starting transfers between devices: 2.64 us -> 7.22 us  [the longest x2 2.09 us: shifted(): lax.ppermute(value, 'freq', [(i, (i + s) % freq) for i in range(freq)])]
    ppermute x4 -> x3, starting transfers between devices: 5.74 us -> 1.8 us  [body(): zmate = lax.ppermute(own, axes, chain)]
    ppermute x4 -> x3, waiting for transfers between devices: 11 us -> 9.1 us  [body(): zmate = lax.ppermute(own, axes, chain)]
    ppermute x6 -> x12, waiting for transfers between devices: 3.17 us -> 2.07 us  [the longest x2 0.87 us: shifted(): lax.ppermute(value, 'freq', [(i, (i + s) % freq) for i in range(freq)])]
    ppermute x1, starting transfers between devices: 0.21 us -> 1.2 us  [body(): theirs = lax.ppermute(send, 'sub', SWAP)]
    pad x1, local copies, waits for them, and re-layouts: 0.61 us -> 0.01 us  [body(): table = jnp.pad(table, ((0, 0), (0, LANES - bins)))]
  transfers between devices with their start and end apart: 13 -> 18, of which waited for: 6 -> 7; matrix products, arithmetic and copies ran while one was open for 2% -> 2% of each run, Pallas kernels for 8% -> 14%
where the time goes in v3:
time: 38.5 us; the launch traced here: 38.4 us
  starting transfers between devices  13.3 us (35%)
  waiting for transfers between devices  11.5 us (30%)
  Pallas kernels  10.6 us (28%)
  local copies, waits for them, and re-layouts  1.6 us (4%)
  between operations  1.43 us (4%)
    pallas_call x13, Pallas kernels, call(): pl.pallas_call(kernel, out_shape=tuple((jax.ShapeDtypeStruct(o, f32) for...  10.6 us
    ppermute x3, waiting for transfers between devices, body(): zmate = lax.ppermute(own, axes, chain)  9.1 us
    ppermute x1, starting transfers between devices, body(): lax.ppermute(velocity, 'freq', [((i + s) % freq, i) for i in range(freq)])  3.03 us
    ppermute x2, starting transfers between devices, shifted(): lax.ppermute(value, 'freq', [(i, (i + s) % freq) for i in range(freq)])  2.09 us
    ppermute x3, starting transfers between devices, body(): zmate = lax.ppermute(own, axes, chain)  1.8 us
    ppermute x2, starting transfers between devices, crossed(): return lax.ppermute(value, ('freq', 'sub'), pairs)  1.75 us
    ppermute x1, starting transfers between devices, body(): start = (own, across, mate, lax.ppermute(own, 'sub', SWAP))  1.68 us
    ppermute x1, starting transfers between devices, body(): theirs = lax.ppermute(send, 'sub', SWAP)  1.2 us
  transfers between devices with their start and end apart: 18, of which 7 were waited for; matrix products, arithmetic and copies ran while one was open for 2% of the time, Pallas kernels for 14%

profile of v3, /device:TPU:0, one launch (start us, length us, event | category | flops | bytes accessed | tf_op | source)
XLA Modules:
  0.0 38.4 jit_solution(11783785482935181761)
XLA Ops:
  0.6 3.0 %collective-permute-start = (f32[4,16,512]{2,1,0:T(8,128)}, f32[4,16,512]{2,1,0:T(8,128)S(1)}, u32[]{:S(2)}, u32[]{:S(2)}) collective-permute-start(f32[4,16,512]{2,1,0:T(8,128)} %refs_0_.1), channel_id=1, source_target_pairs={{2,0},{0,2},{3,1},{1,3},{6,4},{4,6},{7,5},{5,7},{10,8},{8,10},{11,... | collective-permute-start | bytes 393224 | tf_op jit(solution)/shard_map/ppermute | solution.py:361
  3.7 0.9 %copy-done.1 = f32[1,4,16,512]{3,2,1,0:T(8,128)S(1)} copy-done((f32[1,4,16,512]{3,2,1,0:T(8,128)S(1)}, f32[1,4,16,512]{3,2,1,0:T(8,128)}, u32[]{:S(2)}) %copy-start.1) | copy-done | bytes 131096
  4.6 0.3 shard_map.70
  5.1 1.7 %collective-permute-start.3 = (f32[16,8,128]{2,1,0:T(8,128)S(1)}, f32[16,8,128]{2,1,0:T(8,128)S(1)}, u32[]{:S(2)}, u32[]{:S(2)}) collective-permute-start(f32[16,8,128]{2,1,0:T(8,128)S(1)} %get-tuple-element.22.refs_1_), channel_id=1, source_target_pairs={{0,1},{1,0},{2,3},{3,2},{4,5},{5,4},{6,7},{7,6},{8,9},{9,8},{10,11... | collective-permute-start | bytes 196616 | tf_op jit(solution)/shard_map/ppermute | solution.py:373
  7.4 0.6 %collective-permute-start.4 = (f32[16,8,128]{2,1,0:T(8,128)S(1)}, f32[16,8,128]{2,1,0:T(8,128)S(1)}, u32[]{:S(2)}, u32[]{:S(2)}) collective-permute-start(f32[16,8,128]{2,1,0:T(8,128)S(1)} %collective-permute-done.2.refs_2_), channel_id=1, source_target_pairs={{1,4},{4,1},{5,8},{8,5},{9,12},{12,9},{0,2},{13,15},{3,6},{6,3},{7... | collective-permute-start | bytes 196616 | tf_op jit(solution)/shard_map/ppermute | solution.py:374
  8.2 1.2 %collective-permute-start.1 = (f32[4,8,512]{2,1,0:T(8,128)S(1)}, f32[4,8,512]{2,1,0:T(8,128)S(1)}, u32[]{:S(2)}, u32[]{:S(2)}) collective-permute-start(f32[4,8,512]{2,1,0:T(8,128)S(1)} %get-tuple-element.21), channel_id=1, source_target_pairs={{0,1},{1,0},{2,3},{3,2},{4,5},{5,4},{6,7},{7,6},{8,9},{9,8},{10,11... | collective-permute-start | bytes 196616 | tf_op jit(solution)/shard_map/ppermute | solution.py:378
  9.4 0.4 constant_dynamic-slice_fusion
  10.0 0.3 collective-permute-done.1.other_ref
  10.3 1.0 %shard_map.69.refs_0_ = f32[18,8,8,128]{3,2,1,0:T(8,128)S(1)} custom-call(f32[18,128]{1,0:T(8,128)S(1)} %pad.4.table_ref, f32[4,8,512]{2,1,0:T(8,128)S(1)} %get-tuple-element.20.keep_ref, f32[4,8,512]{2,1,0:T(8,128)S(1)} %collective-permute-done.1.other_ref), custom_call_target="tpu_custom_call" | custom-call | flops 1048576 | bytes 65536 | tf_op jit(solution)/shard_map/pallas_call | solution.py:342
  11.3 0.5 %collective-permute-done.4.refs_5_ = f32[16,8,128]{2,1,0:T(8,128)S(1)} collective-permute-done((f32[16,8,128]{2,1,0:T(8,128)S(1)}, f32[16,8,128]{2,1,0:T(8,128)S(1)}, u32[]{:S(2)}, u32[]{:S(2)}) %collective-permute-start.4) | collective-permute-done | bytes 65568 | tf_op jit(solution)/shard_map/ppermute | solution.py:374
  11.7 1.2 %shard_map.71 = (f32[32,8,128]{2,1,0:T(8,128)S(1)}, f32[8,8,128]{2,1,0:T(8,128)S(1)}) custom-call(f32[18,8,8,128]{3,2,1,0:T(8,128)S(1)} %shard_map.69.refs_0_, f32[16,8,128]{2,1,0:T(8,128)S(1)} %get-tuple-element.22.refs_1_, f32[16,8,128]{2,1,0:T(8,128)S(1)} %collective-permute-done.2.refs_2_, f32[16,8,128]{2,1,0:T(8,128)S(1)} %get-tuple-element.23.refs_3_, ...), custom_call_target="tpu_custom_call" | custom-call | flops 1048576 | bytes 65536 | tf_op jit(solution)/shard_map/pallas_call | solution.py:342
  12.9 0.6 %collective-permute-start.7 = (f32[32,8,128]{2,1,0:T(8,128)S(1)}, f32[32,8,128]{2,1,0:T(8,128)S(1)}, u32[]{:S(2)}, u32[]{:S(2)}) collective-permute-start(f32[32,8,128]{2,1,0:T(8,128)S(1)} %get-tuple-element.24.refs_0_.refs_1_), channel_id=1, source_target_pairs={{1,4},{4,1},{5,8},{8,5},{9,12},{12,9},{0,2},{13,15},{3,6},{6,3},{7... | collective-permute-start | bytes 393224 | tf_op jit(solution)/shard_map/ppermute | solution.py:401
  13.5 0.7 %collective-permute-start.6 = (f32[32,8,128]{2,1,0:T(8,128)S(1)}, f32[32,8,128]{2,1,0:T(8,128)S(1)}, u32[]{:S(2)}, u32[]{:S(2)}) collective-permute-start(f32[32,8,128]{2,1,0:T(8,128)S(1)} %get-tuple-element.24.refs_0_.refs_1_), channel_id=1, source_target_pairs={{0,1},{1,0},{2,3},{3,2},{4,5},{5,4},{6,7},{7,6},{8,9},{9,8},{10,11... | collective-permute-start | bytes 393224 | tf_op jit(solution)/shard_map/ppermute | solution.py:402
  14.2 1.0 %shard_map.72.refs_0_ = f32[18,8,8,128]{3,2,1,0:T(8,128)S(1)} custom-call(f32[18,128]{1,0:T(8,128)S(1)} %pad.4.table_ref, f32[4,8,512]{2,1,0:T(8,128)S(1)} %get-tuple-element.20.keep_ref, f32[4,8,512]{2,1,0:T(8,128)S(1)} %collective-permute-done.1.other_ref, f32[32,8,128]{2,1,0:T(8,128)S(1)} %get-tuple-element.24.refs_0_.refs_1_), custom_call_target="tpu_custom_call" | custom-call | flops 1048576 | bytes 65536 | tf_op jit(solution)/shard_map/pallas_call | solution.py:342
  15.2 2.8 %collective-permute-done.7.refs_3_ = f32[32,8,128]{2,1,0:T(8,128)S(1)} collective-permute-done((f32[32,8,128]{2,1,0:T(8,128)S(1)}, f32[32,8,128]{2,1,0:T(8,128)S(1)}, u32[]{:S(2)}, u32[]{:S(2)}) %collective-permute-start.7) | collective-permute-done | bytes 131104 | tf_op jit(solution)/shard_map/ppermute | solution.py:401
  18.0 0.9 %shard_map.73 = (f32[32,8,128]{2,1,0:T(8,128)S(1)}, f32[8,8,128]{2,1,0:T(8,128)S(1)}) custom-call(f32[18,8,8,128]{3,2,1,0:T(8,128)S(1)} %shard_map.72.refs_0_, f32[32,8,128]{2,1,0:T(8,128)S(1)} %get-tuple-element.24.refs_0_.refs_1_, f32[32,8,128]{2,1,0:T(8,128)S(1)} %collective-permute-done.6.refs_2_, f32[32,8,128]{2,1,0:T(8,128)S(1)} %collective-permute-done.7.refs_3_), custom_call_target="tpu_custom_call" | custom-call | flops 1048576 | bytes 65536 | tf_op jit(solution)/shard_map/pallas_call | solution.py:342
  18.9 0.6 %collective-permute-start.9 = (f32[32,8,128]{2,1,0:T(8,128)S(1)}, f32[32,8,128]{2,1,0:T(8,128)S(1)}, u32[]{:S(2)}, u32[]{:S(2)}) collective-permute-start(f32[32,8,128]{2,1,0:T(8,128)S(1)} %get-tuple-element.25.refs_0_.refs_1_), channel_id=1, source_target_pairs={{1,4},{4,1},{5,8},{8,5},{9,12},{12,9},{0,2},{13,15},{3,6},{6,3},{7... | collective-permute-start | bytes 393224 | tf_op jit(solution)/shard_map/ppermute | solution.py:401
  19.6 1.0 %shard_map.74.refs_0_ = f32[18,8,8,128]{3,2,1,0:T(8,128)S(1)} custom-call(f32[18,128]{1,0:T(8,128)S(1)} %pad.4.table_ref, f32[4,8,512]{2,1,0:T(8,128)S(1)} %get-tuple-element.20.keep_ref, f32[4,8,512]{2,1,0:T(8,128)S(1)} %collective-permute-done.1.other_ref, f32[32,8,128]{2,1,0:T(8,128)S(1)} %get-tuple-element.25.refs_0_.refs_1_), custom_call_target="tpu_custom_call" | custom-call | flops 1048576 | bytes 65536 | tf_op jit(solution)/shard_map/pallas_call | solution.py:342
  20.6 3.4 %collective-permute-done.9.refs_3_ = f32[32,8,128]{2,1,0:T(8,128)S(1)} collective-permute-done((f32[32,8,128]{2,1,0:T(8,128)S(1)}, f32[32,8,128]{2,1,0:T(8,128)S(1)}, u32[]{:S(2)}, u32[]{:S(2)}) %collective-permute-start.9) | collective-permute-done | bytes 131104 | tf_op jit(solution)/shard_map/ppermute | solution.py:401
  23.9 0.9 %shard_map.75 = (f32[32,8,128]{2,1,0:T(8,128)S(1)}, f32[8,8,128]{2,1,0:T(8,128)S(1)}) custom-call(f32[18,8,8,128]{3,2,1,0:T(8,128)S(1)} %shard_map.74.refs_0_, f32[32,8,128]{2,1,0:T(8,128)S(1)} %get-tuple-element.25.refs_0_.refs_1_, f32[32,8,128]{2,1,0:T(8,128)S(1)} %collective-permute-done.8.refs_2_, f32[32,8,128]{2,1,0:T(8,128)S(1)} %collective-permute-done.9.refs_3_), custom_call_target="tpu_custom_call" | custom-call | flops 1048576 | bytes 65536 | tf_op jit(solution)/shard_map/pallas_call | solution.py:342
  24.9 0.6 %collective-permute-start.11 = (f32[32,8,128]{2,1,0:T(8,128)S(1)}, f32[32,8,128]{2,1,0:T(8,128)S(1)}, u32[]{:S(2)}, u32[]{:S(2)}) collective-permute-start(f32[32,8,128]{2,1,0:T(8,128)S(1)} %get-tuple-element.26.refs_0_.refs_1_), channel_id=1, source_target_pairs={{1,4},{4,1},{5,8},{8,5},{9,12},{12,9},{0,2},{13,15},{3,6},{6,3},{7... | collective-permute-start | bytes 393224 | tf_op jit(solution)/shard_map/ppermute | solution.py:401
  25.5 1.0 %shard_map.76.refs_3_.refs_0_ = f32[18,8,8,128]{3,2,1,0:T(8,128)S(1)} custom-call(f32[18,128]{1,0:T(8,128)S(1)} %pad.4.table_ref, f32[4,8,512]{2,1,0:T(8,128)S(1)} %get-tuple-element.20.keep_ref, f32[4,8,512]{2,1,0:T(8,128)S(1)} %collective-permute-done.1.other_ref, f32[32,8,128]{2,1,0:T(8,128)S(1)} %get-tuple-element.26.refs_0_.refs_1_), custom_call_target="tpu_custom_call" | custom-call | flops 1048576 | bytes 65536 | tf_op jit(solution)/shard_map/pallas_call | solution.py:342
  26.4 0.5 %shard_map.77 = (f32[2,8,512]{2,1,0:T(8,128)S(1)}, f32[2,8,512]{2,1,0:T(8,128)S(1)}, f32[1,2,8,512]{3,2,1,0:T(8,128)S(1)}, f32[1,2,8,512]{3,2,1,0:T(8,128)S(1)}) custom-call(f32[8,8,128]{2,1,0:T(8,128)S(1)} %get-tuple-element.27.refs_0_, f32[8,8,128]{2,1,0:T(8,128)S(1)} %get-tuple-element.28.refs_1_, f32[8,8,128]{2,1,0:T(8,128)S(1)} %get-tuple-element.29.refs_2_, ...), custom_call_target="tpu_custom_call" | custom-call | flops 1048576 | bytes 65536 | tf_op jit(solution)/shard_map/pallas_call | solution.py:342
  27.0 3.0 %collective-permute-done.11.refs_3_ = f32[32,8,128]{2,1,0:T(8,128)S(1)} collective-permute-done((f32[32,8,128]{2,1,0:T(8,128)S(1)}, f32[32,8,128]{2,1,0:T(8,128)S(1)}, u32[]{:S(2)}, u32[]{:S(2)}) %collective-permute-start.11) | collective-permute-done | bytes 131104 | tf_op jit(solution)/shard_map/ppermute | solution.py:401
  29.9 1.5 %shard_map.78 = (f32[4,8,512]{2,1,0:T(8,128)S(1)}, f32[1,8,512]{2,1,0:T(8,128)S(1)}, f32[5,8,512]{2,1,0:T(8,128)S(1)}, f32[1,8,512]{2,1,0:T(8,128)S(1)}) custom-call(f32[18,8,8,128]{3,2,1,0:T(8,128)S(1)} %shard_map.76.refs_3_.refs_0_, f32[32,8,128]{2,1,0:T(8,128)S(1)} %get-tuple-element.26.refs_0_.refs_1_, ...), custom_call_target="tpu_custom_call" | custom-call | flops 1048576 | bytes 65536 | tf_op jit(solution)/shard_map/pallas_call | solution.py:342
  31.5 0.6 %collective-permute-start.14 = (f32[2,8,512]{2,1,0:T(8,128)S(1)}, f32[2,8,512]{2,1,0:T(8,128)S(1)}, u32[]{:S(2)}, u32[]{:S(2)}) collective-permute-start(f32[2,8,512]{2,1,0:T(8,128)S(1)} %bitcast.10), channel_id=1, source_target_pairs={{0,2},{2,0},{1,3},{3,1},{4,6},{6,4},{5,7},{7,5},{8,10},{10,8},{9,1... | collective-permute-start | bytes 98312 | tf_op jit(solution)/shard_map/ppermute | solution.py:353
  32.3 1.5 %collective-permute-start.15 = (f32[2,8,512]{2,1,0:T(8,128)S(1)}, f32[2,8,512]{2,1,0:T(8,128)S(1)}, u32[]{:S(2)}, u32[]{:S(2)}) collective-permute-start(f32[2,8,512]{2,1,0:T(8,128)S(1)} %bitcast.9), channel_id=1, source_target_pairs={{0,3},{1,2},{2,1},{3,0},{4,7},{5,6},{6,5},{7,4},{8,11},{9,10},{10,... | collective-permute-start | bytes 98312 | tf_op jit(solution)/shard_map/ppermute | solution.py:357
  34.0 1.5 %collective-permute-start.16 = (f32[1,8,512]{2,1,0:T(8,128)S(1)}, f32[1,8,512]{2,1,0:T(8,128)S(1)}, u32[]{:S(2)}, u32[]{:S(2)}) collective-permute-start(f32[1,8,512]{2,1,0:T(8,128)S(1)} %get-tuple-element.36.refs_4_), channel_id=1, source_target_pairs={{0,2},{2,0},{1,3},{3,1},{4,6},{6,4},{5,7},{7,5},{8,10},{10,8},{9,1... | collective-permute-start | bytes 49160 | tf_op jit(solution)/shard_map/ppermute | solution.py:353
  35.5 0.7 %shard_map.79 = f32[1,4,16,512]{3,2,1,0:T(8,128)} custom-call(f32[4,8,512]{2,1,0:T(8,128)S(1)} %get-tuple-element.31.kept_ref, f32[5,8,512]{2,1,0:T(8,128)S(1)} %collective-permute-done.12.sub_ref.refs_5_), custom_call_target="tpu_custom_call" | custom-call | flops 1048576 | bytes 65536 | tf_op jit(solution)/shard_map/pallas_call | solution.py:342
  36.2 0.7 %collective-permute-done.17.refs_7_ = f32[1,8,512]{2,1,0:T(8,128)S(1)} collective-permute-done((f32[1,8,512]{2,1,0:T(8,128)S(1)}, f32[1,8,512]{2,1,0:T(8,128)S(1)}, u32[]{:S(2)}, u32[]{:S(2)}) %collective-permute-start.17) | collective-permute-done | bytes 16416 | tf_op jit(solution)/shard_map/ppermute | solution.py:357
  36.9 0.9 %collective-permute-done.16.refs_6_ = f32[1,8,512]{2,1,0:T(8,128)S(1)} collective-permute-done((f32[1,8,512]{2,1,0:T(8,128)S(1)}, f32[1,8,512]{2,1,0:T(8,128)S(1)}, u32[]{:S(2)}, u32[]{:S(2)}) %collective-permute-start.16) | collective-permute-done | bytes 16416 | tf_op jit(solution)/shard_map/ppermute | solution.py:353
  37.7 0.6 %shard_map.80 = f32[2,16,512]{2,1,0:T(8,128)} custom-call(f32[2,8,512]{2,1,0:T(8,128)S(1)} %get-tuple-element.30.refs_4_.refs_0_, f32[2,8,512]{2,1,0:T(8,128)S(1)} %collective-permute-done.13.refs_1_, f32[2,8,512]{2,1,0:T(8,128)S(1)} %collective-permute-done.14.refs_2_, f32[2,8,512]{2,1,0:T(8,128)S(1)} %collective-permute-done.15.refs_3_, ...), custom_call_target="tpu_custom_call" | custom-call | flops 1048576 | bytes 65536 | tf_op jit(solution)/shard_map/pallas_call | solution.py:342
  (30 shorter events, 1.2 us)
Async XLA Ops:
  0.6 8.8 %copy-start = (f32[32,32,9,2]{1,3,2,0:T(2,128)S(1)}, f32[32,32,9,2]{1,3,2,0:T(2,128)}, u32[]{:S(2)}) copy-start(f32[32,32,9,2]{1,3,2,0:T(2,128)} %param.7) | copy-start | bytes 221188
  0.6 7.4 %collective-permute-start = (f32[4,16,512]{2,1,0:T(8,128)}, f32[4,16,512]{2,1,0:T(8,128)S(1)}, u32[]{:S(2)}, u32[]{:S(2)}) collective-permute-start(f32[4,16,512]{2,1,0:T(8,128)} %refs_0_.1), channel_id=1, source_target_pairs={{2,0},{0,2},{3,1},{1,3},{6,4},{4,6},{7,5},{5,7},{10,8},{8,10},{11,... | collective-permute-start | bytes 393224 | tf_op jit(solution)/shard_map/ppermute | solution.py:361
  3.7 0.9 %copy-start.1 = (f32[1,4,16,512]{3,2,1,0:T(8,128)S(1)}, f32[1,4,16,512]{3,2,1,0:T(8,128)}, u32[]{:S(2)}) copy-start(f32[1,4,16,512]{3,2,1,0:T(8,128)} %x_ref.1) | copy-start | bytes 393220
  4.6 3.5 %copy-start.2 = (f32[4,16,512]{2,1,0:T(8,128)S(1)}, f32[4,16,512]{2,1,0:T(8,128)}, u32[]{:S(2)}) copy-start(f32[4,16,512]{2,1,0:T(8,128)} %refs_0_.1) | copy-start | bytes 393220
  4.9 2.5 %collective-permute-start.2 = (f32[16,8,128]{2,1,0:T(8,128)S(1)}, f32[16,8,128]{2,1,0:T(8,128)S(1)}, u32[]{:S(2)}, u32[]{:S(2)}) collective-permute-start(f32[16,8,128]{2,1,0:T(8,128)S(1)} %get-tuple-element.23.refs_3_), channel_id=1, source_target_pairs={{0,1},{1,0},{2,3},{3,2},{4,5},{5,4},{6,7},{7,6},{8,9},{9,8},{10,11... | collective-permute-start | bytes 196616 | tf_op jit(solution)/shard_map/ppermute | solution.py:372
  5.0 6.3 %collective-permute-start.5 = (f32[16,8,128]{2,1,0:T(8,128)S(1)}, f32[16,8,128]{2,1,0:T(8,128)S(1)}, u32[]{:S(2)}, u32[]{:S(2)}) collective-permute-start(f32[16,8,128]{2,1,0:T(8,128)S(1)} %get-tuple-element.22.refs_1_), channel_id=1, source_target_pairs={{1,4},{4,1},{5,8},{8,5},{9,12},{12,9},{0,2},{13,15},{3,6},{6,3},{7... | collective-permute-start | bytes 196616 | tf_op jit(solution)/shard_map/ppermute | solution.py:374
  5.1 6.2 %collective-permute-start.3 = (f32[16,8,128]{2,1,0:T(8,128)S(1)}, f32[16,8,128]{2,1,0:T(8,128)S(1)}, u32[]{:S(2)}, u32[]{:S(2)}) collective-permute-start(f32[16,8,128]{2,1,0:T(8,128)S(1)} %get-tuple-element.22.refs_1_), channel_id=1, source_target_pairs={{0,1},{1,0},{2,3},{3,2},{4,5},{5,4},{6,7},{7,6},{8,9},{9,8},{10,11... | collective-permute-start | bytes 196616 | tf_op jit(solution)/shard_map/ppermute | solution.py:373
  7.4 0.7 %copy-start.3 = (s32[4]{0:T(128)S(1)}, s32[4]{0:T(128)}, u32[]{:S(2)}) copy-start(s32[4]{0:T(128)} %param.9) | copy-start | bytes 52
  7.4 4.3 %collective-permute-start.4 = (f32[16,8,128]{2,1,0:T(8,128)S(1)}, f32[16,8,128]{2,1,0:T(8,128)S(1)}, u32[]{:S(2)}, u32[]{:S(2)}) collective-permute-start(f32[16,8,128]{2,1,0:T(8,128)S(1)} %collective-permute-done.2.refs_2_), channel_id=1, source_target_pairs={{1,4},{4,1},{5,8},{8,5},{9,12},{12,9},{0,2},{13,15},{3,6},{6,3},{7... | collective-permute-start | bytes 196616 | tf_op jit(solution)/shard_map/ppermute | solution.py:374
  8.2 2.1 %collective-permute-start.1 = (f32[4,8,512]{2,1,0:T(8,128)S(1)}, f32[4,8,512]{2,1,0:T(8,128)S(1)}, u32[]{:S(2)}, u32[]{:S(2)}) collective-permute-start(f32[4,8,512]{2,1,0:T(8,128)S(1)} %get-tuple-element.21), channel_id=1, source_target_pairs={{0,1},{1,0},{2,3},{3,2},{4,5},{5,4},{6,7},{7,6},{8,9},{9,8},{10,11... | collective-permute-start | bytes 196616 | tf_op jit(solution)/shard_map/ppermute | solution.py:378
  12.9 5.0 %collective-permute-start.7 = (f32[32,8,128]{2,1,0:T(8,128)S(1)}, f32[32,8,128]{2,1,0:T(8,128)S(1)}, u32[]{:S(2)}, u32[]{:S(2)}) collective-permute-start(f32[32,8,128]{2,1,0:T(8,128)S(1)} %get-tuple-element.24.refs_0_.refs_1_), channel_id=1, source_target_pairs={{1,4},{4,1},{5,8},{8,5},{9,12},{12,9},{0,2},{13,15},{3,6},{6,3},{7... | collective-permute-start | bytes 393224 | tf_op jit(solution)/shard_map/ppermute | solution.py:401
  13.5 4.4 %collective-permute-start.6 = (f32[32,8,128]{2,1,0:T(8,128)S(1)}, f32[32,8,128]{2,1,0:T(8,128)S(1)}, u32[]{:S(2)}, u32[]{:S(2)}) collective-permute-start(f32[32,8,128]{2,1,0:T(8,128)S(1)} %get-tuple-element.24.refs_0_.refs_1_), channel_id=1, source_target_pairs={{0,1},{1,0},{2,3},{3,2},{4,5},{5,4},{6,7},{7,6},{8,9},{9,8},{10,11... | collective-permute-start | bytes 393224 | tf_op jit(solution)/shard_map/ppermute | solution.py:402
  18.9 5.0 %collective-permute-start.9 = (f32[32,8,128]{2,1,0:T(8,128)S(1)}, f32[32,8,128]{2,1,0:T(8,128)S(1)}, u32[]{:S(2)}, u32[]{:S(2)}) collective-permute-start(f32[32,8,128]{2,1,0:T(8,128)S(1)} %get-tuple-element.25.refs_0_.refs_1_), channel_id=1, source_target_pairs={{1,4},{4,1},{5,8},{8,5},{9,12},{12,9},{0,2},{13,15},{3,6},{6,3},{7... | collective-permute-start | bytes 393224 | tf_op jit(solution)/shard_map/ppermute | solution.py:401
  19.5 4.4 %collective-permute-start.8 = (f32[32,8,128]{2,1,0:T(8,128)S(1)}, f32[32,8,128]{2,1,0:T(8,128)S(1)}, u32[]{:S(2)}, u32[]{:S(2)}) collective-permute-start(f32[32,8,128]{2,1,0:T(8,128)S(1)} %get-tuple-element.25.refs_0_.refs_1_), channel_id=1, source_target_pairs={{0,1},{1,0},{2,3},{3,2},{4,5},{5,4},{6,7},{7,6},{8,9},{9,8},{10,11... | collective-permute-start | bytes 393224 | tf_op jit(solution)/shard_map/ppermute | solution.py:402
  24.9 5.0 %collective-permute-start.11 = (f32[32,8,128]{2,1,0:T(8,128)S(1)}, f32[32,8,128]{2,1,0:T(8,128)S(1)}, u32[]{:S(2)}, u32[]{:S(2)}) collective-permute-start(f32[32,8,128]{2,1,0:T(8,128)S(1)} %get-tuple-element.26.refs_0_.refs_1_), channel_id=1, source_target_pairs={{1,4},{4,1},{5,8},{8,5},{9,12},{12,9},{0,2},{13,15},{3,6},{6,3},{7... | collective-permute-start | bytes 393224 | tf_op jit(solution)/shard_map/ppermute | solution.py:401
  25.5 4.4 %collective-permute-start.10 = (f32[32,8,128]{2,1,0:T(8,128)S(1)}, f32[32,8,128]{2,1,0:T(8,128)S(1)}, u32[]{:S(2)}, u32[]{:S(2)}) collective-permute-start(f32[32,8,128]{2,1,0:T(8,128)S(1)} %get-tuple-element.26.refs_0_.refs_1_), channel_id=1, source_target_pairs={{0,1},{1,0},{2,3},{3,2},{4,5},{5,4},{6,7},{7,6},{8,9},{9,8},{10,11... | collective-permute-start | bytes 393224 | tf_op jit(solution)/shard_map/ppermute | solution.py:402
  31.4 2.6 %collective-permute-start.12 = (f32[5,8,512]{2,1,0:T(8,128)S(1)}, f32[5,8,512]{2,1,0:T(8,128)S(1)}, u32[]{:S(2)}, u32[]{:S(2)}) collective-permute-start(f32[5,8,512]{2,1,0:T(8,128)S(1)} %get-tuple-element.32), channel_id=1, source_target_pairs={{0,1},{1,0},{2,3},{3,2},{4,5},{5,4},{6,7},{7,6},{8,9},{9,8},{10,11... | collective-permute-start | bytes 245768 | tf_op jit(solution)/shard_map/ppermute | solution.py:421
  31.5 4.7 %collective-permute-start.14 = (f32[2,8,512]{2,1,0:T(8,128)S(1)}, f32[2,8,512]{2,1,0:T(8,128)S(1)}, u32[]{:S(2)}, u32[]{:S(2)}) collective-permute-start(f32[2,8,512]{2,1,0:T(8,128)S(1)} %bitcast.10), channel_id=1, source_target_pairs={{0,2},{2,0},{1,3},{3,1},{4,6},{6,4},{5,7},{7,5},{8,10},{10,8},{9,1... | collective-permute-start | bytes 98312 | tf_op jit(solution)/shard_map/ppermute | solution.py:353
  32.1 4.1 %collective-permute-start.13 = (f32[2,8,512]{2,1,0:T(8,128)S(1)}, f32[2,8,512]{2,1,0:T(8,128)S(1)}, u32[]{:S(2)}, u32[]{:S(2)}) collective-permute-start(f32[2,8,512]{2,1,0:T(8,128)S(1)} %get-tuple-element.33), channel_id=1, source_target_pairs={{0,1},{1,0},{2,3},{3,2},{4,5},{5,4},{6,7},{7,6},{8,9},{9,8},{10,11... | collective-permute-start | bytes 98312 | tf_op jit(solution)/shard_map/ppermute | solution.py:408
  32.3 3.9 %collective-permute-start.15 = (f32[2,8,512]{2,1,0:T(8,128)S(1)}, f32[2,8,512]{2,1,0:T(8,128)S(1)}, u32[]{:S(2)}, u32[]{:S(2)}) collective-permute-start(f32[2,8,512]{2,1,0:T(8,128)S(1)} %bitcast.9), channel_id=1, source_target_pairs={{0,3},{1,2},{2,1},{3,0},{4,7},{5,6},{6,5},{7,4},{8,11},{9,10},{10,... | collective-permute-start | bytes 98312 | tf_op jit(solution)/shard_map/ppermute | solution.py:357
  33.7 3.2 %collective-permute-start.17 = (f32[1,8,512]{2,1,0:T(8,128)S(1)}, f32[1,8,512]{2,1,0:T(8,128)S(1)}, u32[]{:S(2)}, u32[]{:S(2)}) collective-permute-start(f32[1,8,512]{2,1,0:T(8,128)S(1)} %get-tuple-element.37), channel_id=1, source_target_pairs={{0,3},{1,2},{2,1},{3,0},{4,7},{5,6},{6,5},{7,4},{8,11},{9,10},{10,... | collective-permute-start | bytes 49160 | tf_op jit(solution)/shard_map/ppermute | solution.py:357
  34.0 3.7 %collective-permute-start.16 = (f32[1,8,512]{2,1,0:T(8,128)S(1)}, f32[1,8,512]{2,1,0:T(8,128)S(1)}, u32[]{:S(2)}, u32[]{:S(2)}) collective-permute-start(f32[1,8,512]{2,1,0:T(8,128)S(1)} %get-tuple-element.36.refs_4_), channel_id=1, source_target_pairs={{0,2},{2,0},{1,3},{3,1},{4,6},{6,4},{5,7},{7,5},{8,10},{10,8},{9,1... | collective-permute-start | bytes 49160 | tf_op jit(solution)/shard_map/ppermute | solution.py:353

commit v4 on v3

--- a/solution.py
+++ b/solution.py
@@ -35,18 +35,19 @@
     return natural
 
 
-def chain_permutation(lat, freq):
-    def flat(z, f, c):
-        return (z * freq + f) * 2 + c
+def chain_permutation(shots, lat, freq):
+    def flat(s, z, f, c):
+        return ((s * lat + z) * freq + f) * 2 + c
 
     pairs = []
-    for f in range(freq):
-        for z in range(lat - 1):
-            pairs.append((flat(z, f, 1), flat(z + 1, f, 0)))
-            pairs.append((flat(z + 1, f, 0), flat(z, f, 1)))
-        if freq % 2 == 0:
-            pairs.append((flat(0, f, 0), flat(0, f ^ 1, 0)))
-            pairs.append((flat(lat - 1, f, 1), flat(lat - 1, f ^ 1, 1)))
+    for s in range(shots):
+        for f in range(freq):
+            for z in range(lat - 1):
+                pairs.append((flat(s, z, f, 1), flat(s, z + 1, f, 0)))
+                pairs.append((flat(s, z + 1, f, 0), flat(s, z, f, 1)))
+            if shots % 2 == 0:
+                pairs.append((flat(s, 0, f, 0), flat(s ^ 1, 0, f, 0)))
+                pairs.append((flat(s, lat - 1, f, 1), flat(s ^ 1, lat - 1, f, 1)))
     return pairs
 
 
@@ -177,17 +178,21 @@
                     terms[k + 1, base + j, pl.ds(row, ROWS), :] = new
 
 
-def coefficients(depth, bins, table_ref, keep_ref, other_ref, *refs):
-    out_ref = refs[-1]
-    core = lax.axis_index("sub")
-    count, tiles = out_ref.shape[:2]
+def bins_of(depth, bins, keep_ref, other_ref, tiles):
+    core = lax.axis_index("sub")
     half = tiles // 2
     velocity = [None] * tiles
     for ref, home in ((keep_ref, core), (other_ref, 1 - core)):
         strips = [ref[depth, :, t * LANES : (t + 1) * LANES] for t in range(half)]
         velocity = spread_half(strips, home, velocity, tiles)
     lows = [jnp.clip(v.astype(jnp.int32), 0, bins - 1) for v in velocity]
-    parts = [v - low.astype(jnp.float32) for v, low in zip(velocity, lows)]
+    return lows, [v - low.astype(jnp.float32) for v, low in zip(velocity, lows)]
+
+
+def coefficients(depth, bins, table_ref, keep_ref, other_ref, *refs):
+    out_ref = refs[-1]
+    count, tiles = out_ref.shape[:2]
+    lows, parts = bins_of(depth, bins, keep_ref, other_ref, tiles)
     table = table_ref[...]
     step = pltpu.roll(table, LANES - 1, 1) - table
     for i in range(count):
@@ -201,8 +206,8 @@
     own = 2 * ROWS
     total = None
     for k in range(kcheb + 1):
-        a = coefficient[2 * k, j]
-        b = coefficient[2 * k + 1, j]
+        a = coefficient(2 * k, j)
+        b = coefficient(2 * k + 1, j)
         sr, si, rr, ri = [terms[k, p * tiles + j, pl.ds(own, ROWS), :] for p in range(PARTS)]
         adds = (a * sr + b * si, a * si - b * sr, a * rr - b * ri, a * ri + b * rr)
         total = adds if total is None else tuple(y + x for x, y in zip(adds, total))
@@ -234,13 +239,29 @@
     return blocks
 
 
-def depth_step(kcheb, first, final, *refs):
+def depth_step(kcheb, bins, first, final, *refs):
     core = lax.axis_index("sub")
     block = lax.axis_index("lat") * 2 + core
     blocks = 2 * lax.axis_size("lat")
-    terms = refs[-1]
-    coefficient, refs = refs[0], refs[1:-1]
-    tiles = coefficient.shape[1]
+    refs, terms, lookup = refs[:-2], refs[-2], refs[-1]
+    tiles = terms.shape[1] // PARTS
+    if first:
+        (table_ref, keep_ref, other_ref), refs = refs[:3], refs[3:]
+        table = table_ref[...]
+        step = pltpu.roll(table, LANES - 1, 1) - table
+        for i in range(2 * (kcheb + 1)):
+            lookup[0, i] = jnp.broadcast_to(table[i : i + 1], (ROWS, LANES))
+            lookup[1, i] = jnp.broadcast_to(step[i : i + 1], (ROWS, LANES))
+        lows, between = bins_of(0, bins, keep_ref, other_ref, tiles)
+
+        def coefficient(i, j):
+            return pick(lookup[0, i], lows[j]) + between[j] * pick(lookup[1, i], lows[j])
+    else:
+        ready, refs = refs[0], refs[1:]
+
+        def coefficient(i, j):
+            return ready[i, j]
+
     own = 2 * ROWS
     up_ok = block > 0
     down_ok = block < blocks - 1
@@ -365,8 +386,8 @@
     table = jnp.pad(table, ((0, 0), (0, LANES - bins)))
     order = jnp.broadcast_to(slab_order[:, None, None], (depths, ROWS, LANES))
 
-    chain = chain_permutation(lat, freq)
-    axes = ("lat", "freq", "sub")
+    chain = chain_permutation(lax.axis_size("shots"), lat, freq)
+    axes = ("shots", "lat", "freq", "sub")
     compact = (PARTS * tiles // 2, ROWS, LANES)
     own, mate = call(arrange_fields, (compact, compact), (wavefields,))
     across = lax.ppermute(mate, "sub", SWAP)
@@ -384,27 +405,34 @@
             (table, keep, theirs) + after,
         )[0]
 
-    scratch = [pltpu.VMEM((terms, PARTS * tiles, 5 * ROWS, LANES), f32)]
-    coefficient = coefficients_of(0, ())
+    scratch = [
+        pltpu.VMEM((terms, PARTS * tiles, 5 * ROWS, LANES), f32),
+        pltpu.VMEM((2, 2 * terms, ROWS, LANES), f32),
+    ]
+    ready = [(table, keep, theirs)] + [None] * (depths - 1)
     block = (PARTS * tiles, ROWS, LANES)
     state = start
     images = []
     for depth in range(depths - 1):
         own, image = call(
-            functools.partial(depth_step, kcheb, depth == 0, False),
+            functools.partial(depth_step, kcheb, bins, depth == 0, False),
             (block, (tiles, ROWS, LANES)),
-            (coefficient, *state),
+            (*ready[depth], *state),
             params=STEP,
             scratch=scratch,
         )
         images.append(image)
         zmate = lax.ppermute(own, axes, chain)
         state = (own, lax.ppermute(own, "sub", SWAP), zmate)
-        coefficient = coefficients_of(depth + 1, (own,))
+        wanted = [depth + 1] if depth + 1 < depths - 1 else []
+        if depth == max(depths - 3, 0):
+            wanted.append(depths - 1)
+        for d in wanted:
+            ready[d] = (coefficients_of(d, (own,)),)
 
     row = (each, ROWS, cols)
     outs = (row, row, (freq - 1,) + row, (freq - 1,) + row)
-    kept, sub_send, here_send, cross_send = call(early_images, outs, (*images, coefficient))
+    kept, sub_send, here_send, cross_send = call(early_images, outs, (*images, *ready[-1]))
     early = [kept, lax.ppermute(sub_send, "sub", SWAP)]
     for s in range(1, freq):
         early.append(shifted(here_send[s - 1], s))
@@ -412,16 +440,17 @@
 
     strip = (ROWS, cols)
     fields, here, sub_send, cross = call(
-        functools.partial(depth_step, kcheb, depths == 1, True),
+        functools.partial(depth_step, kcheb, bins, depths == 1, True),
         ((PARTS,) + strip, (1,) + strip, (PARTS + 1,) + strip, (1,) + strip),
-        (coefficient, *state, kept),
+        (*ready[-1], *state, kept),
         params=STEP,
         scratch=scratch,
     )
     sub_got = lax.ppermute(sub_send, "sub", SWAP)
     late = [here, sub_got]
     for s in range(1, freq):
-        late += [shifted(here, s), crossed(cross, s)]
+        late.append(shifted(here, s))
+        late.append(crossed(cross, s))
     fields = call(assemble_fields, (wavefields.shape,), (fields, sub_got))[0]
     image = call(functools.partial(assemble_images, freq), ((each, rows, cols),), (*early, *late))[0]
     return fields, image

time: 38.5 us -> 38.8 us (level)
  Pallas kernels: 10.6 us -> 9.66 us
  waiting for transfers between devices: 11.5 us -> 12.4 us
    ppermute x2, waiting for transfers between devices: 0.48 us -> 2.71 us  [body(): start += (lax.ppermute(across, axes, chain), lax.ppermute(own, axes, chain))]
    ppermute x2, starting transfers between devices: 0.68 us -> 2.09 us  [body(): start += (lax.ppermute(across, axes, chain), lax.ppermute(own, axes, chain))]
    ppermute x3, starting transfers between devices: 1.8 us -> 3.11 us  [body(): zmate = lax.ppermute(own, axes, chain)]
    ppermute x1, starting transfers between devices: 1.68 us -> 0.5 us  [body(): start = (own, across, mate, lax.ppermute(own, 'sub', SWAP))]
    ppermute x2, starting transfers between devices: 2.09 us -> 1.1 us  [shifted(): lax.ppermute(value, 'freq', [(i, (i + s) % freq) for i in range(freq)])]
    ppermute x1, starting transfers between devices: 1.2 us -> 0.24 us  [body(): theirs = lax.ppermute(send, 'sub', SWAP)]
    pallas_call x13 -> x12, Pallas kernels: 10.6 us -> 9.66 us  [call(): pl.pallas_call(kernel, out_shape=tuple((jax.ShapeDtypeStruct(o, f32) for...]
    ppermute x2, waiting for transfers between devices: 0.7 us -> 0.01 us  [crossed(): return lax.ppermute(value, ('freq', 'sub'), pairs)]
  transfers between devices with their start and end apart: 18 -> 18, of which waited for: 7 -> 7; matrix products, arithmetic and copies ran while one was open for 2% -> 2% of each run, Pallas kernels for 14% -> 11%
where the time goes in v4:
time: 38.8 us; the launch traced here: 38.6 us
  starting transfers between devices  13.5 us (35%)
  waiting for transfers between devices  12.4 us (32%)
  Pallas kernels  9.66 us (25%)
  local copies, waits for them, and re-layouts  1.62 us (4%)
  between operations  1.44 us (4%)
    pallas_call x12, Pallas kernels, call(): pl.pallas_call(kernel, out_shape=tuple((jax.ShapeDtypeStruct(o, f32) for...  9.66 us
    ppermute x3, waiting for transfers between devices, body(): zmate = lax.ppermute(own, axes, chain)  8.44 us
    ppermute x3, starting transfers between devices, body(): zmate = lax.ppermute(own, axes, chain)  3.11 us
    ppermute x1, starting transfers between devices, body(): lax.ppermute(velocity, 'freq', [((i + s) % freq, i) for i in range(freq)])  3.03 us
    ppermute x2, waiting for transfers between devices, body(): start += (lax.ppermute(across, axes, chain), lax.ppermute(own, axes, chain))  2.71 us
    ppermute x2, starting transfers between devices, crossed(): return lax.ppermute(value, ('freq', 'sub'), pairs)  2.39 us
    ppermute x2, starting transfers between devices, body(): start += (lax.ppermute(across, axes, chain), lax.ppermute(own, axes, chain))  2.09 us
    ppermute x2, waiting for transfers between devices, shifted(): lax.ppermute(value, 'freq', [(i, (i + s) % freq) for i in range(freq)])  1.2 us
  transfers between devices with their start and end apart: 18, of which 7 were waited for; matrix products, arithmetic and copies ran while one was open for 2% of the time, Pallas kernels for 11%

profile of v4, /device:TPU:0, one launch (start us, length us, event | category | flops | bytes accessed | tf_op | source)
XLA Modules:
  0.0 38.6 jit_solution(8368034254399587215)
XLA Ops:
  0.6 3.0 %collective-permute-start = (f32[4,16,512]{2,1,0:T(8,128)}, f32[4,16,512]{2,1,0:T(8,128)S(1)}, u32[]{:S(2)}, u32[]{:S(2)}) collective-permute-start(f32[4,16,512]{2,1,0:T(8,128)} %refs_0_.1), channel_id=1, source_target_pairs={{2,0},{0,2},{3,1},{1,3},{6,4},{4,6},{7,5},{5,7},{10,8},{8,10},{11,... | collective-permute-start | bytes 393224 | tf_op jit(solution)/shard_map/ppermute | solution.py:382
  3.7 0.9 %copy-done.1 = f32[1,4,16,512]{3,2,1,0:T(8,128)S(1)} copy-done((f32[1,4,16,512]{3,2,1,0:T(8,128)S(1)}, f32[1,4,16,512]{3,2,1,0:T(8,128)}, u32[]{:S(2)}) %copy-start.1) | copy-done | bytes 131096
  4.6 0.3 shard_map.69
  5.0 0.5 %collective-permute-start.3 = (f32[16,8,128]{2,1,0:T(8,128)S(1)}, f32[16,8,128]{2,1,0:T(8,128)S(1)}, u32[]{:S(2)}, u32[]{:S(2)}) collective-permute-start(f32[16,8,128]{2,1,0:T(8,128)S(1)} %get-tuple-element.22.refs_3_), channel_id=1, source_target_pairs={{0,1},{1,0},{2,3},{3,2},{4,5},{5,4},{6,7},{7,6},{8,9},{9,8},{10,11... | collective-permute-start | bytes 196616 | tf_op jit(solution)/shard_map/ppermute | solution.py:394
  5.5 1.5 %collective-permute-start.5 = (f32[16,8,128]{2,1,0:T(8,128)S(1)}, f32[16,8,128]{2,1,0:T(8,128)S(1)}, u32[]{:S(2)}, u32[]{:S(2)}) collective-permute-start(f32[16,8,128]{2,1,0:T(8,128)S(1)} %get-tuple-element.22.refs_3_), channel_id=1, source_target_pairs={{1,4},{4,1},{5,8},{8,5},{9,12},{12,9},{0,16},{13,29},{3,6},{6,3},{... | collective-permute-start | bytes 196616 | tf_op jit(solution)/shard_map/ppermute | solution.py:395
  7.7 0.6 %collective-permute-start.4 = (f32[16,8,128]{2,1,0:T(8,128)S(1)}, f32[16,8,128]{2,1,0:T(8,128)S(1)}, u32[]{:S(2)}, u32[]{:S(2)}) collective-permute-start(f32[16,8,128]{2,1,0:T(8,128)S(1)} %collective-permute-done.2.refs_4_), channel_id=1, source_target_pairs={{1,4},{4,1},{5,8},{8,5},{9,12},{12,9},{0,16},{13,29},{3,6},{6,3},{... | collective-permute-start | bytes 196616 | tf_op jit(solution)/shard_map/ppermute | solution.py:395
  8.4 0.2 collective-permute-start.1
  8.7 0.4 constant_dynamic-slice_fusion
  9.3 0.4 %collective-permute-done.5.refs_8_ = f32[16,8,128]{2,1,0:T(8,128)S(1)} collective-permute-done((f32[16,8,128]{2,1,0:T(8,128)S(1)}, f32[16,8,128]{2,1,0:T(8,128)S(1)}, u32[]{:S(2)}, u32[]{:S(2)}) %collective-permute-start.5) | collective-permute-done | bytes 65568 | tf_op jit(solution)/shard_map/ppermute | solution.py:395
  9.7 2.3 %collective-permute-done.4.refs_7_ = f32[16,8,128]{2,1,0:T(8,128)S(1)} collective-permute-done((f32[16,8,128]{2,1,0:T(8,128)S(1)}, f32[16,8,128]{2,1,0:T(8,128)S(1)}, u32[]{:S(2)}, u32[]{:S(2)}) %collective-permute-start.4) | collective-permute-done | bytes 65568 | tf_op jit(solution)/shard_map/ppermute | solution.py:395
  12.0 1.2 %shard_map.70 = (f32[32,8,128]{2,1,0:T(8,128)S(1)}, f32[8,8,128]{2,1,0:T(8,128)S(1)}) custom-call(f32[18,128]{1,0:T(8,128)S(1)} %pad.4.refs_0_.table_ref, f32[4,8,512]{2,1,0:T(8,128)S(1)} %get-tuple-element.20.refs_1_.keep_ref, f32[4,8,512]{2,1,0:T(8,128)S(1)} %collective-permute-done.1.refs_2_.other_ref, f32[16,8,128]{2,1,0:T(8,128)S(1)} %get-tuple-element.22.refs_3_, ...), custom_call_target="tpu_custom_call" | custom-call | flops 1048576 | bytes 65536 | tf_op jit(solution)/shard_map/pallas_call | solution.py:363
  13.3 1.1 %collective-permute-start.7 = (f32[32,8,128]{2,1,0:T(8,128)S(1)}, f32[32,8,128]{2,1,0:T(8,128)S(1)}, u32[]{:S(2)}, u32[]{:S(2)}) collective-permute-start(f32[32,8,128]{2,1,0:T(8,128)S(1)} %get-tuple-element.24.refs_0_.refs_1_), channel_id=1, source_target_pairs={{1,4},{4,1},{5,8},{8,5},{9,12},{12,9},{0,16},{13,29},{3,6},{6,3},{... | collective-permute-start | bytes 393224 | tf_op jit(solution)/shard_map/ppermute | solution.py:425
  14.4 1.0 %shard_map.71.refs_0_ = f32[18,8,8,128]{3,2,1,0:T(8,128)S(1)} custom-call(f32[18,128]{1,0:T(8,128)S(1)} %pad.4.refs_0_.table_ref, f32[4,8,512]{2,1,0:T(8,128)S(1)} %get-tuple-element.20.refs_1_.keep_ref, f32[4,8,512]{2,1,0:T(8,128)S(1)} %collective-permute-done.1.refs_2_.other_ref, f32[32,8,128]{2,1,0:T(8,128)S(1)} %get-tuple-element.24.refs_0_.refs_1_), custom_call_target="tpu_custom_call" | custom-call | flops 1048576 | bytes 65536 | tf_op jit(solution)/shard_map/pallas_call | solution.py:363
  15.4 3.0 %collective-permute-done.7.refs_3_ = f32[32,8,128]{2,1,0:T(8,128)S(1)} collective-permute-done((f32[32,8,128]{2,1,0:T(8,128)S(1)}, f32[32,8,128]{2,1,0:T(8,128)S(1)}, u32[]{:S(2)}, u32[]{:S(2)}) %collective-permute-start.7) | collective-permute-done | bytes 131104 | tf_op jit(solution)/shard_map/ppermute | solution.py:425
  18.4 0.9 %shard_map.72 = (f32[32,8,128]{2,1,0:T(8,128)S(1)}, f32[8,8,128]{2,1,0:T(8,128)S(1)}) custom-call(f32[18,8,8,128]{3,2,1,0:T(8,128)S(1)} %shard_map.71.refs_0_, f32[32,8,128]{2,1,0:T(8,128)S(1)} %get-tuple-element.24.refs_0_.refs_1_, f32[32,8,128]{2,1,0:T(8,128)S(1)} %collective-permute-done.6.refs_2_, f32[32,8,128]{2,1,0:T(8,128)S(1)} %collective-permute-done.7.refs_3_), custom_call_target="tpu_custom_call" | custom-call | flops 1048576 | bytes 65536 | tf_op jit(solution)/shard_map/pallas_call | solution.py:363
  19.5 1.0 %collective-permute-start.9 = (f32[32,8,128]{2,1,0:T(8,128)S(1)}, f32[32,8,128]{2,1,0:T(8,128)S(1)}, u32[]{:S(2)}, u32[]{:S(2)}) collective-permute-start(f32[32,8,128]{2,1,0:T(8,128)S(1)} %get-tuple-element.25.refs_0_.refs_1_), channel_id=1, source_target_pairs={{1,4},{4,1},{5,8},{8,5},{9,12},{12,9},{0,16},{13,29},{3,6},{6,3},{... | collective-permute-start | bytes 393224 | tf_op jit(solution)/shard_map/ppermute | solution.py:425
  20.5 1.0 %shard_map.74.refs_0_ = f32[18,8,8,128]{3,2,1,0:T(8,128)S(1)} custom-call(f32[18,128]{1,0:T(8,128)S(1)} %pad.4.refs_0_.table_ref, f32[4,8,512]{2,1,0:T(8,128)S(1)} %get-tuple-element.20.refs_1_.keep_ref, f32[4,8,512]{2,1,0:T(8,128)S(1)} %collective-permute-done.1.refs_2_.other_ref, f32[32,8,128]{2,1,0:T(8,128)S(1)} %get-tuple-element.25.refs_0_.refs_1_), custom_call_target="tpu_custom_call" | custom-call | flops 1048576 | bytes 65536 | tf_op jit(solution)/shard_map/pallas_call | solution.py:363
  21.5 3.0 %collective-permute-done.9.refs_3_ = f32[32,8,128]{2,1,0:T(8,128)S(1)} collective-permute-done((f32[32,8,128]{2,1,0:T(8,128)S(1)}, f32[32,8,128]{2,1,0:T(8,128)S(1)}, u32[]{:S(2)}, u32[]{:S(2)}) %collective-permute-start.9) | collective-permute-done | bytes 131104 | tf_op jit(solution)/shard_map/ppermute | solution.py:425
  24.5 0.9 %shard_map.75 = (f32[32,8,128]{2,1,0:T(8,128)S(1)}, f32[8,8,128]{2,1,0:T(8,128)S(1)}) custom-call(f32[18,8,8,128]{3,2,1,0:T(8,128)S(1)} %shard_map.74.refs_0_, f32[32,8,128]{2,1,0:T(8,128)S(1)} %get-tuple-element.25.refs_0_.refs_1_, f32[32,8,128]{2,1,0:T(8,128)S(1)} %collective-permute-done.8.refs_2_, f32[32,8,128]{2,1,0:T(8,128)S(1)} %collective-permute-done.9.refs_3_), custom_call_target="tpu_custom_call" | custom-call | flops 1048576 | bytes 65536 | tf_op jit(solution)/shard_map/pallas_call | solution.py:363
  25.6 1.0 %collective-permute-start.11 = (f32[32,8,128]{2,1,0:T(8,128)S(1)}, f32[32,8,128]{2,1,0:T(8,128)S(1)}, u32[]{:S(2)}, u32[]{:S(2)}) collective-permute-start(f32[32,8,128]{2,1,0:T(8,128)S(1)} %get-tuple-element.26.refs_1_), channel_id=1, source_target_pairs={{1,4},{4,1},{5,8},{8,5},{9,12},{12,9},{0,16},{13,29},{3,6},{6,3},{... | collective-permute-start | bytes 393224 | tf_op jit(solution)/shard_map/ppermute | solution.py:425
  26.6 1.0 %shard_map.73.refs_3_.refs_0_ = f32[18,8,8,128]{3,2,1,0:T(8,128)S(1)} custom-call(f32[18,128]{1,0:T(8,128)S(1)} %pad.4.refs_0_.table_ref, f32[4,8,512]{2,1,0:T(8,128)S(1)} %get-tuple-element.20.refs_1_.keep_ref, f32[4,8,512]{2,1,0:T(8,128)S(1)} %collective-permute-done.1.refs_2_.other_ref, f32[32,8,128]{2,1,0:T(8,128)S(1)} %get-tuple-element.25.refs_0_.refs_1_), custom_call_target="tpu_custom_call" | custom-call | flops 1048576 | bytes 65536 | tf_op jit(solution)/shard_map/pallas_call | solution.py:363
  27.5 0.5 %shard_map.76 = (f32[2,8,512]{2,1,0:T(8,128)S(1)}, f32[2,8,512]{2,1,0:T(8,128)S(1)}, f32[1,2,8,512]{3,2,1,0:T(8,128)S(1)}, f32[1,2,8,512]{3,2,1,0:T(8,128)S(1)}) custom-call(f32[8,8,128]{2,1,0:T(8,128)S(1)} %get-tuple-element.27.refs_0_, f32[8,8,128]{2,1,0:T(8,128)S(1)} %get-tuple-element.28.refs_1_, f32[8,8,128]{2,1,0:T(8,128)S(1)} %get-tuple-element.29.refs_2_, ...), custom_call_target="tpu_custom_call" | custom-call | flops 1048576 | bytes 65536 | tf_op jit(solution)/shard_map/pallas_call | solution.py:363
  28.1 2.5 %collective-permute-done.11.refs_3_ = f32[32,8,128]{2,1,0:T(8,128)S(1)} collective-permute-done((f32[32,8,128]{2,1,0:T(8,128)S(1)}, f32[32,8,128]{2,1,0:T(8,128)S(1)}, u32[]{:S(2)}, u32[]{:S(2)}) %collective-permute-start.11) | collective-permute-done | bytes 131104 | tf_op jit(solution)/shard_map/ppermute | solution.py:425
  30.5 1.5 %shard_map.77 = (f32[4,8,512]{2,1,0:T(8,128)S(1)}, f32[1,8,512]{2,1,0:T(8,128)S(1)}, f32[5,8,512]{2,1,0:T(8,128)S(1)}, f32[1,8,512]{2,1,0:T(8,128)S(1)}) custom-call(f32[18,8,8,128]{3,2,1,0:T(8,128)S(1)} %shard_map.73.refs_3_.refs_0_, f32[32,8,128]{2,1,0:T(8,128)S(1)} %get-tuple-element.26.refs_1_, f32[32,8,128]{2,1,0:T(8,128)S(1)} %collective-permute-done.10.refs_2_, ...), custom_call_target="tpu_custom_call" | custom-call | flops 1048576 | bytes 65536 | tf_op jit(solution)/shard_map/pallas_call | solution.py:363
  32.2 0.4 %collective-permute-start.13 = (f32[2,8,512]{2,1,0:T(8,128)S(1)}, f32[2,8,512]{2,1,0:T(8,128)S(1)}, u32[]{:S(2)}, u32[]{:S(2)}) collective-permute-start(f32[2,8,512]{2,1,0:T(8,128)S(1)} %get-tuple-element.33), channel_id=1, source_target_pairs={{0,1},{1,0},{2,3},{3,2},{4,5},{5,4},{6,7},{7,6},{8,9},{9,8},{10,11... | collective-permute-start | bytes 98312 | tf_op jit(solution)/shard_map/ppermute | solution.py:436
  32.6 0.5 %collective-permute-start.14 = (f32[2,8,512]{2,1,0:T(8,128)S(1)}, f32[2,8,512]{2,1,0:T(8,128)S(1)}, u32[]{:S(2)}, u32[]{:S(2)}) collective-permute-start(f32[2,8,512]{2,1,0:T(8,128)S(1)} %bitcast.10), channel_id=1, source_target_pairs={{0,2},{2,0},{1,3},{3,1},{4,6},{6,4},{5,7},{7,5},{8,10},{10,8},{9,1... | collective-permute-start | bytes 98312 | tf_op jit(solution)/shard_map/ppermute | solution.py:374
  33.2 0.9 %collective-permute-start.15 = (f32[2,8,512]{2,1,0:T(8,128)S(1)}, f32[2,8,512]{2,1,0:T(8,128)S(1)}, u32[]{:S(2)}, u32[]{:S(2)}) collective-permute-start(f32[2,8,512]{2,1,0:T(8,128)S(1)} %bitcast.9), channel_id=1, source_target_pairs={{0,3},{1,2},{2,1},{3,0},{4,7},{5,6},{6,5},{7,4},{8,11},{9,10},{10,... | collective-permute-start | bytes 98312 | tf_op jit(solution)/shard_map/ppermute | solution.py:378
  34.1 0.6 %collective-permute-start.16 = (f32[1,8,512]{2,1,0:T(8,128)S(1)}, f32[1,8,512]{2,1,0:T(8,128)S(1)}, u32[]{:S(2)}, u32[]{:S(2)}) collective-permute-start(f32[1,8,512]{2,1,0:T(8,128)S(1)} %get-tuple-element.36.refs_4_), channel_id=1, source_target_pairs={{0,2},{2,0},{1,3},{3,1},{4,6},{6,4},{5,7},{7,5},{8,10},{10,8},{9,1... | collective-permute-start | bytes 49160 | tf_op jit(solution)/shard_map/ppermute | solution.py:374
  34.7 1.5 %collective-permute-start.17 = (f32[1,8,512]{2,1,0:T(8,128)S(1)}, f32[1,8,512]{2,1,0:T(8,128)S(1)}, u32[]{:S(2)}, u32[]{:S(2)}) collective-permute-start(f32[1,8,512]{2,1,0:T(8,128)S(1)} %get-tuple-element.37), channel_id=1, source_target_pairs={{0,3},{1,2},{2,1},{3,0},{4,7},{5,6},{6,5},{7,4},{8,11},{9,10},{10,... | collective-permute-start | bytes 49160 | tf_op jit(solution)/shard_map/ppermute | solution.py:378
  36.1 0.7 %shard_map.78 = f32[1,4,16,512]{3,2,1,0:T(8,128)} custom-call(f32[4,8,512]{2,1,0:T(8,128)S(1)} %get-tuple-element.31.kept_ref, f32[5,8,512]{2,1,0:T(8,128)S(1)} %collective-permute-done.12.sub_ref.refs_5_), custom_call_target="tpu_custom_call" | custom-call | flops 1048576 | bytes 65536 | tf_op jit(solution)/shard_map/pallas_call | solution.py:363
  36.9 1.1 %collective-permute-done.16.refs_6_ = f32[1,8,512]{2,1,0:T(8,128)S(1)} collective-permute-done((f32[1,8,512]{2,1,0:T(8,128)S(1)}, f32[1,8,512]{2,1,0:T(8,128)S(1)}, u32[]{:S(2)}, u32[]{:S(2)}) %collective-permute-start.16) | collective-permute-done | bytes 16416 | tf_op jit(solution)/shard_map/ppermute | solution.py:374
  38.0 0.6 %shard_map.79 = f32[2,16,512]{2,1,0:T(8,128)} custom-call(f32[2,8,512]{2,1,0:T(8,128)S(1)} %get-tuple-element.30.refs_4_.refs_0_, f32[2,8,512]{2,1,0:T(8,128)S(1)} %collective-permute-done.13.refs_1_, f32[2,8,512]{2,1,0:T(8,128)S(1)} %collective-permute-done.14.refs_2_, f32[2,8,512]{2,1,0:T(8,128)S(1)} %collective-permute-done.15.refs_3_, ...), custom_call_target="tpu_custom_call" | custom-call | flops 1048576 | bytes 65536 | tf_op jit(solution)/shard_map/pallas_call | solution.py:363
  (29 shorter events, 1.2 us)
Async XLA Ops:
  0.6 8.1 %copy-start = (f32[32,32,9,2]{1,3,2,0:T(2,128)S(1)}, f32[32,32,9,2]{1,3,2,0:T(2,128)}, u32[]{:S(2)}) copy-start(f32[32,32,9,2]{1,3,2,0:T(2,128)} %param.7) | copy-start | bytes 221188
  0.6 7.6 %collective-permute-start = (f32[4,16,512]{2,1,0:T(8,128)}, f32[4,16,512]{2,1,0:T(8,128)S(1)}, u32[]{:S(2)}, u32[]{:S(2)}) collective-permute-start(f32[4,16,512]{2,1,0:T(8,128)} %refs_0_.1), channel_id=1, source_target_pairs={{2,0},{0,2},{3,1},{1,3},{6,4},{4,6},{7,5},{5,7},{10,8},{8,10},{11,... | collective-permute-start | bytes 393224 | tf_op jit(solution)/shard_map/ppermute | solution.py:382
  3.7 0.9 %copy-start.1 = (f32[1,4,16,512]{3,2,1,0:T(8,128)S(1)}, f32[1,4,16,512]{3,2,1,0:T(8,128)}, u32[]{:S(2)}) copy-start(f32[1,4,16,512]{3,2,1,0:T(8,128)} %x_ref.1) | copy-start | bytes 393220
  4.6 3.8 %copy-start.2 = (f32[4,16,512]{2,1,0:T(8,128)S(1)}, f32[4,16,512]{2,1,0:T(8,128)}, u32[]{:S(2)}) copy-start(f32[4,16,512]{2,1,0:T(8,128)} %refs_0_.1) | copy-start | bytes 393220
  4.9 2.8 %collective-permute-start.2 = (f32[16,8,128]{2,1,0:T(8,128)S(1)}, f32[16,8,128]{2,1,0:T(8,128)S(1)}, u32[]{:S(2)}, u32[]{:S(2)}) collective-permute-start(f32[16,8,128]{2,1,0:T(8,128)S(1)} %get-tuple-element.23.refs_5_), channel_id=1, source_target_pairs={{0,1},{1,0},{2,3},{3,2},{4,5},{5,4},{6,7},{7,6},{8,9},{9,8},{10,11... | collective-permute-start | bytes 196616 | tf_op jit(solution)/shard_map/ppermute | solution.py:393
  5.0 4.3 %collective-permute-start.3 = (f32[16,8,128]{2,1,0:T(8,128)S(1)}, f32[16,8,128]{2,1,0:T(8,128)S(1)}, u32[]{:S(2)}, u32[]{:S(2)}) collective-permute-start(f32[16,8,128]{2,1,0:T(8,128)S(1)} %get-tuple-element.22.refs_3_), channel_id=1, source_target_pairs={{0,1},{1,0},{2,3},{3,2},{4,5},{5,4},{6,7},{7,6},{8,9},{9,8},{10,11... | collective-permute-start | bytes 196616 | tf_op jit(solution)/shard_map/ppermute | solution.py:394
  5.5 4.3 %collective-permute-start.5 = (f32[16,8,128]{2,1,0:T(8,128)S(1)}, f32[16,8,128]{2,1,0:T(8,128)S(1)}, u32[]{:S(2)}, u32[]{:S(2)}) collective-permute-start(f32[16,8,128]{2,1,0:T(8,128)S(1)} %get-tuple-element.22.refs_3_), channel_id=1, source_target_pairs={{1,4},{4,1},{5,8},{8,5},{9,12},{12,9},{0,16},{13,29},{3,6},{6,3},{... | collective-permute-start | bytes 196616 | tf_op jit(solution)/shard_map/ppermute | solution.py:395
  7.6 0.7 %copy-start.3 = (s32[4]{0:T(128)S(1)}, s32[4]{0:T(128)}, u32[]{:S(2)}) copy-start(s32[4]{0:T(128)} %param.9) | copy-start | bytes 52
  7.7 4.3 %collective-permute-start.4 = (f32[16,8,128]{2,1,0:T(8,128)S(1)}, f32[16,8,128]{2,1,0:T(8,128)S(1)}, u32[]{:S(2)}, u32[]{:S(2)}) collective-permute-start(f32[16,8,128]{2,1,0:T(8,128)S(1)} %collective-permute-done.2.refs_4_), channel_id=1, source_target_pairs={{1,4},{4,1},{5,8},{8,5},{9,12},{12,9},{0,16},{13,29},{3,6},{6,3},{... | collective-permute-start | bytes 196616 | tf_op jit(solution)/shard_map/ppermute | solution.py:395
  8.4 3.6 %collective-permute-start.1 = (f32[4,8,512]{2,1,0:T(8,128)S(1)}, f32[4,8,512]{2,1,0:T(8,128)S(1)}, u32[]{:S(2)}, u32[]{:S(2)}) collective-permute-start(f32[4,8,512]{2,1,0:T(8,128)S(1)} %get-tuple-element.21), channel_id=1, source_target_pairs={{0,1},{1,0},{2,3},{3,2},{4,5},{5,4},{6,7},{7,6},{8,9},{9,8},{10,11... | collective-permute-start | bytes 196616 | tf_op jit(solution)/shard_map/ppermute | solution.py:399
  13.3 2.1 %collective-permute-start.6 = (f32[32,8,128]{2,1,0:T(8,128)S(1)}, f32[32,8,128]{2,1,0:T(8,128)S(1)}, u32[]{:S(2)}, u32[]{:S(2)}) collective-permute-start(f32[32,8,128]{2,1,0:T(8,128)S(1)} %get-tuple-element.24.refs_0_.refs_1_), channel_id=1, source_target_pairs={{0,1},{1,0},{2,3},{3,2},{4,5},{5,4},{6,7},{7,6},{8,9},{9,8},{10,11... | collective-permute-start | bytes 393224 | tf_op jit(solution)/shard_map/ppermute | solution.py:426
  13.3 5.0 %collective-permute-start.7 = (f32[32,8,128]{2,1,0:T(8,128)S(1)}, f32[32,8,128]{2,1,0:T(8,128)S(1)}, u32[]{:S(2)}, u32[]{:S(2)}) collective-permute-start(f32[32,8,128]{2,1,0:T(8,128)S(1)} %get-tuple-element.24.refs_0_.refs_1_), channel_id=1, source_target_pairs={{1,4},{4,1},{5,8},{8,5},{9,12},{12,9},{0,16},{13,29},{3,6},{6,3},{... | collective-permute-start | bytes 393224 | tf_op jit(solution)/shard_map/ppermute | solution.py:425
  19.3 2.1 %collective-permute-start.8 = (f32[32,8,128]{2,1,0:T(8,128)S(1)}, f32[32,8,128]{2,1,0:T(8,128)S(1)}, u32[]{:S(2)}, u32[]{:S(2)}) collective-permute-start(f32[32,8,128]{2,1,0:T(8,128)S(1)} %get-tuple-element.25.refs_0_.refs_1_), channel_id=1, source_target_pairs={{0,1},{1,0},{2,3},{3,2},{4,5},{5,4},{6,7},{7,6},{8,9},{9,8},{10,11... | collective-permute-start | bytes 393224 | tf_op jit(solution)/shard_map/ppermute | solution.py:426
  19.5 5.0 %collective-permute-start.9 = (f32[32,8,128]{2,1,0:T(8,128)S(1)}, f32[32,8,128]{2,1,0:T(8,128)S(1)}, u32[]{:S(2)}, u32[]{:S(2)}) collective-permute-start(f32[32,8,128]{2,1,0:T(8,128)S(1)} %get-tuple-element.25.refs_0_.refs_1_), channel_id=1, source_target_pairs={{1,4},{4,1},{5,8},{8,5},{9,12},{12,9},{0,16},{13,29},{3,6},{6,3},{... | collective-permute-start | bytes 393224 | tf_op jit(solution)/shard_map/ppermute | solution.py:425
  25.4 2.7 %collective-permute-start.10 = (f32[32,8,128]{2,1,0:T(8,128)S(1)}, f32[32,8,128]{2,1,0:T(8,128)S(1)}, u32[]{:S(2)}, u32[]{:S(2)}) collective-permute-start(f32[32,8,128]{2,1,0:T(8,128)S(1)} %get-tuple-element.26.refs_1_), channel_id=1, source_target_pairs={{0,1},{1,0},{2,3},{3,2},{4,5},{5,4},{6,7},{7,6},{8,9},{9,8},{10,11... | collective-permute-start | bytes 393224 | tf_op jit(solution)/shard_map/ppermute | solution.py:426
  25.6 5.0 %collective-permute-start.11 = (f32[32,8,128]{2,1,0:T(8,128)S(1)}, f32[32,8,128]{2,1,0:T(8,128)S(1)}, u32[]{:S(2)}, u32[]{:S(2)}) collective-permute-start(f32[32,8,128]{2,1,0:T(8,128)S(1)} %get-tuple-element.26.refs_1_), channel_id=1, source_target_pairs={{1,4},{4,1},{5,8},{8,5},{9,12},{12,9},{0,16},{13,29},{3,6},{6,3},{... | collective-permute-start | bytes 393224 | tf_op jit(solution)/shard_map/ppermute | solution.py:425
  32.0 2.6 %collective-permute-start.12 = (f32[5,8,512]{2,1,0:T(8,128)S(1)}, f32[5,8,512]{2,1,0:T(8,128)S(1)}, u32[]{:S(2)}, u32[]{:S(2)}) collective-permute-start(f32[5,8,512]{2,1,0:T(8,128)S(1)} %get-tuple-element.32), channel_id=1, source_target_pairs={{0,1},{1,0},{2,3},{3,2},{4,5},{5,4},{6,7},{7,6},{8,9},{9,8},{10,11... | collective-permute-start | bytes 245768 | tf_op jit(solution)/shard_map/ppermute | solution.py:449
  32.2 4.6 %collective-permute-start.13 = (f32[2,8,512]{2,1,0:T(8,128)S(1)}, f32[2,8,512]{2,1,0:T(8,128)S(1)}, u32[]{:S(2)}, u32[]{:S(2)}) collective-permute-start(f32[2,8,512]{2,1,0:T(8,128)S(1)} %get-tuple-element.33), channel_id=1, source_target_pairs={{0,1},{1,0},{2,3},{3,2},{4,5},{5,4},{6,7},{7,6},{8,9},{9,8},{10,11... | collective-permute-start | bytes 98312 | tf_op jit(solution)/shard_map/ppermute | solution.py:436
  32.6 4.2 %collective-permute-start.14 = (f32[2,8,512]{2,1,0:T(8,128)S(1)}, f32[2,8,512]{2,1,0:T(8,128)S(1)}, u32[]{:S(2)}, u32[]{:S(2)}) collective-permute-start(f32[2,8,512]{2,1,0:T(8,128)S(1)} %bitcast.10), channel_id=1, source_target_pairs={{0,2},{2,0},{1,3},{3,1},{4,6},{6,4},{5,7},{7,5},{8,10},{10,8},{9,1... | collective-permute-start | bytes 98312 | tf_op jit(solution)/shard_map/ppermute | solution.py:374
  33.2 3.7 %collective-permute-start.15 = (f32[2,8,512]{2,1,0:T(8,128)S(1)}, f32[2,8,512]{2,1,0:T(8,128)S(1)}, u32[]{:S(2)}, u32[]{:S(2)}) collective-permute-start(f32[2,8,512]{2,1,0:T(8,128)S(1)} %bitcast.9), channel_id=1, source_target_pairs={{0,3},{1,2},{2,1},{3,0},{4,7},{5,6},{6,5},{7,4},{8,11},{9,10},{10,... | collective-permute-start | bytes 98312 | tf_op jit(solution)/shard_map/ppermute | solution.py:378
  34.1 3.9 %collective-permute-start.16 = (f32[1,8,512]{2,1,0:T(8,128)S(1)}, f32[1,8,512]{2,1,0:T(8,128)S(1)}, u32[]{:S(2)}, u32[]{:S(2)}) collective-permute-start(f32[1,8,512]{2,1,0:T(8,128)S(1)} %get-tuple-element.36.refs_4_), channel_id=1, source_target_pairs={{0,2},{2,0},{1,3},{3,1},{4,6},{6,4},{5,7},{7,5},{8,10},{10,8},{9,1... | collective-permute-start | bytes 49160 | tf_op jit(solution)/shard_map/ppermute | solution.py:374
  34.7 3.3 %collective-permute-start.17 = (f32[1,8,512]{2,1,0:T(8,128)S(1)}, f32[1,8,512]{2,1,0:T(8,128)S(1)}, u32[]{:S(2)}, u32[]{:S(2)}) collective-permute-start(f32[1,8,512]{2,1,0:T(8,128)S(1)} %get-tuple-element.37), channel_id=1, source_target_pairs={{0,3},{1,2},{2,1},{3,0},{4,7},{5,6},{6,5},{7,4},{8,11},{9,10},{10,... | collective-permute-start | bytes 49160 | tf_op jit(solution)/shard_map/ppermute | solution.py:378

commit v5 on v4

--- a/solution.py
+++ b/solution.py
@@ -110,6 +110,20 @@
             natural = [x_ref[0, p, rows, t * LANES : (t + 1) * LANES] for t in range(half)]
             for i, tile in enumerate(compacted(natural)):
                 target[p * half + i] = tile
+
+
+def pack_block(mate, part_ref, other_ref, *refs):
+    core = lax.axis_index("sub")
+    block_ref = refs[-1]
+    half = part_ref.shape[0] // PARTS
+    rows = both_rows()[1 if mate else 0]
+    for p in range(PARTS):
+        mine = [part_ref[p * half + i] for i in range(half)]
+        theirs = compacted([other_ref[0, p, rows, t * LANES : (t + 1) * LANES] for t in range(half)])
+        left = [jnp.where(core == 0, x, y) for x, y in zip(mine, theirs)]
+        right = [jnp.where(core == 0, y, x) for x, y in zip(mine, theirs)]
+        for j, tile in enumerate(merged(left, right)):
+            block_ref[2 * p * half + j] = tile
 
 
 def pack_velocity(order_ref, *refs):
@@ -223,22 +237,6 @@
     return jnp.concatenate(mine, axis=1), jnp.concatenate(theirs, axis=1)
 
 
-def whole_blocks(refs):
-    core = lax.axis_index("sub")
-    half = refs[0].shape[0] // PARTS
-    blocks = []
-    for ours, others in (refs[0:2], refs[2:4], refs[4:6]):
-        tiles = []
-        for p in range(PARTS):
-            a = [ours[p * half + i] for i in range(half)]
-            b = [others[p * half + i] for i in range(half)]
-            left = [jnp.where(core == 0, x, y) for x, y in zip(a, b)]
-            right = [jnp.where(core == 0, y, x) for x, y in zip(a, b)]
-            tiles += merged(left, right)
-        blocks.append(tiles)
-    return blocks
-
-
 def depth_step(kcheb, bins, first, final, *refs):
     core = lax.axis_index("sub")
     block = lax.axis_index("lat") * 2 + core
@@ -265,12 +263,9 @@
     own = 2 * ROWS
     up_ok = block > 0
     down_ok = block < blocks - 1
-    if first:
-        parts, refs = whole_blocks(refs[:6]), refs[6:]
-    else:
-        parts, refs = [[r[i] for i in range(PARTS * tiles)] for r in refs[:3]], refs[3:]
+    sources, refs = refs[:3], refs[3:]
     for i in range(PARTS * tiles):
-        mine, a, b = [part[i] for part in parts]
+        mine, a, b = [source[i] for source in sources]
         terms[0, i, pl.ds(own, ROWS), :] = mine
         terms[0, i, pl.ds(own - ROWS, ROWS), :] = jnp.where(up_ok, jnp.where(core == 0, b, a), 0.0)
         terms[0, i, pl.ds(own + ROWS, ROWS), :] = jnp.where(down_ok, jnp.where(core == 0, a, b), 0.0)
@@ -389,10 +384,12 @@
     chain = chain_permutation(lax.axis_size("shots"), lat, freq)
     axes = ("shots", "lat", "freq", "sub")
     compact = (PARTS * tiles // 2, ROWS, LANES)
-    own, mate = call(arrange_fields, (compact, compact), (wavefields,))
-    across = lax.ppermute(mate, "sub", SWAP)
-    start = (own, across, mate, lax.ppermute(own, "sub", SWAP))
-    start += (lax.ppermute(across, axes, chain), lax.ppermute(own, axes, chain))
+    block = (PARTS * tiles, ROWS, LANES)
+    other = lax.ppermute(wavefields, "sub", SWAP)
+    own_part, mate_part = call(arrange_fields, (compact, compact), (wavefields,))
+    own = call(functools.partial(pack_block, False), (block,), (own_part, other))[0]
+    zmate = lax.ppermute(own, axes, chain)
+    mate = call(functools.partial(pack_block, True), (block,), (mate_part, other, own))[0]
 
     strip = (depths, ROWS, cols)
     keep, send = call(pack_velocity, (strip, strip), (order, *slabs))
@@ -410,8 +407,7 @@
         pltpu.VMEM((2, 2 * terms, ROWS, LANES), f32),
     ]
     ready = [(table, keep, theirs)] + [None] * (depths - 1)
-    block = (PARTS * tiles, ROWS, LANES)
-    state = start
+    state = (own, mate, zmate)
     images = []
     for depth in range(depths - 1):
         own, image = call(
@@ -423,7 +419,8 @@
         )
         images.append(image)
         zmate = lax.ppermute(own, axes, chain)
-        state = (own, lax.ppermute(own, "sub", SWAP), zmate)
+        mate = lax.ppermute(own, "sub", SWAP)
+        state = (own, mate, zmate)
         wanted = [depth + 1] if depth + 1 < depths - 1 else []
         if depth == max(depths - 3, 0):
             wanted.append(depths - 1)

time: 38.8 us -> 37.3 us (0.961)
  waiting for transfers between devices: 12.4 us -> 9.75 us
  starting transfers between devices: 13.5 us -> 14.1 us
  Pallas kernels: 9.66 us -> 10.1 us
    ppermute x3 -> x4, starting transfers between devices: 3.11 us -> 6.21 us  [body(): zmate = lax.ppermute(own, axes, chain)]
    ppermute x7 -> x4, waiting for transfers between devices: 2.72 us -> 0.01 us  [the longest x3 0.01 us: body(): mate = lax.ppermute(own, 'sub', SWAP)]
    ppermute x7 -> x4, starting transfers between devices: 3.09 us -> 0.99 us  [the longest x1 0.56 us: body(): other = lax.ppermute(wavefields, 'sub', SWAP)]
    ppermute x2, waiting for transfers between devices: 0.01 us -> 0.93 us  [crossed(): return lax.ppermute(value, ('freq', 'sub'), pairs)]
    ppermute x2, starting transfers between devices: 2.39 us -> 1.49 us  [crossed(): return lax.ppermute(value, ('freq', 'sub'), pairs)]
    ppermute x2, starting transfers between devices: 1.1 us -> 2 us  [shifted(): lax.ppermute(value, 'freq', [(i, (i + s) % freq) for i in range(freq)])]
    ppermute x3 -> x4, waiting for transfers between devices: 8.44 us -> 7.6 us  [body(): zmate = lax.ppermute(own, axes, chain)]
    ppermute x2, waiting for transfers between devices: 1.2 us -> 0.53 us  [shifted(): lax.ppermute(value, 'freq', [(i, (i + s) % freq) for i in range(freq)])]
  transfers between devices with their start and end apart: 18 -> 16, of which waited for: 7 -> 9; matrix products, arithmetic and copies ran while one was open for 2% -> 2% of each run, Pallas kernels for 11% -> 14%
where the time goes in v5:
time: 37.3 us; the launch traced here: 37.1 us
  starting transfers between devices  14.1 us (38%)
  Pallas kernels  10.1 us (27%)
  waiting for transfers between devices  9.75 us (26%)
  local copies, waits for them, and re-layouts  1.71 us (5%)
  between operations  1.45 us (4%)
    pallas_call x14, Pallas kernels, call(): pl.pallas_call(kernel, out_shape=tuple((jax.ShapeDtypeStruct(o, f32) for...  10.1 us
    ppermute x4, waiting for transfers between devices, body(): zmate = lax.ppermute(own, axes, chain)  7.6 us
    ppermute x4, starting transfers between devices, body(): zmate = lax.ppermute(own, axes, chain)  6.21 us
    ppermute x1, starting transfers between devices, body(): lax.ppermute(velocity, 'freq', [((i + s) % freq, i) for i in range(freq)])  2.55 us
    ppermute x2, starting transfers between devices, shifted(): lax.ppermute(value, 'freq', [(i, (i + s) % freq) for i in range(freq)])  2 us
    ppermute x2, starting transfers between devices, crossed(): return lax.ppermute(value, ('freq', 'sub'), pairs)  1.49 us
    unnamed x8, local copies, waits for them, and re-layouts  1.07 us
    ppermute x2, waiting for transfers between devices, crossed(): return lax.ppermute(value, ('freq', 'sub'), pairs)  0.93 us
  transfers between devices with their start and end apart: 16, of which 9 were waited for; matrix products, arithmetic and copies ran while one was open for 2% of the time, Pallas kernels for 14%

profile of v5, /device:TPU:0, one launch (start us, length us, event | category | flops | bytes accessed | tf_op | source)
XLA Modules:
  0.0 37.1 jit_solution(17527432702718609939)
XLA Ops:
  0.6 0.6 %collective-permute-start.2 = (f32[1,4,16,512]{3,2,1,0:T(8,128)}, f32[1,4,16,512]{3,2,1,0:T(8,128)S(1)}, u32[]{:S(2)}, u32[]{:S(2)}) collective-permute-start(f32[1,4,16,512]{3,2,1,0:T(8,128)} %x_ref.1), channel_id=1, source_target_pairs={{0,1},{1,0},{2,3},{3,2},{4,5},{5,4},{6,7},{7,6},{8,9},{9,8},{10,11... | collective-permute-start | bytes 393224 | tf_op jit(solution)/shard_map/ppermute | solution.py:388
  1.2 2.6 %collective-permute-start = (f32[4,16,512]{2,1,0:T(8,128)}, f32[4,16,512]{2,1,0:T(8,128)S(1)}, u32[]{:S(2)}, u32[]{:S(2)}) collective-permute-start(f32[4,16,512]{2,1,0:T(8,128)} %refs_0_.1), channel_id=1, source_target_pairs={{2,0},{0,2},{3,1},{1,3},{6,4},{4,6},{7,5},{5,7},{10,8},{8,10},{11,... | collective-permute-start | bytes 393224 | tf_op jit(solution)/shard_map/ppermute | solution.py:377
  3.8 0.9 %copy-done.1 = f32[1,4,16,512]{3,2,1,0:T(8,128)S(1)} copy-done((f32[1,4,16,512]{3,2,1,0:T(8,128)S(1)}, f32[1,4,16,512]{3,2,1,0:T(8,128)}, u32[]{:S(2)}) %copy-start.1) | copy-done | bytes 131096
  4.7 0.3 shard_map.69
  5.3 1.6 %collective-permute-start.3 = (f32[32,8,128]{2,1,0:T(8,128)S(1)}, f32[32,8,128]{2,1,0:T(8,128)S(1)}, u32[]{:S(2)}, u32[]{:S(2)}) collective-permute-start(f32[32,8,128]{2,1,0:T(8,128)S(1)} %shard_map.70.refs_0_.refs_3_), channel_id=1, source_target_pairs={{1,4},{4,1},{5,8},{8,5},{9,12},{12,9},{0,16},{13,29},{3,6},{6,3},{... | collective-permute-start | bytes 393224 | tf_op jit(solution)/shard_map/ppermute | solution.py:391
  7.6 0.5 %collective-permute-done.refs_1_ = f32[4,16,512]{2,1,0:T(8,128)S(1)} collective-permute-done((f32[4,16,512]{2,1,0:T(8,128)}, f32[4,16,512]{2,1,0:T(8,128)S(1)}, u32[]{:S(2)}, u32[]{:S(2)}) %collective-permute-start) | collective-permute-done | bytes 131104 | tf_op jit(solution)/shard_map/ppermute | solution.py:377
  8.6 0.4 constant_dynamic-slice_fusion
  9.7 0.7 %collective-permute-done.3.refs_5_ = f32[32,8,128]{2,1,0:T(8,128)S(1)} collective-permute-done((f32[32,8,128]{2,1,0:T(8,128)S(1)}, f32[32,8,128]{2,1,0:T(8,128)S(1)}, u32[]{:S(2)}, u32[]{:S(2)}) %collective-permute-start.3) | collective-permute-done | bytes 131104 | tf_op jit(solution)/shard_map/ppermute | solution.py:391
  10.3 1.1 %shard_map.72 = (f32[32,8,128]{2,1,0:T(8,128)S(1)}, f32[8,8,128]{2,1,0:T(8,128)S(1)}) custom-call(f32[18,128]{1,0:T(8,128)S(1)} %pad.4.refs_0_.table_ref, f32[4,8,512]{2,1,0:T(8,128)S(1)} %get-tuple-element.20.refs_1_.keep_ref, f32[4,8,512]{2,1,0:T(8,128)S(1)} %collective-permute-done.1.refs_2_.other_ref, f32[32,8,128]{2,1,0:T(8,128)S(1)} %shard_map.70.refs_0_.refs_3_, ...), custom_call_target="tpu_custom_call" | custom-call | flops 1048576 | bytes 65536 | tf_op jit(solution)/shard_map/pallas_call | solution.py:358
  11.5 1.6 %collective-permute-start.5 = (f32[32,8,128]{2,1,0:T(8,128)S(1)}, f32[32,8,128]{2,1,0:T(8,128)S(1)}, u32[]{:S(2)}, u32[]{:S(2)}) collective-permute-start(f32[32,8,128]{2,1,0:T(8,128)S(1)} %get-tuple-element.24.refs_0_.refs_1_), channel_id=1, source_target_pairs={{1,4},{4,1},{5,8},{8,5},{9,12},{12,9},{0,16},{13,29},{3,6},{6,3},{... | collective-permute-start | bytes 393224 | tf_op jit(solution)/shard_map/ppermute | solution.py:421
  13.1 1.0 %shard_map.73.refs_0_ = f32[18,8,8,128]{3,2,1,0:T(8,128)S(1)} custom-call(f32[18,128]{1,0:T(8,128)S(1)} %pad.4.refs_0_.table_ref, f32[4,8,512]{2,1,0:T(8,128)S(1)} %get-tuple-element.20.refs_1_.keep_ref, f32[4,8,512]{2,1,0:T(8,128)S(1)} %collective-permute-done.1.refs_2_.other_ref, f32[32,8,128]{2,1,0:T(8,128)S(1)} %get-tuple-element.24.refs_0_.refs_1_), custom_call_target="tpu_custom_call" | custom-call | flops 1048576 | bytes 65536 | tf_op jit(solution)/shard_map/pallas_call | solution.py:358
  14.1 2.5 %collective-permute-done.5.refs_3_ = f32[32,8,128]{2,1,0:T(8,128)S(1)} collective-permute-done((f32[32,8,128]{2,1,0:T(8,128)S(1)}, f32[32,8,128]{2,1,0:T(8,128)S(1)}, u32[]{:S(2)}, u32[]{:S(2)}) %collective-permute-start.5) | collective-permute-done | bytes 131104 | tf_op jit(solution)/shard_map/ppermute | solution.py:421
  16.6 0.9 %shard_map.74 = (f32[32,8,128]{2,1,0:T(8,128)S(1)}, f32[8,8,128]{2,1,0:T(8,128)S(1)}) custom-call(f32[18,8,8,128]{3,2,1,0:T(8,128)S(1)} %shard_map.73.refs_0_, f32[32,8,128]{2,1,0:T(8,128)S(1)} %get-tuple-element.24.refs_0_.refs_1_, f32[32,8,128]{2,1,0:T(8,128)S(1)} %collective-permute-done.4.refs_2_, f32[32,8,128]{2,1,0:T(8,128)S(1)} %collective-permute-done.5.refs_3_), custom_call_target="tpu_custom_call" | custom-call | flops 1048576 | bytes 65536 | tf_op jit(solution)/shard_map/pallas_call | solution.py:358
  17.7 1.5 %collective-permute-start.7 = (f32[32,8,128]{2,1,0:T(8,128)S(1)}, f32[32,8,128]{2,1,0:T(8,128)S(1)}, u32[]{:S(2)}, u32[]{:S(2)}) collective-permute-start(f32[32,8,128]{2,1,0:T(8,128)S(1)} %get-tuple-element.25.refs_0_.refs_1_), channel_id=1, source_target_pairs={{1,4},{4,1},{5,8},{8,5},{9,12},{12,9},{0,16},{13,29},{3,6},{6,3},{... | collective-permute-start | bytes 393224 | tf_op jit(solution)/shard_map/ppermute | solution.py:421
  19.2 1.0 %shard_map.76.refs_0_ = f32[18,8,8,128]{3,2,1,0:T(8,128)S(1)} custom-call(f32[18,128]{1,0:T(8,128)S(1)} %pad.4.refs_0_.table_ref, f32[4,8,512]{2,1,0:T(8,128)S(1)} %get-tuple-element.20.refs_1_.keep_ref, f32[4,8,512]{2,1,0:T(8,128)S(1)} %collective-permute-done.1.refs_2_.other_ref, f32[32,8,128]{2,1,0:T(8,128)S(1)} %get-tuple-element.25.refs_0_.refs_1_), custom_call_target="tpu_custom_call" | custom-call | flops 1048576 | bytes 65536 | tf_op jit(solution)/shard_map/pallas_call | solution.py:358
  20.2 2.5 %collective-permute-done.7.refs_3_ = f32[32,8,128]{2,1,0:T(8,128)S(1)} collective-permute-done((f32[32,8,128]{2,1,0:T(8,128)S(1)}, f32[32,8,128]{2,1,0:T(8,128)S(1)}, u32[]{:S(2)}, u32[]{:S(2)}) %collective-permute-start.7) | collective-permute-done | bytes 131104 | tf_op jit(solution)/shard_map/ppermute | solution.py:421
  22.7 0.9 %shard_map.77 = (f32[32,8,128]{2,1,0:T(8,128)S(1)}, f32[8,8,128]{2,1,0:T(8,128)S(1)}) custom-call(f32[18,8,8,128]{3,2,1,0:T(8,128)S(1)} %shard_map.76.refs_0_, f32[32,8,128]{2,1,0:T(8,128)S(1)} %get-tuple-element.25.refs_0_.refs_1_, f32[32,8,128]{2,1,0:T(8,128)S(1)} %collective-permute-done.6.refs_2_, f32[32,8,128]{2,1,0:T(8,128)S(1)} %collective-permute-done.7.refs_3_), custom_call_target="tpu_custom_call" | custom-call | flops 1048576 | bytes 65536 | tf_op jit(solution)/shard_map/pallas_call | solution.py:358
  23.8 1.5 %collective-permute-start.9 = (f32[32,8,128]{2,1,0:T(8,128)S(1)}, f32[32,8,128]{2,1,0:T(8,128)S(1)}, u32[]{:S(2)}, u32[]{:S(2)}) collective-permute-start(f32[32,8,128]{2,1,0:T(8,128)S(1)} %get-tuple-element.26.refs_1_), channel_id=1, source_target_pairs={{1,4},{4,1},{5,8},{8,5},{9,12},{12,9},{0,16},{13,29},{3,6},{6,3},{... | collective-permute-start | bytes 393224 | tf_op jit(solution)/shard_map/ppermute | solution.py:421
  25.3 1.0 %shard_map.75.refs_3_.refs_0_ = f32[18,8,8,128]{3,2,1,0:T(8,128)S(1)} custom-call(f32[18,128]{1,0:T(8,128)S(1)} %pad.4.refs_0_.table_ref, f32[4,8,512]{2,1,0:T(8,128)S(1)} %get-tuple-element.20.refs_1_.keep_ref, f32[4,8,512]{2,1,0:T(8,128)S(1)} %collective-permute-done.1.refs_2_.other_ref, f32[32,8,128]{2,1,0:T(8,128)S(1)} %get-tuple-element.25.refs_0_.refs_1_), custom_call_target="tpu_custom_call" | custom-call | flops 1048576 | bytes 65536 | tf_op jit(solution)/shard_map/pallas_call | solution.py:358
  26.3 0.5 %shard_map.78 = (f32[2,8,512]{2,1,0:T(8,128)S(1)}, f32[2,8,512]{2,1,0:T(8,128)S(1)}, f32[1,2,8,512]{3,2,1,0:T(8,128)S(1)}, f32[1,2,8,512]{3,2,1,0:T(8,128)S(1)}) custom-call(f32[8,8,128]{2,1,0:T(8,128)S(1)} %get-tuple-element.27.refs_0_, f32[8,8,128]{2,1,0:T(8,128)S(1)} %get-tuple-element.28.refs_1_, f32[8,8,128]{2,1,0:T(8,128)S(1)} %get-tuple-element.29.refs_2_, ...), custom_call_target="tpu_custom_call" | custom-call | flops 1048576 | bytes 65536 | tf_op jit(solution)/shard_map/pallas_call | solution.py:358
  26.8 2.0 %collective-permute-done.9.refs_3_ = f32[32,8,128]{2,1,0:T(8,128)S(1)} collective-permute-done((f32[32,8,128]{2,1,0:T(8,128)S(1)}, f32[32,8,128]{2,1,0:T(8,128)S(1)}, u32[]{:S(2)}, u32[]{:S(2)}) %collective-permute-start.9) | collective-permute-done | bytes 131104 | tf_op jit(solution)/shard_map/ppermute | solution.py:421
  28.8 1.5 %shard_map.79 = (f32[4,8,512]{2,1,0:T(8,128)S(1)}, f32[1,8,512]{2,1,0:T(8,128)S(1)}, f32[5,8,512]{2,1,0:T(8,128)S(1)}, f32[1,8,512]{2,1,0:T(8,128)S(1)}) custom-call(f32[18,8,8,128]{3,2,1,0:T(8,128)S(1)} %shard_map.75.refs_3_.refs_0_, f32[32,8,128]{2,1,0:T(8,128)S(1)} %get-tuple-element.26.refs_1_, f32[32,8,128]{2,1,0:T(8,128)S(1)} %collective-permute-done.8.refs_2_, ...), custom_call_target="tpu_custom_call" | custom-call | flops 1048576 | bytes 65536 | tf_op jit(solution)/shard_map/pallas_call | solution.py:358
  30.4 0.4 %collective-permute-start.11 = (f32[2,8,512]{2,1,0:T(8,128)S(1)}, f32[2,8,512]{2,1,0:T(8,128)S(1)}, u32[]{:S(2)}, u32[]{:S(2)}) collective-permute-start(f32[2,8,512]{2,1,0:T(8,128)S(1)} %get-tuple-element.33), channel_id=1, source_target_pairs={{0,1},{1,0},{2,3},{3,2},{4,5},{5,4},{6,7},{7,6},{8,9},{9,8},{10,11... | collective-permute-start | bytes 98312 | tf_op jit(solution)/shard_map/ppermute | solution.py:433
  30.8 1.0 %collective-permute-start.12 = (f32[2,8,512]{2,1,0:T(8,128)S(1)}, f32[2,8,512]{2,1,0:T(8,128)S(1)}, u32[]{:S(2)}, u32[]{:S(2)}) collective-permute-start(f32[2,8,512]{2,1,0:T(8,128)S(1)} %bitcast.10), channel_id=1, source_target_pairs={{0,2},{2,0},{1,3},{3,1},{4,6},{6,4},{5,7},{7,5},{8,10},{10,8},{9,1... | collective-permute-start | bytes 98312 | tf_op jit(solution)/shard_map/ppermute | solution.py:369
  31.8 0.5 %collective-permute-start.13 = (f32[2,8,512]{2,1,0:T(8,128)S(1)}, f32[2,8,512]{2,1,0:T(8,128)S(1)}, u32[]{:S(2)}, u32[]{:S(2)}) collective-permute-start(f32[2,8,512]{2,1,0:T(8,128)S(1)} %bitcast.9), channel_id=1, source_target_pairs={{0,3},{1,2},{2,1},{3,0},{4,7},{5,6},{6,5},{7,4},{8,11},{9,10},{10,... | collective-permute-start | bytes 98312 | tf_op jit(solution)/shard_map/ppermute | solution.py:373
  32.3 1.0 %collective-permute-start.14 = (f32[1,8,512]{2,1,0:T(8,128)S(1)}, f32[1,8,512]{2,1,0:T(8,128)S(1)}, u32[]{:S(2)}, u32[]{:S(2)}) collective-permute-start(f32[1,8,512]{2,1,0:T(8,128)S(1)} %get-tuple-element.36.refs_4_), channel_id=1, source_target_pairs={{0,2},{2,0},{1,3},{3,1},{4,6},{6,4},{5,7},{7,5},{8,10},{10,8},{9,1... | collective-permute-start | bytes 49160 | tf_op jit(solution)/shard_map/ppermute | solution.py:369
  33.3 1.0 %collective-permute-start.15 = (f32[1,8,512]{2,1,0:T(8,128)S(1)}, f32[1,8,512]{2,1,0:T(8,128)S(1)}, u32[]{:S(2)}, u32[]{:S(2)}) collective-permute-start(f32[1,8,512]{2,1,0:T(8,128)S(1)} %get-tuple-element.37), channel_id=1, source_target_pairs={{0,3},{1,2},{2,1},{3,0},{4,7},{5,6},{6,5},{7,4},{8,11},{9,10},{10,... | collective-permute-start | bytes 49160 | tf_op jit(solution)/shard_map/ppermute | solution.py:373
  34.3 0.7 %shard_map.80 = f32[1,4,16,512]{3,2,1,0:T(8,128)} custom-call(f32[4,8,512]{2,1,0:T(8,128)S(1)} %get-tuple-element.31.kept_ref, f32[5,8,512]{2,1,0:T(8,128)S(1)} %collective-permute-done.10.sub_ref.refs_5_), custom_call_target="tpu_custom_call" | custom-call | flops 1048576 | bytes 65536 | tf_op jit(solution)/shard_map/pallas_call | solution.py:358
  35.0 0.5 %collective-permute-done.13.refs_3_ = f32[2,8,512]{2,1,0:T(8,128)S(1)} collective-permute-done((f32[2,8,512]{2,1,0:T(8,128)S(1)}, f32[2,8,512]{2,1,0:T(8,128)S(1)}, u32[]{:S(2)}, u32[]{:S(2)}) %collective-permute-start.13) | collective-permute-done | bytes 32800 | tf_op jit(solution)/shard_map/ppermute | solution.py:373
  35.5 0.5 %collective-permute-done.14.refs_6_ = f32[1,8,512]{2,1,0:T(8,128)S(1)} collective-permute-done((f32[1,8,512]{2,1,0:T(8,128)S(1)}, f32[1,8,512]{2,1,0:T(8,128)S(1)}, u32[]{:S(2)}, u32[]{:S(2)}) %collective-permute-start.14) | collective-permute-done | bytes 16416 | tf_op jit(solution)/shard_map/ppermute | solution.py:369
  36.0 0.4 %collective-permute-done.15.refs_7_ = f32[1,8,512]{2,1,0:T(8,128)S(1)} collective-permute-done((f32[1,8,512]{2,1,0:T(8,128)S(1)}, f32[1,8,512]{2,1,0:T(8,128)S(1)}, u32[]{:S(2)}, u32[]{:S(2)}) %collective-permute-start.15) | collective-permute-done | bytes 16416 | tf_op jit(solution)/shard_map/ppermute | solution.py:373
  36.5 0.6 %shard_map.81 = f32[2,16,512]{2,1,0:T(8,128)} custom-call(f32[2,8,512]{2,1,0:T(8,128)S(1)} %get-tuple-element.30.refs_4_.refs_0_, f32[2,8,512]{2,1,0:T(8,128)S(1)} %collective-permute-done.11.refs_1_, f32[2,8,512]{2,1,0:T(8,128)S(1)} %collective-permute-done.12.refs_2_, f32[2,8,512]{2,1,0:T(8,128)S(1)} %collective-permute-done.13.refs_3_, ...), custom_call_target="tpu_custom_call" | custom-call | flops 1048576 | bytes 65536 | tf_op jit(solution)/shard_map/pallas_call | solution.py:358
  (27 shorter events, 2.2 us)
Async XLA Ops:
  0.6 8.0 %copy-start = (f32[32,32,9,2]{1,3,2,0:T(2,128)S(1)}, f32[32,32,9,2]{1,3,2,0:T(2,128)}, u32[]{:S(2)}) copy-start(f32[32,32,9,2]{1,3,2,0:T(2,128)} %param.7) | copy-start | bytes 221188
  0.6 4.3 %collective-permute-start.2 = (f32[1,4,16,512]{3,2,1,0:T(8,128)}, f32[1,4,16,512]{3,2,1,0:T(8,128)S(1)}, u32[]{:S(2)}, u32[]{:S(2)}) collective-permute-start(f32[1,4,16,512]{3,2,1,0:T(8,128)} %x_ref.1), channel_id=1, source_target_pairs={{0,1},{1,0},{2,3},{3,2},{4,5},{5,4},{6,7},{7,6},{8,9},{9,8},{10,11... | collective-permute-start | bytes 393224 | tf_op jit(solution)/shard_map/ppermute | solution.py:388
  1.2 6.9 %collective-permute-start = (f32[4,16,512]{2,1,0:T(8,128)}, f32[4,16,512]{2,1,0:T(8,128)S(1)}, u32[]{:S(2)}, u32[]{:S(2)}) collective-permute-start(f32[4,16,512]{2,1,0:T(8,128)} %refs_0_.1), channel_id=1, source_target_pairs={{2,0},{0,2},{3,1},{1,3},{6,4},{4,6},{7,5},{5,7},{10,8},{8,10},{11,... | collective-permute-start | bytes 393224 | tf_op jit(solution)/shard_map/ppermute | solution.py:377
  3.8 0.9 %copy-start.1 = (f32[1,4,16,512]{3,2,1,0:T(8,128)S(1)}, f32[1,4,16,512]{3,2,1,0:T(8,128)}, u32[]{:S(2)}) copy-start(f32[1,4,16,512]{3,2,1,0:T(8,128)} %x_ref.1) | copy-start | bytes 393220
  5.0 3.3 %copy-start.2 = (f32[4,16,512]{2,1,0:T(8,128)S(1)}, f32[4,16,512]{2,1,0:T(8,128)}, u32[]{:S(2)}) copy-start(f32[4,16,512]{2,1,0:T(8,128)} %refs_0_.1) | copy-start | bytes 393220
  5.3 5.0 %collective-permute-start.3 = (f32[32,8,128]{2,1,0:T(8,128)S(1)}, f32[32,8,128]{2,1,0:T(8,128)S(1)}, u32[]{:S(2)}, u32[]{:S(2)}) collective-permute-start(f32[32,8,128]{2,1,0:T(8,128)S(1)} %shard_map.70.refs_0_.refs_3_), channel_id=1, source_target_pairs={{1,4},{4,1},{5,8},{8,5},{9,12},{12,9},{0,16},{13,29},{3,6},{6,3},{... | collective-permute-start | bytes 393224 | tf_op jit(solution)/shard_map/ppermute | solution.py:391
  7.5 0.7 %copy-start.3 = (s32[4]{0:T(128)S(1)}, s32[4]{0:T(128)}, u32[]{:S(2)}) copy-start(s32[4]{0:T(128)} %param.9) | copy-start | bytes 52
  8.3 1.3 %collective-permute-start.1 = (f32[4,8,512]{2,1,0:T(8,128)S(1)}, f32[4,8,512]{2,1,0:T(8,128)S(1)}, u32[]{:S(2)}, u32[]{:S(2)}) collective-permute-start(f32[4,8,512]{2,1,0:T(8,128)S(1)} %get-tuple-element.21), channel_id=1, source_target_pairs={{0,1},{1,0},{2,3},{3,2},{4,5},{5,4},{6,7},{7,6},{8,9},{9,8},{10,11... | collective-permute-start | bytes 196616 | tf_op jit(solution)/shard_map/ppermute | solution.py:396
  11.4 2.6 %collective-permute-start.4 = (f32[32,8,128]{2,1,0:T(8,128)S(1)}, f32[32,8,128]{2,1,0:T(8,128)S(1)}, u32[]{:S(2)}, u32[]{:S(2)}) collective-permute-start(f32[32,8,128]{2,1,0:T(8,128)S(1)} %get-tuple-element.24.refs_0_.refs_1_), channel_id=1, source_target_pairs={{0,1},{1,0},{2,3},{3,2},{4,5},{5,4},{6,7},{7,6},{8,9},{9,8},{10,11... | collective-permute-start | bytes 393224 | tf_op jit(solution)/shard_map/ppermute | solution.py:422
  11.5 5.0 %collective-permute-start.5 = (f32[32,8,128]{2,1,0:T(8,128)S(1)}, f32[32,8,128]{2,1,0:T(8,128)S(1)}, u32[]{:S(2)}, u32[]{:S(2)}) collective-permute-start(f32[32,8,128]{2,1,0:T(8,128)S(1)} %get-tuple-element.24.refs_0_.refs_1_), channel_id=1, source_target_pairs={{1,4},{4,1},{5,8},{8,5},{9,12},{12,9},{0,16},{13,29},{3,6},{6,3},{... | collective-permute-start | bytes 393224 | tf_op jit(solution)/shard_map/ppermute | solution.py:421
  17.5 2.7 %collective-permute-start.6 = (f32[32,8,128]{2,1,0:T(8,128)S(1)}, f32[32,8,128]{2,1,0:T(8,128)S(1)}, u32[]{:S(2)}, u32[]{:S(2)}) collective-permute-start(f32[32,8,128]{2,1,0:T(8,128)S(1)} %get-tuple-element.25.refs_0_.refs_1_), channel_id=1, source_target_pairs={{0,1},{1,0},{2,3},{3,2},{4,5},{5,4},{6,7},{7,6},{8,9},{9,8},{10,11... | collective-permute-start | bytes 393224 | tf_op jit(solution)/shard_map/ppermute | solution.py:422
  17.7 5.0 %collective-permute-start.7 = (f32[32,8,128]{2,1,0:T(8,128)S(1)}, f32[32,8,128]{2,1,0:T(8,128)S(1)}, u32[]{:S(2)}, u32[]{:S(2)}) collective-permute-start(f32[32,8,128]{2,1,0:T(8,128)S(1)} %get-tuple-element.25.refs_0_.refs_1_), channel_id=1, source_target_pairs={{1,4},{4,1},{5,8},{8,5},{9,12},{12,9},{0,16},{13,29},{3,6},{6,3},{... | collective-permute-start | bytes 393224 | tf_op jit(solution)/shard_map/ppermute | solution.py:421
  23.6 3.2 %collective-permute-start.8 = (f32[32,8,128]{2,1,0:T(8,128)S(1)}, f32[32,8,128]{2,1,0:T(8,128)S(1)}, u32[]{:S(2)}, u32[]{:S(2)}) collective-permute-start(f32[32,8,128]{2,1,0:T(8,128)S(1)} %get-tuple-element.26.refs_1_), channel_id=1, source_target_pairs={{0,1},{1,0},{2,3},{3,2},{4,5},{5,4},{6,7},{7,6},{8,9},{9,8},{10,11... | collective-permute-start | bytes 393224 | tf_op jit(solution)/shard_map/ppermute | solution.py:422
  23.8 5.0 %collective-permute-start.9 = (f32[32,8,128]{2,1,0:T(8,128)S(1)}, f32[32,8,128]{2,1,0:T(8,128)S(1)}, u32[]{:S(2)}, u32[]{:S(2)}) collective-permute-start(f32[32,8,128]{2,1,0:T(8,128)S(1)} %get-tuple-element.26.refs_1_), channel_id=1, source_target_pairs={{1,4},{4,1},{5,8},{8,5},{9,12},{12,9},{0,16},{13,29},{3,6},{6,3},{... | collective-permute-start | bytes 393224 | tf_op jit(solution)/shard_map/ppermute | solution.py:421
  30.3 3.0 %collective-permute-start.10 = (f32[5,8,512]{2,1,0:T(8,128)S(1)}, f32[5,8,512]{2,1,0:T(8,128)S(1)}, u32[]{:S(2)}, u32[]{:S(2)}) collective-permute-start(f32[5,8,512]{2,1,0:T(8,128)S(1)} %get-tuple-element.32), channel_id=1, source_target_pairs={{0,1},{1,0},{2,3},{3,2},{4,5},{5,4},{6,7},{7,6},{8,9},{9,8},{10,11... | collective-permute-start | bytes 245768 | tf_op jit(solution)/shard_map/ppermute | solution.py:446
  30.4 4.6 %collective-permute-start.11 = (f32[2,8,512]{2,1,0:T(8,128)S(1)}, f32[2,8,512]{2,1,0:T(8,128)S(1)}, u32[]{:S(2)}, u32[]{:S(2)}) collective-permute-start(f32[2,8,512]{2,1,0:T(8,128)S(1)} %get-tuple-element.33), channel_id=1, source_target_pairs={{0,1},{1,0},{2,3},{3,2},{4,5},{5,4},{6,7},{7,6},{8,9},{9,8},{10,11... | collective-permute-start | bytes 98312 | tf_op jit(solution)/shard_map/ppermute | solution.py:433
  30.8 4.2 %collective-permute-start.12 = (f32[2,8,512]{2,1,0:T(8,128)S(1)}, f32[2,8,512]{2,1,0:T(8,128)S(1)}, u32[]{:S(2)}, u32[]{:S(2)}) collective-permute-start(f32[2,8,512]{2,1,0:T(8,128)S(1)} %bitcast.10), channel_id=1, source_target_pairs={{0,2},{2,0},{1,3},{3,1},{4,6},{6,4},{5,7},{7,5},{8,10},{10,8},{9,1... | collective-permute-start | bytes 98312 | tf_op jit(solution)/shard_map/ppermute | solution.py:369
  31.8 3.7 %collective-permute-start.13 = (f32[2,8,512]{2,1,0:T(8,128)S(1)}, f32[2,8,512]{2,1,0:T(8,128)S(1)}, u32[]{:S(2)}, u32[]{:S(2)}) collective-permute-start(f32[2,8,512]{2,1,0:T(8,128)S(1)} %bitcast.9), channel_id=1, source_target_pairs={{0,3},{1,2},{2,1},{3,0},{4,7},{5,6},{6,5},{7,4},{8,11},{9,10},{10,... | collective-permute-start | bytes 98312 | tf_op jit(solution)/shard_map/ppermute | solution.py:373
  32.3 3.7 %collective-permute-start.14 = (f32[1,8,512]{2,1,0:T(8,128)S(1)}, f32[1,8,512]{2,1,0:T(8,128)S(1)}, u32[]{:S(2)}, u32[]{:S(2)}) collective-permute-start(f32[1,8,512]{2,1,0:T(8,128)S(1)} %get-tuple-element.36.refs_4_), channel_id=1, source_target_pairs={{0,2},{2,0},{1,3},{3,1},{4,6},{6,4},{5,7},{7,5},{8,10},{10,8},{9,1... | collective-permute-start | bytes 49160 | tf_op jit(solution)/shard_map/ppermute | solution.py:369
  33.3 3.2 %collective-permute-start.15 = (f32[1,8,512]{2,1,0:T(8,128)S(1)}, f32[1,8,512]{2,1,0:T(8,128)S(1)}, u32[]{:S(2)}, u32[]{:S(2)}) collective-permute-start(f32[1,8,512]{2,1,0:T(8,128)S(1)} %get-tuple-element.37), channel_id=1, source_target_pairs={{0,3},{1,2},{2,1},{3,0},{4,7},{5,6},{6,5},{7,4},{8,11},{9,10},{10,... | collective-permute-start | bytes 49160 | tf_op jit(solution)/shard_map/ppermute | solution.py:373

commit v6 on v5

--- a/solution.py
+++ b/solution.py
@@ -103,7 +103,32 @@
     return first + second
 
 
-def arrange_fields(x_ref, own_ref, mate_ref):
+def parted(tiles, core):
+    half = len(tiles) // 2
+    middle = LANES // 2
+    low = lane_ids() < middle
+    left = [jnp.where(low, tiles[i], pltpu.roll(tiles[i + half], middle, 1)) for i in range(half)]
+    right = [jnp.where(low, pltpu.roll(tiles[i], middle, 1), tiles[i + half]) for i in range(half)]
+    mine = [jnp.where(core == 0, a, b) for a, b in zip(left, right)]
+    theirs = [jnp.where(core == 0, b, a) for a, b in zip(left, right)]
+    return mine, theirs
+
+
+def loosened(tiles):
+    half = len(tiles)
+    lane = lane_ids()
+    natural = []
+    for t in range(half):
+        index = LANES // (2 * half) * t + lane // (2 * half) + LANES // 2 * (lane % (2 * half) // half)
+        value = pick(tiles[0], index)
+        for i in range(1, half):
+            value = jnp.where(lane % half == i, pick(tiles[i], index), value)
+        natural.append(value)
+    return jnp.concatenate(natural, axis=1)
+
+
+def arrange_fields(x_ref, *refs):
+    own_ref, mate_ref = refs[-2:]
     half = x_ref.shape[3] // LANES
     for target, rows in zip((own_ref, mate_ref), both_rows()):
         for p in range(PARTS):
@@ -127,7 +152,7 @@
 
 
 def pack_velocity(order_ref, *refs):
-    slabs, (keep_ref, send_ref) = refs[:-2], refs[-2:]
+    slabs, (keep_ref, send_ref) = refs[:-3], refs[-2:]
     core = lax.axis_index("sub")
     here = lax.axis_index("freq")
     count = len(slabs)
@@ -282,13 +307,15 @@
                 new_ref[p * tiles + j] = result[j][p]
             image_ref[j] = images[j]
         return
-    fields_ref, here_ref, sub_ref, cross_ref = refs[1:]
-    mine, theirs = halves(images, core)
-    here_ref[0] = mine
-    cross_ref[0] = theirs
-    sub_ref[PARTS] = theirs
+    fields_ref, send_ref, here_ref, image_ref = refs[1:]
+    half = tiles // 2
+    for i, (mine, theirs) in enumerate(zip(*parted(images, core))):
+        here_ref[i] = mine
+        image_ref[i] = theirs
     for p in range(PARTS):
-        fields_ref[p], sub_ref[p] = halves([total[p] for total in result], core)
+        for i, (mine, theirs) in enumerate(zip(*parted([total[p] for total in result], core))):
+            fields_ref[p * half + i] = mine
+            send_ref[p * half + i] = theirs
 
 
 def early_images(*refs):
@@ -322,11 +349,11 @@
     return [pl.ds(pl.multiple_of(c * ROWS, ROWS), ROWS) for c in (core, 1 - core)]
 
 
-def assemble_fields(kept_ref, sub_ref, fields_ref):
-    mine, theirs = both_rows()
-    for p in range(PARTS):
-        fields_ref[0, p, mine, :] = kept_ref[p]
-        fields_ref[0, p, theirs, :] = sub_ref[p]
+def assemble_fields(own_ref, got_ref, fields_ref):
+    half = own_ref.shape[0] // PARTS
+    for rows, ref in zip(both_rows(), (own_ref, got_ref)):
+        for p in range(PARTS):
+            fields_ref[0, p, rows, :] = loosened([ref[p * half + i] for i in range(half)])
 
 
 def assemble_images(count, *refs):
@@ -337,8 +364,9 @@
         for d in range(each):
             value = functools.reduce(jnp.add, [r[d] for r in early[side::2]])
             if d == each - 1:
-                last = functools.reduce(jnp.add, [r[r.shape[0] - 1] for r in late[side::2]])
-                value = value + jnp.where(holds_last, last, 0.0)
+                half = late[0].shape[0]
+                last = [functools.reduce(jnp.add, [r[i] for r in late[side::2]]) for i in range(half)]
+                value = value + jnp.where(holds_last, loosened(last), 0.0)
             image_ref[d, rows, :] = value
 
 
@@ -392,7 +420,7 @@
     mate = call(functools.partial(pack_block, True), (block,), (mate_part, other, own))[0]
 
     strip = (depths, ROWS, cols)
-    keep, send = call(pack_velocity, (strip, strip), (order, *slabs))
+    keep, send = call(pack_velocity, (strip, strip), (order, *slabs, mate))
     theirs = lax.ppermute(send, "sub", SWAP)
 
     def coefficients_of(depth, after):
@@ -435,20 +463,21 @@
         early.append(shifted(here_send[s - 1], s))
         early.append(crossed(cross_send[s - 1], s))
 
-    strip = (ROWS, cols)
-    fields, here, sub_send, cross = call(
+    part = (tiles // 2, ROWS, LANES)
+    fields, send, here, image_send = call(
         functools.partial(depth_step, kcheb, bins, depths == 1, True),
-        ((PARTS,) + strip, (1,) + strip, (PARTS + 1,) + strip, (1,) + strip),
+        (compact, compact, part, part),
         (*ready[-1], *state, kept),
         params=STEP,
         scratch=scratch,
     )
-    sub_got = lax.ppermute(sub_send, "sub", SWAP)
-    late = [here, sub_got]
+    image_got = lax.ppermute(image_send, "sub", SWAP)
+    got = lax.ppermute(send, "sub", SWAP)
+    late = [here, image_got]
     for s in range(1, freq):
         late.append(shifted(here, s))
-        late.append(crossed(cross, s))
-    fields = call(assemble_fields, (wavefields.shape,), (fields, sub_got))[0]
+        late.append(crossed(image_send, s))
+    fields = call(assemble_fields, (wavefields.shape,), (fields, got))[0]
     image = call(functools.partial(assemble_images, freq), ((each, rows, cols),), (*early, *late))[0]
     return fields, image
 

time: 37.3 us -> 39.4 us (1.056)
  waiting for transfers between devices: 9.75 us -> 12 us
  starting transfers between devices: 14.1 us -> 13.7 us
    ppermute x2, waiting for transfers between devices: 0.53 us -> 2.02 us  [shifted(): lax.ppermute(value, 'freq', [(i, (i + s) % freq) for i in range(freq)])]
    ppermute x2, starting transfers between devices: 1.49 us -> 0.49 us  [crossed(): return lax.ppermute(value, ('freq', 'sub'), pairs)]
    ppermute x2, waiting for transfers between devices: 0.93 us -> 1.93 us  [crossed(): return lax.ppermute(value, ('freq', 'sub'), pairs)]
    ppermute x1 -> x2, starting transfers between devices: 0.18 us -> 0.86 us  [the longest x1 0.68 us: body(): image_got = lax.ppermute(image_send, 'sub', SWAP)]
  transfers between devices with their start and end apart: 16 -> 17, of which waited for: 9 -> 10; matrix products, arithmetic and copies ran while one was open for 2% -> 2% of each run, Pallas kernels for 14% -> 13%
where the time goes in v6:
time: 39.4 us; the launch traced here: 39.2 us
  starting transfers between devices  13.7 us (35%)
  waiting for transfers between devices  12 us (30%)
  Pallas kernels  10.1 us (26%)
  local copies, waits for them, and re-layouts  1.9 us (5%)
  between operations  1.44 us (4%)
    pallas_call x14, Pallas kernels, call(): pl.pallas_call(kernel, out_shape=tuple((jax.ShapeDtypeStruct(o, f32) for...  10.1 us
    ppermute x4, waiting for transfers between devices, body(): zmate = lax.ppermute(own, axes, chain)  7.41 us
    ppermute x4, starting transfers between devices, body(): zmate = lax.ppermute(own, axes, chain)  6.21 us
    ppermute x1, starting transfers between devices, body(): lax.ppermute(velocity, 'freq', [((i + s) % freq, i) for i in range(freq)])  2.55 us
    ppermute x2, waiting for transfers between devices, shifted(): lax.ppermute(value, 'freq', [(i, (i + s) % freq) for i in range(freq)])  2.02 us
    ppermute x2, starting transfers between devices, shifted(): lax.ppermute(value, 'freq', [(i, (i + s) % freq) for i in range(freq)])  1.95 us
    ppermute x2, waiting for transfers between devices, crossed(): return lax.ppermute(value, ('freq', 'sub'), pairs)  1.93 us
    unnamed x8, local copies, waits for them, and re-layouts  1.26 us
  transfers between devices with their start and end apart: 17, of which 10 were waited for; matrix products, arithmetic and copies ran while one was open for 2% of the time, Pallas kernels for 13%

profile of v6, /device:TPU:0, one launch (start us, length us, event | category | flops | bytes accessed | tf_op | source)
XLA Modules:
  0.0 39.2 jit_solution(11435790258163440764)
XLA Ops:
  0.6 0.6 %collective-permute-start.1 = (f32[1,4,16,512]{3,2,1,0:T(8,128)}, f32[1,4,16,512]{3,2,1,0:T(8,128)S(1)}, u32[]{:S(2)}, u32[]{:S(2)}) collective-permute-start(f32[1,4,16,512]{3,2,1,0:T(8,128)} %x_ref.1), channel_id=1, source_target_pairs={{0,1},{1,0},{2,3},{3,2},{4,5},{5,4},{6,7},{7,6},{8,9},{9,8},{10,11... | collective-permute-start | bytes 393224 | tf_op jit(solution)/shard_map/ppermute | solution.py:416
  1.2 2.6 %collective-permute-start = (f32[4,16,512]{2,1,0:T(8,128)}, f32[4,16,512]{2,1,0:T(8,128)S(1)}, u32[]{:S(2)}, u32[]{:S(2)}) collective-permute-start(f32[4,16,512]{2,1,0:T(8,128)} %refs_0_.1), channel_id=1, source_target_pairs={{2,0},{0,2},{3,1},{1,3},{6,4},{4,6},{7,5},{5,7},{10,8},{8,10},{11,... | collective-permute-start | bytes 393224 | tf_op jit(solution)/shard_map/ppermute | solution.py:405
  3.8 0.9 %copy-done.2 = f32[1,4,16,512]{3,2,1,0:T(8,128)S(1)} copy-done((f32[1,4,16,512]{3,2,1,0:T(8,128)S(1)}, f32[1,4,16,512]{3,2,1,0:T(8,128)}, u32[]{:S(2)}) %copy-start.2) | copy-done | bytes 131096
  5.3 1.6 %collective-permute-start.3 = (f32[32,8,128]{2,1,0:T(8,128)S(1)}, f32[32,8,128]{2,1,0:T(8,128)S(1)}, u32[]{:S(2)}, u32[]{:S(2)}) collective-permute-start(f32[32,8,128]{2,1,0:T(8,128)S(1)} %shard_map.69.refs_0_.refs_3_), channel_id=1, source_target_pairs={{1,4},{4,1},{5,8},{8,5},{9,12},{12,9},{0,16},{13,29},{3,6},{6,3},{... | collective-permute-start | bytes 393224 | tf_op jit(solution)/shard_map/ppermute | solution.py:419
  8.8 0.4 constant_dynamic-slice_fusion
  9.4 0.5 %collective-permute-done.2.refs_2_.other_ref = f32[4,8,512]{2,1,0:T(8,128)S(1)} collective-permute-done((f32[4,8,512]{2,1,0:T(8,128)S(1)}, f32[4,8,512]{2,1,0:T(8,128)S(1)}, u32[]{:S(2)}, u32[]{:S(2)}) %collective-permute-start.2) | collective-permute-done | bytes 65568 | tf_op jit(solution)/shard_map/ppermute | solution.py:424
  9.9 0.5 %collective-permute-done.3.refs_5_ = f32[32,8,128]{2,1,0:T(8,128)S(1)} collective-permute-done((f32[32,8,128]{2,1,0:T(8,128)S(1)}, f32[32,8,128]{2,1,0:T(8,128)S(1)}, u32[]{:S(2)}, u32[]{:S(2)}) %collective-permute-start.3) | collective-permute-done | bytes 131104 | tf_op jit(solution)/shard_map/ppermute | solution.py:419
  10.3 1.1 %shard_map.72 = (f32[32,8,128]{2,1,0:T(8,128)S(1)}, f32[8,8,128]{2,1,0:T(8,128)S(1)}) custom-call(f32[18,128]{1,0:T(8,128)S(1)} %pad.4.refs_0_.table_ref, f32[4,8,512]{2,1,0:T(8,128)S(1)} %get-tuple-element.22.refs_1_.keep_ref, f32[4,8,512]{2,1,0:T(8,128)S(1)} %collective-permute-done.2.refs_2_.other_ref, f32[32,8,128]{2,1,0:T(8,128)S(1)} %shard_map.69.refs_0_.refs_3_, ...), custom_call_target="tpu_custom_call" | custom-call | flops 1048576 | bytes 65536 | tf_op jit(solution)/shard_map/pallas_call | solution.py:386
  11.5 1.6 %collective-permute-start.5 = (f32[32,8,128]{2,1,0:T(8,128)S(1)}, f32[32,8,128]{2,1,0:T(8,128)S(1)}, u32[]{:S(2)}, u32[]{:S(2)}) collective-permute-start(f32[32,8,128]{2,1,0:T(8,128)S(1)} %get-tuple-element.24.refs_0_.refs_1_), channel_id=1, source_target_pairs={{1,4},{4,1},{5,8},{8,5},{9,12},{12,9},{0,16},{13,29},{3,6},{6,3},{... | collective-permute-start | bytes 393224 | tf_op jit(solution)/shard_map/ppermute | solution.py:449
  13.1 1.0 %shard_map.73.refs_0_ = f32[18,8,8,128]{3,2,1,0:T(8,128)S(1)} custom-call(f32[18,128]{1,0:T(8,128)S(1)} %pad.4.refs_0_.table_ref, f32[4,8,512]{2,1,0:T(8,128)S(1)} %get-tuple-element.22.refs_1_.keep_ref, f32[4,8,512]{2,1,0:T(8,128)S(1)} %collective-permute-done.2.refs_2_.other_ref, f32[32,8,128]{2,1,0:T(8,128)S(1)} %get-tuple-element.24.refs_0_.refs_1_), custom_call_target="tpu_custom_call" | custom-call | flops 1048576 | bytes 65536 | tf_op jit(solution)/shard_map/pallas_call | solution.py:386
  14.1 2.5 %collective-permute-done.5.refs_3_ = f32[32,8,128]{2,1,0:T(8,128)S(1)} collective-permute-done((f32[32,8,128]{2,1,0:T(8,128)S(1)}, f32[32,8,128]{2,1,0:T(8,128)S(1)}, u32[]{:S(2)}, u32[]{:S(2)}) %collective-permute-start.5) | collective-permute-done | bytes 131104 | tf_op jit(solution)/shard_map/ppermute | solution.py:449
  16.6 0.9 %shard_map.74 = (f32[32,8,128]{2,1,0:T(8,128)S(1)}, f32[8,8,128]{2,1,0:T(8,128)S(1)}) custom-call(f32[18,8,8,128]{3,2,1,0:T(8,128)S(1)} %shard_map.73.refs_0_, f32[32,8,128]{2,1,0:T(8,128)S(1)} %get-tuple-element.24.refs_0_.refs_1_, f32[32,8,128]{2,1,0:T(8,128)S(1)} %collective-permute-done.4.refs_2_, f32[32,8,128]{2,1,0:T(8,128)S(1)} %collective-permute-done.5.refs_3_), custom_call_target="tpu_custom_call" | custom-call | flops 1048576 | bytes 65536 | tf_op jit(solution)/shard_map/pallas_call | solution.py:386
  17.7 1.5 %collective-permute-start.7 = (f32[32,8,128]{2,1,0:T(8,128)S(1)}, f32[32,8,128]{2,1,0:T(8,128)S(1)}, u32[]{:S(2)}, u32[]{:S(2)}) collective-permute-start(f32[32,8,128]{2,1,0:T(8,128)S(1)} %get-tuple-element.25.refs_0_.refs_1_), channel_id=1, source_target_pairs={{1,4},{4,1},{5,8},{8,5},{9,12},{12,9},{0,16},{13,29},{3,6},{6,3},{... | collective-permute-start | bytes 393224 | tf_op jit(solution)/shard_map/ppermute | solution.py:449
  19.2 1.0 %shard_map.76.refs_0_ = f32[18,8,8,128]{3,2,1,0:T(8,128)S(1)} custom-call(f32[18,128]{1,0:T(8,128)S(1)} %pad.4.refs_0_.table_ref, f32[4,8,512]{2,1,0:T(8,128)S(1)} %get-tuple-element.22.refs_1_.keep_ref, f32[4,8,512]{2,1,0:T(8,128)S(1)} %collective-permute-done.2.refs_2_.other_ref, f32[32,8,128]{2,1,0:T(8,128)S(1)} %get-tuple-element.25.refs_0_.refs_1_), custom_call_target="tpu_custom_call" | custom-call | flops 1048576 | bytes 65536 | tf_op jit(solution)/shard_map/pallas_call | solution.py:386
  20.2 2.5 %collective-permute-done.7.refs_3_ = f32[32,8,128]{2,1,0:T(8,128)S(1)} collective-permute-done((f32[32,8,128]{2,1,0:T(8,128)S(1)}, f32[32,8,128]{2,1,0:T(8,128)S(1)}, u32[]{:S(2)}, u32[]{:S(2)}) %collective-permute-start.7) | collective-permute-done | bytes 131104 | tf_op jit(solution)/shard_map/ppermute | solution.py:449
  22.6 0.9 %shard_map.77 = (f32[32,8,128]{2,1,0:T(8,128)S(1)}, f32[8,8,128]{2,1,0:T(8,128)S(1)}) custom-call(f32[18,8,8,128]{3,2,1,0:T(8,128)S(1)} %shard_map.76.refs_0_, f32[32,8,128]{2,1,0:T(8,128)S(1)} %get-tuple-element.25.refs_0_.refs_1_, f32[32,8,128]{2,1,0:T(8,128)S(1)} %collective-permute-done.6.refs_2_, f32[32,8,128]{2,1,0:T(8,128)S(1)} %collective-permute-done.7.refs_3_), custom_call_target="tpu_custom_call" | custom-call | flops 1048576 | bytes 65536 | tf_op jit(solution)/shard_map/pallas_call | solution.py:386
  23.8 1.5 %collective-permute-start.9 = (f32[32,8,128]{2,1,0:T(8,128)S(1)}, f32[32,8,128]{2,1,0:T(8,128)S(1)}, u32[]{:S(2)}, u32[]{:S(2)}) collective-permute-start(f32[32,8,128]{2,1,0:T(8,128)S(1)} %get-tuple-element.26.refs_1_), channel_id=1, source_target_pairs={{1,4},{4,1},{5,8},{8,5},{9,12},{12,9},{0,16},{13,29},{3,6},{6,3},{... | collective-permute-start | bytes 393224 | tf_op jit(solution)/shard_map/ppermute | solution.py:449
  25.3 1.0 %shard_map.75.refs_3_.refs_0_ = f32[18,8,8,128]{3,2,1,0:T(8,128)S(1)} custom-call(f32[18,128]{1,0:T(8,128)S(1)} %pad.4.refs_0_.table_ref, f32[4,8,512]{2,1,0:T(8,128)S(1)} %get-tuple-element.22.refs_1_.keep_ref, f32[4,8,512]{2,1,0:T(8,128)S(1)} %collective-permute-done.2.refs_2_.other_ref, f32[32,8,128]{2,1,0:T(8,128)S(1)} %get-tuple-element.25.refs_0_.refs_1_), custom_call_target="tpu_custom_call" | custom-call | flops 1048576 | bytes 65536 | tf_op jit(solution)/shard_map/pallas_call | solution.py:386
  26.3 0.5 %shard_map.78 = (f32[2,8,512]{2,1,0:T(8,128)S(1)}, f32[2,8,512]{2,1,0:T(8,128)S(1)}, f32[1,2,8,512]{3,2,1,0:T(8,128)S(1)}, f32[1,2,8,512]{3,2,1,0:T(8,128)S(1)}) custom-call(f32[8,8,128]{2,1,0:T(8,128)S(1)} %get-tuple-element.27.refs_0_, f32[8,8,128]{2,1,0:T(8,128)S(1)} %get-tuple-element.28.refs_1_, f32[8,8,128]{2,1,0:T(8,128)S(1)} %get-tuple-element.29.refs_2_, ...), custom_call_target="tpu_custom_call" | custom-call | flops 1048576 | bytes 65536 | tf_op jit(solution)/shard_map/pallas_call | solution.py:386
  26.8 2.0 %collective-permute-done.9.refs_3_ = f32[32,8,128]{2,1,0:T(8,128)S(1)} collective-permute-done((f32[32,8,128]{2,1,0:T(8,128)S(1)}, f32[32,8,128]{2,1,0:T(8,128)S(1)}, u32[]{:S(2)}, u32[]{:S(2)}) %collective-permute-start.9) | collective-permute-done | bytes 131104 | tf_op jit(solution)/shard_map/ppermute | solution.py:449
  28.7 1.0 %shard_map.79 = (f32[16,8,128]{2,1,0:T(8,128)S(1)}, f32[16,8,128]{2,1,0:T(8,128)S(1)}, f32[4,8,128]{2,1,0:T(8,128)S(1)}, f32[4,8,128]{2,1,0:T(8,128)S(1)}) custom-call(f32[18,8,8,128]{3,2,1,0:T(8,128)S(1)} %shard_map.75.refs_3_.refs_0_, f32[32,8,128]{2,1,0:T(8,128)S(1)} %get-tuple-element.26.refs_1_, f32[32,8,128]{2,1,0:T(8,128)S(1)} %collective-permute-done.8.refs_2_, ...), custom_call_target="tpu_custom_call" | custom-call | flops 1048576 | bytes 65536 | tf_op jit(solution)/shard_map/pallas_call | solution.py:386
  30.0 0.4 %collective-permute-start.11 = (f32[2,8,512]{2,1,0:T(8,128)S(1)}, f32[2,8,512]{2,1,0:T(8,128)S(1)}, u32[]{:S(2)}, u32[]{:S(2)}) collective-permute-start(f32[2,8,512]{2,1,0:T(8,128)S(1)} %get-tuple-element.33), channel_id=1, source_target_pairs={{0,1},{1,0},{2,3},{3,2},{4,5},{5,4},{6,7},{7,6},{8,9},{9,8},{10,11... | collective-permute-start | bytes 98312 | tf_op jit(solution)/shard_map/ppermute | solution.py:461
  30.4 1.0 %collective-permute-start.12 = (f32[2,8,512]{2,1,0:T(8,128)S(1)}, f32[2,8,512]{2,1,0:T(8,128)S(1)}, u32[]{:S(2)}, u32[]{:S(2)}) collective-permute-start(f32[2,8,512]{2,1,0:T(8,128)S(1)} %bitcast.10), channel_id=1, source_target_pairs={{0,2},{2,0},{1,3},{3,1},{4,6},{6,4},{5,7},{7,5},{8,10},{10,8},{9,1... | collective-permute-start | bytes 98312 | tf_op jit(solution)/shard_map/ppermute | solution.py:397
  31.3 0.5 %collective-permute-start.13 = (f32[2,8,512]{2,1,0:T(8,128)S(1)}, f32[2,8,512]{2,1,0:T(8,128)S(1)}, u32[]{:S(2)}, u32[]{:S(2)}) collective-permute-start(f32[2,8,512]{2,1,0:T(8,128)S(1)} %bitcast.9), channel_id=1, source_target_pairs={{0,3},{1,2},{2,1},{3,0},{4,7},{5,6},{6,5},{7,4},{8,11},{9,10},{10,... | collective-permute-start | bytes 98312 | tf_op jit(solution)/shard_map/ppermute | solution.py:401
  31.8 0.7 %collective-permute-start.14 = (f32[4,8,128]{2,1,0:T(8,128)S(1)}, f32[4,8,128]{2,1,0:T(8,128)S(1)}, u32[]{:S(2)}, u32[]{:S(2)}) collective-permute-start(f32[4,8,128]{2,1,0:T(8,128)S(1)} %get-tuple-element.37), channel_id=1, source_target_pairs={{0,1},{1,0},{2,3},{3,2},{4,5},{5,4},{6,7},{7,6},{8,9},{9,8},{10,11... | collective-permute-start | bytes 49160 | tf_op jit(solution)/shard_map/ppermute | solution.py:474
  32.5 1.0 %collective-permute-start.15 = (f32[4,8,128]{2,1,0:T(8,128)S(1)}, f32[4,8,128]{2,1,0:T(8,128)S(1)}, u32[]{:S(2)}, u32[]{:S(2)}) collective-permute-start(f32[4,8,128]{2,1,0:T(8,128)S(1)} %get-tuple-element.36.refs_4_), channel_id=1, source_target_pairs={{0,2},{2,0},{1,3},{3,1},{4,6},{6,4},{5,7},{7,5},{8,10},{10,8},{9,1... | collective-permute-start | bytes 49160 | tf_op jit(solution)/shard_map/ppermute | solution.py:397
  33.5 0.8 %collective-permute-done.12.refs_2_ = f32[2,8,512]{2,1,0:T(8,128)S(1)} collective-permute-done((f32[2,8,512]{2,1,0:T(8,128)S(1)}, f32[2,8,512]{2,1,0:T(8,128)S(1)}, u32[]{:S(2)}, u32[]{:S(2)}) %collective-permute-start.12) | collective-permute-done | bytes 32800 | tf_op jit(solution)/shard_map/ppermute | solution.py:397
  34.3 0.7 %collective-permute-done.13.refs_3_ = f32[2,8,512]{2,1,0:T(8,128)S(1)} collective-permute-done((f32[2,8,512]{2,1,0:T(8,128)S(1)}, f32[2,8,512]{2,1,0:T(8,128)S(1)}, u32[]{:S(2)}, u32[]{:S(2)}) %collective-permute-start.13) | collective-permute-done | bytes 32800 | tf_op jit(solution)/shard_map/ppermute | solution.py:401
  35.0 1.2 %collective-permute-done.15.refs_6_ = f32[4,8,128]{2,1,0:T(8,128)S(1)} collective-permute-done((f32[4,8,128]{2,1,0:T(8,128)S(1)}, f32[4,8,128]{2,1,0:T(8,128)S(1)}, u32[]{:S(2)}, u32[]{:S(2)}) %collective-permute-start.15) | collective-permute-done | bytes 16416 | tf_op jit(solution)/shard_map/ppermute | solution.py:397
  36.2 1.2 %collective-permute-done.16.refs_7_ = f32[4,8,128]{2,1,0:T(8,128)S(1)} collective-permute-done((f32[4,8,128]{2,1,0:T(8,128)S(1)}, f32[4,8,128]{2,1,0:T(8,128)S(1)}, u32[]{:S(2)}, u32[]{:S(2)}) %collective-permute-start.16) | collective-permute-done | bytes 16416 | tf_op jit(solution)/shard_map/ppermute | solution.py:401
  37.4 0.8 %shard_map.81 = f32[2,16,512]{2,1,0:T(8,128)} custom-call(f32[2,8,512]{2,1,0:T(8,128)S(1)} %get-tuple-element.30.refs_4_.refs_0_, f32[2,8,512]{2,1,0:T(8,128)S(1)} %collective-permute-done.11.refs_1_, f32[2,8,512]{2,1,0:T(8,128)S(1)} %collective-permute-done.12.refs_2_, f32[2,8,512]{2,1,0:T(8,128)S(1)} %collective-permute-done.13.refs_3_, ...), custom_call_target="tpu_custom_call" | custom-call | flops 1048576 | bytes 65536 | tf_op jit(solution)/shard_map/pallas_call | solution.py:386
  38.2 1.0 %shard_map.80 = f32[1,4,16,512]{3,2,1,0:T(8,128)} custom-call(f32[16,8,128]{2,1,0:T(8,128)S(1)} %get-tuple-element.31.own_ref, f32[16,8,128]{2,1,0:T(8,128)S(1)} %collective-permute-done.10.got_ref), custom_call_target="tpu_custom_call" | custom-call | flops 1048576 | bytes 65536 | tf_op jit(solution)/shard_map/pallas_call | solution.py:386
  (29 shorter events, 2.7 us)
Async XLA Ops:
  0.6 8.1 %copy-start = (f32[32,32,9,2]{1,3,2,0:T(2,128)S(1)}, f32[32,32,9,2]{1,3,2,0:T(2,128)}, u32[]{:S(2)}) copy-start(f32[32,32,9,2]{1,3,2,0:T(2,128)} %param.7) | copy-start | bytes 221188
  0.6 4.3 %collective-permute-start.1 = (f32[1,4,16,512]{3,2,1,0:T(8,128)}, f32[1,4,16,512]{3,2,1,0:T(8,128)S(1)}, u32[]{:S(2)}, u32[]{:S(2)}) collective-permute-start(f32[1,4,16,512]{3,2,1,0:T(8,128)} %x_ref.1), channel_id=1, source_target_pairs={{0,1},{1,0},{2,3},{3,2},{4,5},{5,4},{6,7},{7,6},{8,9},{9,8},{10,11... | collective-permute-start | bytes 393224 | tf_op jit(solution)/shard_map/ppermute | solution.py:416
  1.2 6.9 %collective-permute-start = (f32[4,16,512]{2,1,0:T(8,128)}, f32[4,16,512]{2,1,0:T(8,128)S(1)}, u32[]{:S(2)}, u32[]{:S(2)}) collective-permute-start(f32[4,16,512]{2,1,0:T(8,128)} %refs_0_.1), channel_id=1, source_target_pairs={{2,0},{0,2},{3,1},{1,3},{6,4},{4,6},{7,5},{5,7},{10,8},{8,10},{11,... | collective-permute-start | bytes 393224 | tf_op jit(solution)/shard_map/ppermute | solution.py:405
  3.8 0.9 %copy-start.2 = (f32[1,4,16,512]{3,2,1,0:T(8,128)S(1)}, f32[1,4,16,512]{3,2,1,0:T(8,128)}, u32[]{:S(2)}) copy-start(f32[1,4,16,512]{3,2,1,0:T(8,128)} %x_ref.1) | copy-start | bytes 393220
  5.3 5.0 %collective-permute-start.3 = (f32[32,8,128]{2,1,0:T(8,128)S(1)}, f32[32,8,128]{2,1,0:T(8,128)S(1)}, u32[]{:S(2)}, u32[]{:S(2)}) collective-permute-start(f32[32,8,128]{2,1,0:T(8,128)S(1)} %shard_map.69.refs_0_.refs_3_), channel_id=1, source_target_pairs={{1,4},{4,1},{5,8},{8,5},{9,12},{12,9},{0,16},{13,29},{3,6},{6,3},{... | collective-permute-start | bytes 393224 | tf_op jit(solution)/shard_map/ppermute | solution.py:419
  7.5 0.7 %copy-start.3 = (s32[4]{0:T(128)S(1)}, s32[4]{0:T(128)}, u32[]{:S(2)}) copy-start(s32[4]{0:T(128)} %param.9) | copy-start | bytes 52
  7.6 0.9 %copy-start.1 = (f32[4,16,512]{2,1,0:T(8,128)S(1)}, f32[4,16,512]{2,1,0:T(8,128)}, u32[]{:S(2)}) copy-start(f32[4,16,512]{2,1,0:T(8,128)} %refs_0_.1) | copy-start | bytes 393220
  8.5 1.3 %collective-permute-start.2 = (f32[4,8,512]{2,1,0:T(8,128)S(1)}, f32[4,8,512]{2,1,0:T(8,128)S(1)}, u32[]{:S(2)}, u32[]{:S(2)}) collective-permute-start(f32[4,8,512]{2,1,0:T(8,128)S(1)} %get-tuple-element.23), channel_id=1, source_target_pairs={{0,1},{1,0},{2,3},{3,2},{4,5},{5,4},{6,7},{7,6},{8,9},{9,8},{10,11... | collective-permute-start | bytes 196616 | tf_op jit(solution)/shard_map/ppermute | solution.py:424
  11.4 2.6 %collective-permute-start.4 = (f32[32,8,128]{2,1,0:T(8,128)S(1)}, f32[32,8,128]{2,1,0:T(8,128)S(1)}, u32[]{:S(2)}, u32[]{:S(2)}) collective-permute-start(f32[32,8,128]{2,1,0:T(8,128)S(1)} %get-tuple-element.24.refs_0_.refs_1_), channel_id=1, source_target_pairs={{0,1},{1,0},{2,3},{3,2},{4,5},{5,4},{6,7},{7,6},{8,9},{9,8},{10,11... | collective-permute-start | bytes 393224 | tf_op jit(solution)/shard_map/ppermute | solution.py:450
  11.5 5.0 %collective-permute-start.5 = (f32[32,8,128]{2,1,0:T(8,128)S(1)}, f32[32,8,128]{2,1,0:T(8,128)S(1)}, u32[]{:S(2)}, u32[]{:S(2)}) collective-permute-start(f32[32,8,128]{2,1,0:T(8,128)S(1)} %get-tuple-element.24.refs_0_.refs_1_), channel_id=1, source_target_pairs={{1,4},{4,1},{5,8},{8,5},{9,12},{12,9},{0,16},{13,29},{3,6},{6,3},{... | collective-permute-start | bytes 393224 | tf_op jit(solution)/shard_map/ppermute | solution.py:449
  17.5 2.7 %collective-permute-start.6 = (f32[32,8,128]{2,1,0:T(8,128)S(1)}, f32[32,8,128]{2,1,0:T(8,128)S(1)}, u32[]{:S(2)}, u32[]{:S(2)}) collective-permute-start(f32[32,8,128]{2,1,0:T(8,128)S(1)} %get-tuple-element.25.refs_0_.refs_1_), channel_id=1, source_target_pairs={{0,1},{1,0},{2,3},{3,2},{4,5},{5,4},{6,7},{7,6},{8,9},{9,8},{10,11... | collective-permute-start | bytes 393224 | tf_op jit(solution)/shard_map/ppermute | solution.py:450
  17.7 5.0 %collective-permute-start.7 = (f32[32,8,128]{2,1,0:T(8,128)S(1)}, f32[32,8,128]{2,1,0:T(8,128)S(1)}, u32[]{:S(2)}, u32[]{:S(2)}) collective-permute-start(f32[32,8,128]{2,1,0:T(8,128)S(1)} %get-tuple-element.25.refs_0_.refs_1_), channel_id=1, source_target_pairs={{1,4},{4,1},{5,8},{8,5},{9,12},{12,9},{0,16},{13,29},{3,6},{6,3},{... | collective-permute-start | bytes 393224 | tf_op jit(solution)/shard_map/ppermute | solution.py:449
  23.6 3.2 %collective-permute-start.8 = (f32[32,8,128]{2,1,0:T(8,128)S(1)}, f32[32,8,128]{2,1,0:T(8,128)S(1)}, u32[]{:S(2)}, u32[]{:S(2)}) collective-permute-start(f32[32,8,128]{2,1,0:T(8,128)S(1)} %get-tuple-element.26.refs_1_), channel_id=1, source_target_pairs={{0,1},{1,0},{2,3},{3,2},{4,5},{5,4},{6,7},{7,6},{8,9},{9,8},{10,11... | collective-permute-start | bytes 393224 | tf_op jit(solution)/shard_map/ppermute | solution.py:450
  23.8 5.0 %collective-permute-start.9 = (f32[32,8,128]{2,1,0:T(8,128)S(1)}, f32[32,8,128]{2,1,0:T(8,128)S(1)}, u32[]{:S(2)}, u32[]{:S(2)}) collective-permute-start(f32[32,8,128]{2,1,0:T(8,128)S(1)} %get-tuple-element.26.refs_1_), channel_id=1, source_target_pairs={{1,4},{4,1},{5,8},{8,5},{9,12},{12,9},{0,16},{13,29},{3,6},{6,3},{... | collective-permute-start | bytes 393224 | tf_op jit(solution)/shard_map/ppermute | solution.py:449
  29.8 8.4 %collective-permute-start.10 = (f32[16,8,128]{2,1,0:T(8,128)S(1)}, f32[16,8,128]{2,1,0:T(8,128)S(1)}, u32[]{:S(2)}, u32[]{:S(2)}) collective-permute-start(f32[16,8,128]{2,1,0:T(8,128)S(1)} %get-tuple-element.32), channel_id=1, source_target_pairs={{0,1},{1,0},{2,3},{3,2},{4,5},{5,4},{6,7},{7,6},{8,9},{9,8},{10,11... | collective-permute-start | bytes 196616 | tf_op jit(solution)/shard_map/ppermute | solution.py:475
  30.0 2.5 %collective-permute-start.11 = (f32[2,8,512]{2,1,0:T(8,128)S(1)}, f32[2,8,512]{2,1,0:T(8,128)S(1)}, u32[]{:S(2)}, u32[]{:S(2)}) collective-permute-start(f32[2,8,512]{2,1,0:T(8,128)S(1)} %get-tuple-element.33), channel_id=1, source_target_pairs={{0,1},{1,0},{2,3},{3,2},{4,5},{5,4},{6,7},{7,6},{8,9},{9,8},{10,11... | collective-permute-start | bytes 98312 | tf_op jit(solution)/shard_map/ppermute | solution.py:461
  30.4 3.9 %collective-permute-start.12 = (f32[2,8,512]{2,1,0:T(8,128)S(1)}, f32[2,8,512]{2,1,0:T(8,128)S(1)}, u32[]{:S(2)}, u32[]{:S(2)}) collective-permute-start(f32[2,8,512]{2,1,0:T(8,128)S(1)} %bitcast.10), channel_id=1, source_target_pairs={{0,2},{2,0},{1,3},{3,1},{4,6},{6,4},{5,7},{7,5},{8,10},{10,8},{9,1... | collective-permute-start | bytes 98312 | tf_op jit(solution)/shard_map/ppermute | solution.py:397
  31.3 3.7 %collective-permute-start.13 = (f32[2,8,512]{2,1,0:T(8,128)S(1)}, f32[2,8,512]{2,1,0:T(8,128)S(1)}, u32[]{:S(2)}, u32[]{:S(2)}) collective-permute-start(f32[2,8,512]{2,1,0:T(8,128)S(1)} %bitcast.9), channel_id=1, source_target_pairs={{0,3},{1,2},{2,1},{3,0},{4,7},{5,6},{6,5},{7,4},{8,11},{9,10},{10,... | collective-permute-start | bytes 98312 | tf_op jit(solution)/shard_map/ppermute | solution.py:401
  31.8 3.2 %collective-permute-start.14 = (f32[4,8,128]{2,1,0:T(8,128)S(1)}, f32[4,8,128]{2,1,0:T(8,128)S(1)}, u32[]{:S(2)}, u32[]{:S(2)}) collective-permute-start(f32[4,8,128]{2,1,0:T(8,128)S(1)} %get-tuple-element.37), channel_id=1, source_target_pairs={{0,1},{1,0},{2,3},{3,2},{4,5},{5,4},{6,7},{7,6},{8,9},{9,8},{10,11... | collective-permute-start | bytes 49160 | tf_op jit(solution)/shard_map/ppermute | solution.py:474
  32.5 3.7 %collective-permute-start.15 = (f32[4,8,128]{2,1,0:T(8,128)S(1)}, f32[4,8,128]{2,1,0:T(8,128)S(1)}, u32[]{:S(2)}, u32[]{:S(2)}) collective-permute-start(f32[4,8,128]{2,1,0:T(8,128)S(1)} %get-tuple-element.36.refs_4_), channel_id=1, source_target_pairs={{0,2},{2,0},{1,3},{3,1},{4,6},{6,4},{5,7},{7,5},{8,10},{10,8},{9,1... | collective-permute-start | bytes 49160 | tf_op jit(solution)/shard_map/ppermute | solution.py:397
  34.3 3.2 %collective-permute-start.16 = (f32[4,8,128]{2,1,0:T(8,128)S(1)}, f32[4,8,128]{2,1,0:T(8,128)S(1)}, u32[]{:S(2)}, u32[]{:S(2)}) collective-permute-start(f32[4,8,128]{2,1,0:T(8,128)S(1)} %get-tuple-element.37), channel_id=1, source_target_pairs={{0,3},{1,2},{2,1},{3,0},{4,7},{5,6},{6,5},{7,4},{8,11},{9,10},{10,... | collective-permute-start | bytes 49160 | tf_op jit(solution)/shard_map/ppermute | solution.py:401
